TPU v7x, 256 devices: a whole 4x4x8 slice. The times are simulated.
256 devices in a mesh: rows: 32 (over y, z), mem: 8 (over x, core).
Axes of the slice: x: 4, y: 4, z: 8, core: 2. Of those that a mesh axis runs over, the one named last changes fastest.
Arguments:
- ensemble: float32 [64, 32, 192, 384], P('mem', None, 'rows'), may hold values from 0 to 2
- courant: float32 [3, 32, 192, 384], P(None, None, 'rows'), may hold values from -0.22 to 0.22
- obs_column: int32 [512], P('rows'), may hold values from 0 to 73727, as said below
- obs_value: float32 [32, 512], P(None, 'rows'), may hold values from -6 to 6
- obs_var: float32 [32, 512], P(None, 'rows'), may hold values from 0.5 to 8
Outputs:
- analysis: float32 [64, 32, 192, 384], P('mem', None, 'rows')
Inputs may be any that keep to these rules, and one draw needn't show every extreme that they name: `obs_column`: entry p is x * 384 + y with x from (p // 16) * 6 to (p // 16) * 6 + 5.
All inputs are finite; a program needn't handle non-finite values.
Results may differ from a plain program's by a relative error of at most 0.0003.
Values sent between devices are 32-bit elements; how exact they have to be, the bound alone decides.
No kernel may reach another device: no remote copies, remote signals or barrier semaphores. Data moves between devices by JAX's collectives and lax.ppermute only.
A program may use at most 128 MiB of HBM per device.

v0:
```python
import jax
import jax.numpy as jnp
from jax import lax
from jax.sharding import PartitionSpec as P

STEPS = 3
NS_ITERS = 4


DIFFUSION = 0.05


def padded_2(cells, sides, width):
    for axis, dim in sides:
        count = lax.axis_size(axis)
        ends = count - 1
        head = lax.slice_in_dim(cells, 0, width, axis=dim)
        tail = lax.slice_in_dim(cells, cells.shape[dim] - width, cells.shape[dim], axis=dim)
        cells = jnp.concatenate(
            [
                lax.ppermute(tail, axis, [(i, (i + 1) % count) for i in range(ends)]),
                cells,
                lax.ppermute(head, axis, [((i + 1) % count, i) for i in range(ends)]),
            ],
            axis=dim,
        )
    return cells


def joined_along(parts, dim):
    parts = jnp.moveaxis(parts, 0, dim)
    lengths = parts.shape
    return parts.reshape(*lengths[:dim], lengths[dim] * lengths[dim + 1], *lengths[dim + 2 :])


def from_everyone(shard, axis):
    copies = jnp.broadcast_to(shard, (lax.axis_size(axis), *shard.shape))
    return lax.all_to_all(copies, axis, split_axis=0, concat_axis=0, tiled=True)


def collect(shard, axis, dim):
    return joined_along(from_everyone(shard, axis), dim)


def over_copies(shard, axis):
    everything = from_everyone(shard, axis)
    return jnp.sum(everything, axis=0)


def packed_total(arrays, axis):
    ends = [0]
    for a in arrays:
        ends.append(ends[-1] + a.size)
    so_far = over_copies(jnp.concatenate([a.ravel() for a in arrays]), axis)
    return tuple((so_far[b:e].reshape(a.shape) for a, b, e in zip(arrays, ends, ends[1:])))


def advance(padded, courant):
    center = padded[:, :, 1:-1, :]
    below_x = padded[:, :, :-2, :]
    above_x = padded[:, :, 2:, :]
    padded_y = jnp.pad(center, ((0, 0), (0, 0), (0, 0), (1, 1)))
    below_y = padded_y[:, :, :, :-2]
    above_y = padded_y[:, :, :, 2:]
    padded_z = jnp.pad(center, ((0, 0), (1, 1), (0, 0), (0, 0)))
    below_z = padded_z[:, :-2]
    above_z = padded_z[:, 2:]
    change = jnp.zeros_like(center)
    for component, below, above in (
        (0, below_x, above_x),
        (1, below_y, above_y),
        (2, below_z, above_z),
    ):
        velocity = courant[component][None]
        change = (
            change
            - jnp.maximum(velocity, 0.0) * (center - below)
            - jnp.minimum(velocity, 0.0) * (above - center)
            + DIFFUSION * (above + below - 2.0 * center)
        )
    return center + change


def gram_terms(profiles, obs_value, obs_var):
    members_all = profiles.shape[0]
    center = jnp.mean(profiles, axis=0)
    scaling = 1.0 / jnp.sqrt((members_all - 1.0) * obs_var)
    scaled = ((profiles - center[None]) * scaling[None]).reshape(members_all, -1)
    innovation = ((obs_value - center) / jnp.sqrt(obs_var)).reshape(-1)
    gram_part = jnp.dot(scaled, scaled.T, precision=lax.Precision.HIGHEST)
    pull_part = jnp.dot(scaled, innovation, precision=lax.Precision.HIGHEST)
    return (gram_part, pull_part)


def mixing(gram_sum, pull_sum):
    members_all = gram_sum.shape[0]
    identity_matrix = jnp.eye(members_all, dtype=jnp.float32)
    system = identity_matrix + gram_sum
    frobenius = jnp.sqrt(jnp.sum(system * system))

    def newton(iteration, carry):
        iterate, inverse_root = carry
        factor = 0.5 * (
            3.0 * identity_matrix - jnp.dot(inverse_root, iterate, precision=lax.Precision.HIGHEST)
        )
        return (
            jnp.dot(iterate, factor, precision=lax.Precision.HIGHEST),
            jnp.dot(factor, inverse_root, precision=lax.Precision.HIGHEST),
        )

    iterate, inverse_root = lax.fori_loop(
        0, NS_ITERS, newton, (system / frobenius, identity_matrix)
    )
    root_inverse = inverse_root / jnp.sqrt(frobenius)
    mean_shift = jnp.dot(
        root_inverse,
        jnp.dot(root_inverse, pull_sum, precision=lax.Precision.HIGHEST),
        precision=lax.Precision.HIGHEST,
    ) / jnp.sqrt(members_all - 1.0)
    centering = identity_matrix - 1.0 / members_all
    return 1.0 / members_all + jnp.dot(
        centering, mean_shift[:, None] + root_inverse, precision=lax.Precision.HIGHEST
    )


def per_device(ensemble, courant, obs_column, obs_value, obs_var):
    rows_local = ensemble.shape[2]
    width_y = ensemble.shape[3]
    position = lax.axis_index("rows")
    concentration = ensemble
    for step_index in range(STEPS):
        padded = padded_2(concentration, (("rows", 2),), 1)
        concentration = advance(padded, courant)
    members_dev = concentration.shape[0]
    state_vectors = concentration.reshape(members_dev, concentration.shape[1], rows_local * width_y)
    local_column = obs_column - position * (rows_local * width_y)
    profiles = jnp.take(state_vectors, local_column, axis=2)
    gathered = collect(profiles, "mem", 0)
    gram_part, pull_part = gram_terms(gathered, obs_value, obs_var)
    gram_sum, pull_sum = packed_total((gram_part, pull_part), "rows")
    transform_weights = mixing(gram_sum, pull_sum)
    first_member = lax.axis_index("mem") * members_dev
    own_columns = lax.dynamic_slice_in_dim(transform_weights, first_member, members_dev, 1)
    updated_ensemble = jnp.einsum(
        "jk,jzc->kzc",
        own_columns,
        lax.all_gather(state_vectors, "mem", axis=0, tiled=True),
        precision=lax.Precision.HIGHEST,
    )
    return updated_ensemble.reshape(concentration.shape)


def solution(mesh):
    return jax.shard_map(
        per_device,
        mesh=mesh,
        in_specs=(
            P("mem", None, "rows", None),
            P(None, None, "rows", None),
            P("rows"),
            P(None, "rows"),
            P(None, "rows"),
        ),
        out_specs=P("mem", None, "rows", None),
        check_vma=False,
    )
```

profile of v0, /device:TPU:1, one launch (start us, length us, event | category | flops | bytes accessed | tf_op | source)
XLA Modules:
  0.0 191.4 jit_solution(7177170914299280212)
XLA Ops:
  6.5 1.3 fusion.77
  7.9 4.4 %collective-permute-start = (f32[8,32,1,384]{3,1,2,0:T(8,128)S(1)}, f32[8,32,1,384]{3,1,2,0:T(8,128)S(1)}, u32[]{:S(2)}, u32[]{:S(2)}) collective-permute-start(f32[8,32,1,384]{3,1,2,0:T(8,128)S(1)} %get-tuple-element.60), channel_id=1, source_target_pairs={{0,8},{8,16},{16,24},{24,32},{32,40},{40,48},{48,56},{56,64},{64,7... | collective-permute-start | bytes 1179656 | tf_op jit(solution)/shard_map/ppermute | solution.py:21
  12.3 1.3 collective-permute-start.1
  13.6 1.3 maximum_bitcast_fusion.2
  14.9 5.1 %collective-permute-done = f32[8,32,1,384]{3,1,2,0:T(8,128)S(1)} collective-permute-done((f32[8,32,1,384]{3,1,2,0:T(8,128)S(1)}, f32[8,32,1,384]{3,1,2,0:T(8,128)S(1)}, u32[]{:S(2)}, u32[]{:S(2)}) %collective-permute-start) | collective-permute-done | bytes 393248 | tf_op jit(solution)/shard_map/ppermute | solution.py:21
  20.0 4.2 %collective-permute-done.1 = f32[8,32,1,384]{3,1,2,0:T(8,128)S(1)} collective-permute-done((f32[8,32,1,384]{3,1,2,0:T(8,128)S(1)}, f32[8,32,1,384]{3,1,2,0:T(8,128)S(1)}, u32[]{:S(2)}, u32[]{:S(2)}) %collective-permute-start.1) | collective-permute-done | bytes 393248 | tf_op jit(solution)/shard_map/ppermute | solution.py:23
  24.2 3.7 %fusion.48 = f32[8,32,6,384]{3,1,2,0:T(8,128)S(1)} fusion(f32[8,32,6,384]{3,1,2,0:T(8,128)S(1)} %copy-done.1, f32[8,32,1,384]{3,1,2,0:T(8,128)S(1)} %collective-permute-done.1, f32[8,32,1,384]{3,1,2,0:T(8,128)S(1)} %collective-permute-done, f32[32,6,384]{2,0,1:T(8,128)S(1)} %get-tuple-element.65, f32[32,6,384]{2,0,1:T(8,128)S(1)} %get-tuple-element.66, ...), kind=kLoop, calls=%fused_computation.68 | loop fusion | flops 20054016 | bytes 7274496 | tf_op jit(solution)/shard_map/add | solution.py:81
  28.0 3.6 %collective-permute-start.2 = (f32[8,32,1,384]{3,1,2,0:T(8,128)S(1)}, f32[8,32,1,384]{3,1,2,0:T(8,128)S(1)}, u32[]{:S(2)}, u32[]{:S(2)}) collective-permute-start(f32[8,32,1,384]{3,1,2,0:T(8,128)S(1)} %get-tuple-element.58), channel_id=1, source_target_pairs={{0,8},{8,16},{16,24},{24,32},{32,40},{40,48},{48,56},{56,64},{64,7... | collective-permute-start | bytes 1179656 | tf_op jit(solution)/shard_map/ppermute | solution.py:21
  31.6 1.3 collective-permute-start.3
  32.9 5.5 %collective-permute-done.2 = f32[8,32,1,384]{3,1,2,0:T(8,128)S(1)} collective-permute-done((f32[8,32,1,384]{3,1,2,0:T(8,128)S(1)}, f32[8,32,1,384]{3,1,2,0:T(8,128)S(1)}, u32[]{:S(2)}, u32[]{:S(2)}) %collective-permute-start.2) | collective-permute-done | bytes 393248 | tf_op jit(solution)/shard_map/ppermute | solution.py:21
  38.4 5.7 %collective-permute-done.3 = f32[8,32,1,384]{3,1,2,0:T(8,128)S(1)} collective-permute-done((f32[8,32,1,384]{3,1,2,0:T(8,128)S(1)}, f32[8,32,1,384]{3,1,2,0:T(8,128)S(1)}, u32[]{:S(2)}, u32[]{:S(2)}) %collective-permute-start.3) | collective-permute-done | bytes 393248 | tf_op jit(solution)/shard_map/ppermute | solution.py:23
  44.1 3.7 %fusion.31 = f32[8,32,6,384]{3,1,2,0:T(8,128)S(1)} fusion(f32[8,32,6,384]{3,1,2,0:T(8,128)S(1)} %fusion.48, f32[8,32,1,384]{3,1,2,0:T(8,128)S(1)} %collective-permute-done.3, f32[8,32,1,384]{3,1,2,0:T(8,128)S(1)} %collective-permute-done.2, f32[32,6,384]{2,0,1:T(8,128)S(1)} %get-tuple-element.65, f32[32,6,384]{2,0,1:T(8,128)S(1)} %get-tuple-element.66, ...), kind=kLoop, calls=%fused_computation.49 | loop fusion | flops 20054016 | bytes 7274496 | tf_op jit(solution)/shard_map/add | solution.py:81
  47.9 4.0 %collective-permute-start.4 = (f32[8,32,1,384]{3,1,2,0:T(8,128)S(1)}, f32[8,32,1,384]{3,1,2,0:T(8,128)S(1)}, u32[]{:S(2)}, u32[]{:S(2)}) collective-permute-start(f32[8,32,1,384]{3,1,2,0:T(8,128)S(1)} %get-tuple-element.56), channel_id=1, source_target_pairs={{0,8},{8,16},{16,24},{24,32},{32,40},{40,48},{48,56},{56,64},{64,7... | collective-permute-start | bytes 1179656 | tf_op jit(solution)/shard_map/ppermute | solution.py:21
  51.9 1.3 collective-permute-start.5
  53.2 4.5 %collective-permute-done.4 = f32[8,32,1,384]{3,1,2,0:T(8,128)S(1)} collective-permute-done((f32[8,32,1,384]{3,1,2,0:T(8,128)S(1)}, f32[8,32,1,384]{3,1,2,0:T(8,128)S(1)}, u32[]{:S(2)}, u32[]{:S(2)}) %collective-permute-start.4) | collective-permute-done | bytes 393248 | tf_op jit(solution)/shard_map/ppermute | solution.py:21
  57.7 3.9 %collective-permute-done.5 = f32[8,32,1,384]{3,1,2,0:T(8,128)S(1)} collective-permute-done((f32[8,32,1,384]{3,1,2,0:T(8,128)S(1)}, f32[8,32,1,384]{3,1,2,0:T(8,128)S(1)}, u32[]{:S(2)}, u32[]{:S(2)}) %collective-permute-start.5) | collective-permute-done | bytes 393248 | tf_op jit(solution)/shard_map/ppermute | solution.py:23
  61.5 3.7 %fusion.14 = f32[8,32,6,384]{3,1,2,0:T(8,128)S(1)} fusion(f32[8,32,6,384]{3,1,2,0:T(8,128)S(1)} %fusion.31, f32[8,32,1,384]{3,1,2,0:T(8,128)S(1)} %collective-permute-done.5, f32[8,32,1,384]{3,1,2,0:T(8,128)S(1)} %collective-permute-done.4, f32[32,6,384]{2,0,1:T(8,128)S(1)} %get-tuple-element.65, f32[32,6,384]{2,0,1:T(8,128)S(1)} %get-tuple-element.66, ...), kind=kLoop, calls=%fused_computation.30 | loop fusion | flops 20054016 | bytes 7274496 | tf_op jit(solution)/shard_map/add | solution.py:81
  65.3 2.8 %copy.24 = f32[8,32,6,384]{3,0,2,1:T(8,128)} copy(f32[8,32,6,384]{3,1,2,0:T(8,128)S(1)} %fusion.14) | data formatting | bytes 4718592 | tf_op jit(solution)/shard_map/add | solution.py:81
  68.1 0.6 copy-done.4
  68.7 1.0 copy-done
  69.7 5.9 %copy.25 = f32[8,32,2304]{1,0,2:T(8,128)} copy(f32[8,32,2304]{2,0,1:T(8,128)S(1)} %bitcast.72) | data formatting | bytes 4718592 | tf_op jit(solution)/shard_map/reshape | solution.py:135
  75.6 4.3 %gather_fusion = f32[16,8,32]{2,1,0:T(8,128)S(1)} fusion(f32[8,32,2304]{1,0,2:T(8,128)} %copy.25, s32[1024]{0:T(1024)S(1)} %pad_clamp_fusion), kind=kCustom, calls=%fused_computation | custom fusion | bytes 32832 | tf_op jit(solution)/shard_map/jit(_take)/gather | solution.py:137
  80.1 0.3 reshape.69
  80.3 14.6 %all_to_all.11 = f32[8,1,4096]{2,1,0:T(1,128)S(1)} all-to-all(f32[8,1,4096]{2,1,0:T(1,128)S(1)} %reshape.69), channel_id=1, replica_groups=mesh['rows'=32,'mem'=8] {'mem'}, dimensions={0} | all-to-all | bytes 262144 | tf_op jit(solution)/shard_map/all_to_all | solution.py:38
  95.0 0.6 broadcast.111
  95.6 1.0 reduce.3
  96.5 0.2 reshape.70
  96.9 0.7 convolution_bitcast_fusion.1
  97.8 0.6 convolution_bitcast_fusion.4
  98.4 1.1 broadcast_in_dim.25
  99.5 10.2 %all-to-all-start.1 = ((f32[32,1,4160]{2,1,0:T(1,128)}), f32[32,1,4160]{2,1,0:T(1,128)S(1)}, u32[]{:S(2)}, u32[]{:S(2)}) async-start(f32[32,1,4160]{2,1,0:T(1,128)} %broadcast_in_dim.25), calls=%async_computation.1 | async-start | bytes 1081344 | tf_op jit(solution)/shard_map/all_to_all | solution.py:38
  109.8 14.8 %all-to-all-done.1 = f32[32,1,4160]{2,1,0:T(1,128)S(1)} async-done(((f32[32,1,4160]{2,1,0:T(1,128)}), f32[32,1,4160]{2,1,0:T(1,128)S(1)}, u32[]{:S(2)}, u32[]{:S(2)}) %all-to-all-start.1) | async-done | bytes 532512 | tf_op jit(solution)/shard_map/all_to_all | solution.py:38
  124.6 0.3 reduce_sum.28
  124.9 0.7 multiply_reduce_fusion
  126.5 2.6 %while.13 = (s32[]{:T(128)}, f32[64,64]{0,1:T(8,128)S(1)}, f32[64,64]{1,0:T(8,128)S(1)}, s32[]{:T(128)}) while((s32[]{:T(128)}, f32[64,64]{0,1:T(8,128)S(1)}, f32[64,64]{1,0:T(8,128)S(1)}, s32[]{:T(128)}) %tuple.37), condition=%wide.region_4.5_spmd.clone, body=%wide.region_3.4_spmd.clone.sunk | while | flops 9453570 | bytes 213045 | solution.py:111
  126.5 0.2 fusion.102
  126.9 0.2 convolution_bitcast_fusion.6
  127.1 0.2 fusion.102
  127.5 0.2 convolution_bitcast_fusion.6
  127.8 0.2 fusion.102
  128.2 0.2 convolution_bitcast_fusion.6
  128.4 0.2 fusion.102
  128.8 0.2 convolution_bitcast_fusion.6
  129.2 0.2 fusion.57
  129.4 0.3 fusion.61
  129.7 40.7 %all-gather.2.cloned.1.call-done = f32[64,32,2304]{2,0,1:T(8,128)} async-done(((f32[8,32,2304]{2,0,1:T(8,128)}), f32[64,32,2304]{2,0,1:T(8,128)}) %all-gather.2.cloned.1.call-update) | async-done | bytes 18874384 | tf_op jit(solution)/shard_map/all_gather | solution.py:147
  170.4 12.0 %fusion.69 = f32[8,32,2304]{2,0,1:T(8,128)S(1)} fusion(f32[64,32,2304]{2,0,1:T(8,128)} %all-gather.2.cloned.1.call-done, f32[64,64]{0,1:T(8,128)S(1)} %fusion.61, s32[]{:T(128)S(6)} %select_n.14), kind=kOutput, calls=%fused_computation.113 | convolution fusion | flops 452985344 | bytes 21237764 | tf_op jit(solution)/shard_map/jk,jzc->kzc/dot_general | solution.py:144
  182.4 2.1 %copy.31 = f32[8,32,6,384]{3,1,2,0:T(8,128)} copy(f32[8,32,6,384]{3,0,2,1:T(8,128)S(1)} %bitcast.73) | data formatting | bytes 4718592 | tf_op jit(solution)/shard_map/reshape | solution.py:150
  (41 shorter events, 1.6 us)
Async XLA Ops:
  6.5 17.7 %copy-start.1 = (f32[8,32,6,384]{3,1,2,0:T(8,128)S(1)}, f32[8,32,6,384]{3,1,2,0:T(8,128)}, u32[]{:S(2)}) copy-start(f32[8,32,6,384]{3,1,2,0:T(8,128)} %param.7) | copy-start | bytes 7077892
  6.5 163.9 %all-gather.2.cloned.1.call-start = ((), (), s32[]{:S(2)}) async-start(), calls=%async_computation.2 | async-start | bytes 21233664 | tf_op jit(solution)/shard_map/all_gather | solution.py:147
  7.9 12.1 %collective-permute-start = (f32[8,32,1,384]{3,1,2,0:T(8,128)S(1)}, f32[8,32,1,384]{3,1,2,0:T(8,128)S(1)}, u32[]{:S(2)}, u32[]{:S(2)}) collective-permute-start(f32[8,32,1,384]{3,1,2,0:T(8,128)S(1)} %get-tuple-element.60), channel_id=1, source_target_pairs={{0,8},{8,16},{16,24},{24,32},{32,40},{40,48},{48,56},{56,64},{64,7... | collective-permute-start | bytes 1179656 | tf_op jit(solution)/shard_map/ppermute | solution.py:21
  12.3 11.9 %collective-permute-start.1 = (f32[8,32,1,384]{3,1,2,0:T(8,128)S(1)}, f32[8,32,1,384]{3,1,2,0:T(8,128)S(1)}, u32[]{:S(2)}, u32[]{:S(2)}) collective-permute-start(f32[8,32,1,384]{3,1,2,0:T(8,128)S(1)} %get-tuple-element.61), channel_id=1, source_target_pairs={{8,0},{16,8},{24,16},{32,24},{40,32},{48,40},{56,48},{64,56},{72,6... | collective-permute-start | bytes 1179656 | tf_op jit(solution)/shard_map/ppermute | solution.py:23
  28.0 10.4 %collective-permute-start.2 = (f32[8,32,1,384]{3,1,2,0:T(8,128)S(1)}, f32[8,32,1,384]{3,1,2,0:T(8,128)S(1)}, u32[]{:S(2)}, u32[]{:S(2)}) collective-permute-start(f32[8,32,1,384]{3,1,2,0:T(8,128)S(1)} %get-tuple-element.58), channel_id=1, source_target_pairs={{0,8},{8,16},{16,24},{24,32},{32,40},{40,48},{48,56},{56,64},{64,7... | collective-permute-start | bytes 1179656 | tf_op jit(solution)/shard_map/ppermute | solution.py:21
  31.6 12.5 %collective-permute-start.3 = (f32[8,32,1,384]{3,1,2,0:T(8,128)S(1)}, f32[8,32,1,384]{3,1,2,0:T(8,128)S(1)}, u32[]{:S(2)}, u32[]{:S(2)}) collective-permute-start(f32[8,32,1,384]{3,1,2,0:T(8,128)S(1)} %get-tuple-element.59), channel_id=1, source_target_pairs={{8,0},{16,8},{24,16},{32,24},{40,32},{48,40},{56,48},{64,56},{72,6... | collective-permute-start | bytes 1179656 | tf_op jit(solution)/shard_map/ppermute | solution.py:23
  47.9 9.8 %collective-permute-start.4 = (f32[8,32,1,384]{3,1,2,0:T(8,128)S(1)}, f32[8,32,1,384]{3,1,2,0:T(8,128)S(1)}, u32[]{:S(2)}, u32[]{:S(2)}) collective-permute-start(f32[8,32,1,384]{3,1,2,0:T(8,128)S(1)} %get-tuple-element.56), channel_id=1, source_target_pairs={{0,8},{8,16},{16,24},{24,32},{32,40},{40,48},{48,56},{56,64},{64,7... | collective-permute-start | bytes 1179656 | tf_op jit(solution)/shard_map/ppermute | solution.py:21
  51.9 9.6 %collective-permute-start.5 = (f32[8,32,1,384]{3,1,2,0:T(8,128)S(1)}, f32[8,32,1,384]{3,1,2,0:T(8,128)S(1)}, u32[]{:S(2)}, u32[]{:S(2)}) collective-permute-start(f32[8,32,1,384]{3,1,2,0:T(8,128)S(1)} %get-tuple-element.57), channel_id=1, source_target_pairs={{8,0},{16,8},{24,16},{32,24},{40,32},{48,40},{56,48},{64,56},{72,6... | collective-permute-start | bytes 1179656 | tf_op jit(solution)/shard_map/ppermute | solution.py:23
  68.1 0.7 copy-start.4
  68.1 1.7 copy-start
  75.6 21.2 %copy-start.2 = (f32[32,16]{0,1:T(8,128)S(1)}, f32[32,16]{0,1:T(8,128)}, u32[]{:S(2)}) copy-start(f32[32,16]{0,1:T(8,128)} %param.11) | copy-start | bytes 6148
  75.6 21.2 %copy-start.3 = (f32[32,16]{0,1:T(8,128)S(1)}, f32[32,16]{0,1:T(8,128)}, u32[]{:S(2)}) copy-start(f32[32,16]{0,1:T(8,128)} %param.10) | copy-start | bytes 6148
  99.5 25.1 %all-to-all-start.1 = ((f32[32,1,4160]{2,1,0:T(1,128)}), f32[32,1,4160]{2,1,0:T(1,128)S(1)}, u32[]{:S(2)}, u32[]{:S(2)}) async-start(f32[32,1,4160]{2,1,0:T(1,128)} %broadcast_in_dim.25), calls=%async_computation.1 | async-start | bytes 1081344 | tf_op jit(solution)/shard_map/all_to_all | solution.py:38
Sparse Core Ops, SparseCore 0:
  68.2 102.1 all-gather.1
where the time goes:
time: 192 us; the launch traced here: 191 us
  waiting for transfers between devices  84.3 us (44%)
  starting transfers between devices  26.1 us (14%)
  local copies, waits for them, and re-layouts  20.6 us (11%)
  matrix products  16.3 us (8%)
  other arithmetic  14.8 us (8%)
  blocking collectives  14.6 us (8%)
  between operations  14.4 us (8%)
    all_gather x1, waiting for transfers between devices, per_device(): lax.all_gather(state_vectors, 'mem', axis=0, tiled=True)  40.7 us
    ppermute x3, waiting for transfers between devices, padded_2(): lax.ppermute(tail, axis, [(i, (i + 1) % count) for i in range(ends)])  15.1 us
    all_to_all x1, waiting for transfers between devices, from_everyone(): return lax.all_to_all(copies, axis, split_axis=0, concat_axis=0, tiled=True)  14.8 us
    all_to_all x1, blocking collectives, from_everyone(): return lax.all_to_all(copies, axis, split_axis=0, concat_axis=0, tiled=True)  14.6 us
    ppermute x3, waiting for transfers between devices, padded_2(): lax.ppermute(head, axis, [((i + 1) % count, i) for i in range(ends)])  13.7 us
    ppermute x3, starting transfers between devices, padded_2(): lax.ppermute(tail, axis, [(i, (i + 1) % count) for i in range(ends)])  12 us
    dot_general x1, matrix products, per_device(): jnp.einsum('jk,jzc->kzc', own_columns, lax.all_gather(state_vectors, 'mem...  12 us
    add x3, other arithmetic, advance(): return center + change  11.2 us
  transfers between devices with their start and end apart: 8, of which 8 were waited for; matrix products, arithmetic and copies ran while one was open for 11% of the time, Pallas kernels for 0%

commit v1 on v0

v1 whole, which is shorter than its diff:
```python
import functools
import jax
import jax.numpy as jnp
from jax import lax
from jax.experimental import pallas as pl
from jax.experimental.pallas import tpu as pltpu
from jax.sharding import PartitionSpec as P

NS_ITERS = 4
DIFFUSION = 0.05
INTERPRET = False
F32 = jnp.float32
BF16 = jnp.bfloat16
HIGHEST = lax.Precision.HIGHEST
VM = pl.BlockSpec(memory_space=pltpu.VMEM)
SM = pl.BlockSpec(memory_space=pltpu.SMEM)


def call(body, outs, n_in, name, scratch=(), smem=0, flops=0, nbytes=0):
    single = not isinstance(outs, list)
    shapes = [jax.ShapeDtypeStruct(s, F32) for s in (outs if not single else [outs])]
    return pl.pallas_call(
        body,
        out_shape=shapes[0] if single else shapes,
        in_specs=[SM] * smem + [VM] * (n_in - smem),
        out_specs=VM if single else [VM] * len(shapes),
        scratch_shapes=list(scratch),
        cost_estimate=pl.CostEstimate(flops=flops, transcendentals=0, bytes_accessed=nbytes),
        interpret=INTERPRET,
        name=name,
    )


def members_inside(block):
    return jnp.swapaxes(block, 0, 1)


def edges_body(first_ref, last_ref, first_out, last_out):
    for src, dst in ((first_ref, first_out), (last_ref, last_out)):
        for tile in range(src.shape[2] // 8):
            part = pl.ds(8 * tile, 8)
            dst[part] = members_inside(src[:, 0, part, :])


def middle_body(*refs):
    half = len(refs) // 2
    for src, dst in zip(refs[:half], refs[half:]):
        for tile in range(src.shape[2] // 8):
            part = pl.ds(8 * tile, 8)
            dst[part] = members_inside(src[:, 0, part, :])


def fill_coefficients(coef, courant_ref, rows):
    levels, cells = courant_ref.shape[2], courant_ref.shape[3]
    lane = lax.broadcasted_iota(jnp.int32, (levels, cells), 1)
    level = lax.broadcasted_iota(jnp.int32, (levels, cells), 0)
    for slot, row in enumerate(rows):
        total = None
        for d in range(3):
            a = courant_ref[d, row]
            low = jnp.maximum(a, 0.0) + DIFFUSION
            high = DIFFUSION - jnp.minimum(a, 0.0)
            both = low + high
            total = both if total is None else total + both
            if d == 1:
                low = jnp.where(lane == 0, 0.0, low)
                high = jnp.where(lane == cells - 1, 0.0, high)
            if d == 2:
                low = jnp.where(level == 0, 0.0, low)
                high = jnp.where(level == levels - 1, 0.0, high)
            coef[slot, 2 * d] = low
            coef[slot, 2 * d + 1] = high
        coef[slot, 6] = 1.0 - total


def advance_row(dst, below, here, above, coef, slot):
    levels, members, cells = here.shape

    def level_step(z, carry):
        def k(i):
            return jnp.broadcast_to(coef[slot, i, pl.ds(z, 1), :], (members, cells))

        c = here[z]
        new = c * k(6)
        new += k(0) * below[z] + k(1) * above[z]
        new += k(2) * pltpu.roll(c, 1, 1) + k(3) * pltpu.roll(c, cells - 1, 1)
        new += k(4) * here[jnp.maximum(z - 1, 0)] + k(5) * here[jnp.minimum(z + 1, levels - 1)]
        dst[z] = new
        return carry

    lax.fori_loop(0, levels, level_step, 0, unroll=4)


def step1_edges(e0, e1, e4, e5, lo, hi, courant, f0, f5, coef):
    fill_coefficients(coef, courant, (0, 5))
    advance_row(f0, lo, e0, e1, coef, 0)
    advance_row(f5, e4, e5, hi, coef, 1)


def inner_steps(e0, e1, e2, e3, e4, e5, f0, f5, courant, f1, f4, g1, g2, g3, g4, h2, h3, f2, f3, coef):
    fill_coefficients(coef, courant, (1, 2, 3, 4))
    e = [e0, e1, e2, e3, e4, e5]
    f = [f0, f1, f2, f3, f4, f5]
    g = [None, g1, g2, g3, g4]
    for row in (1, 2, 3, 4):
        advance_row(f[row], e[row - 1], e[row], e[row + 1], coef, row - 1)
    for row in (1, 2, 3, 4):
        advance_row(g[row], f[row - 1], f[row], f[row + 1], coef, row - 1)
    for row, h in ((2, h2), (3, h3)):
        advance_row(h, g[row - 1], g[row], g[row + 1], coef, row - 1)


def pair_step(row_a, row_b, ba, ha, aa, bb, hb, ab, courant, outa, outb, coef):
    fill_coefficients(coef, courant, (row_a, row_b))
    advance_row(outa, ba, ha, aa, coef, 0)
    advance_row(outb, bb, hb, ab, coef, 1)


def last_step(info, lo, g0, g1, g4, g5, hi, h1, h2, h3, h4, courant, *rest):
    chunks, prof, full, coef = rest[:8], rest[8], rest[9], rest[10]
    levels, members, cells = g0.shape
    fill_coefficients(coef, courant, (0, 5))
    for row, h in ((1, h1), (2, h2), (3, h3), (4, h4)):
        full[row] = h[...]
    advance_row(full.at[0], lo, g0, g1, coef, 0)
    advance_row(full.at[5], g4, g5, hi, coef, 1)
    per = prof.shape[1] // levels
    lane = lax.broadcasted_iota(jnp.int32, (members, 128), 1)
    group = 128 // per
    acc = [jnp.zeros((members, 128), F32) for _ in range(levels // group)]
    for p in range(per):
        column = jnp.clip(info[1 + p], 0, 6 * cells - 1)
        row = column // cells
        y = column - row * cells
        tile = y // 128
        shift = p - (y - tile * 128) + 128
        for z in range(levels):
            spot = (z % group) * per
            v = full[row, z, :, pl.ds(pl.multiple_of(tile * 128, 128), 128)]
            v = pltpu.roll(v, lax.rem(shift + spot, 128), 1)
            acc[z // group] = jnp.where(lane == spot + p, v, acc[z // group])
    for i, a in enumerate(acc):
        prof[:, pl.ds(128 * i, 128)] = a
    me = info[0]
    depth = levels // 8
    for k in range(8):
        q = lax.bitwise_xor(me, k)
        for row in range(6):
            chunks[k][row] = full[row, pl.ds(q * depth, depth)]


def gram_body(info, own, other, r1, r2, r3, value, var, out, stack, aug):
    me = info[0]
    x, core = lax.div(me, 2), lax.rem(me, 2)
    members = own.shape[0]
    stack[pl.ds(pl.multiple_of(me * members, members), members), :] = own[...]
    stack[pl.ds(pl.multiple_of(lax.bitwise_xor(me, 1) * members, members), members), :] = other[...]
    for k, r in ((1, r1), (2, r2), (3, r3)):
        mate = 2 * lax.bitwise_xor(x, k) + core
        stack[pl.ds(pl.multiple_of(mate * members, members), members), :] = r[pl.ds(0, members), :]
        mate = lax.bitwise_xor(mate, 1)
        stack[pl.ds(pl.multiple_of(mate * members, members), members), :] = r[pl.ds(members, members), :]
    total = stack.shape[0]
    everyone = stack[...]
    center = jnp.sum(everyone, axis=0, keepdims=True) * (1.0 / total)
    scaling = 1.0 / jnp.sqrt((total - 1.0) * var[...])
    scaled = (everyone - center) * scaling
    innovation = (value[...] - center) / jnp.sqrt(var[...])
    aug[pl.ds(0, total), :] = scaled
    first = lax.broadcasted_iota(jnp.int32, everyone.shape, 0) == 0
    aug[pl.ds(total, total), :] = jnp.where(first, jnp.broadcast_to(innovation, everyone.shape), 0.0)
    out[...] = lax.dot_general(
        scaled, aug[...], (((1,), (1,)), ((), ())), precision=HIGHEST, preferred_element_type=F32
    )


def transform_weights(both):
    n = both.shape[0]
    gram = both[:, :n]
    pull = both[:, n:]

    def dot(a, b):
        return jnp.dot(a, b, precision=HIGHEST, preferred_element_type=F32)

    rows = lax.broadcasted_iota(jnp.int32, (n, n), 0)
    cols = lax.broadcasted_iota(jnp.int32, (n, n), 1)
    eye = jnp.where(rows == cols, 1.0, 0.0).astype(F32)
    system = eye + gram
    squares = jnp.sum(jnp.sum(system * system, axis=1, keepdims=True), axis=0, keepdims=True)
    frobenius = jnp.sqrt(squares)
    y = system / frobenius
    z = None
    for i in range(NS_ITERS):
        factor = 0.5 * (3.0 * eye - (y if z is None else dot(z, y)))
        if i < NS_ITERS - 1:
            y = dot(y, factor)
        z = factor if z is None else dot(factor, z)
    root = z / jnp.sqrt(frobenius)
    shift = dot(root, dot(root, pull)) * (1.0 / (n - 1.0) ** 0.5)
    moved = shift[:, :1] + root
    return moved - jnp.sum(moved, axis=0, keepdims=True) * (1.0 / n) + 1.0 / n


def mix_body(info, own, r1, r2, r3, *rest):
    chunks, outs, w_ref, t_ref = rest[:8], rest[8:16], rest[16], rest[17]
    me = info[0]
    weights = transform_weights(own[...] + r1[...] + r2[...] + r3[...])
    n = weights.shape[0]
    w_ref[...] = weights
    for k in range(8):
        q = lax.bitwise_xor(me, k)
        t_ref[pl.ds(8 * k, 8), :] = w_ref[pl.ds(pl.multiple_of(8 * q, 8), 8), :]
    w_ref[...] = t_ref[...].T
    for k in range(8):
        q = lax.bitwise_xor(me, k)
        t_ref[pl.ds(8 * k, 8), :] = w_ref[pl.ds(pl.multiple_of(8 * q, 8), 8), :]
    left = t_ref[...]
    left_hi = left.astype(BF16)
    left_lo = (left - left_hi.astype(F32)).astype(BF16)
    lhs = jnp.concatenate([left_hi, left_lo, left_hi], axis=1)
    rows, depth = chunks[0].shape[0], chunks[0].shape[1]
    for row in range(rows):
        for z in range(depth):
            f = jnp.concatenate([c[row, z] for c in chunks], axis=0)
            hi = f.astype(BF16)
            lo = (f - hi.astype(F32)).astype(BF16)
            o = jnp.dot(lhs, jnp.concatenate([hi, hi, lo], axis=0), preferred_element_type=F32)
            for k in range(8):
                outs[k][row, z] = o[8 * k : 8 * k + 8]


def place_body(info, *rest):
    parts, out, stack = rest[:8], rest[8], rest[9]
    me = info[0]
    depth = parts[0].shape[1]
    for k in range(8):
        q = lax.bitwise_xor(me, k)
        stack[pl.ds(q * depth, depth)] = parts[k][0]
    for tile in range(stack.shape[0] // 8):
        part = pl.ds(8 * tile, 8)
        out[:, 0, part, :] = members_inside(stack[part])


def per_device(ensemble, courant, obs_column, obs_value, obs_var):
    members, levels, rows, cells = ensemble.shape
    count = lax.axis_size("rows")
    mem = lax.axis_size("mem")
    width = rows * cells
    me = lax.axis_index("mem").astype(jnp.int32)
    info = jnp.concatenate([me[None], obs_column - lax.axis_index("rows").astype(jnp.int32) * width])
    field = jnp.transpose(ensemble, (0, 2, 1, 3))
    flow = jnp.transpose(courant, (0, 2, 1, 3))
    row_shape = (levels, members, cells)
    row_bytes = 4 * levels * members * cells
    coef = lambda n: [pltpu.VMEM((n, 7, levels, cells), F32)]

    def row_spec(row):
        return pl.BlockSpec((members, 1, levels, cells), lambda *_: (0, row, 0, 0))

    def relayout(body, which, name):
        full = pl.BlockSpec(row_shape, lambda *_: (0, 0, 0))
        return pl.pallas_call(
            body,
            grid=(1,),
            out_shape=[jax.ShapeDtypeStruct(row_shape, F32)] * len(which),
            in_specs=[row_spec(r) for r in which],
            out_specs=[full] * len(which),
            interpret=INTERPRET,
            name=name,
        )(*([field] * len(which)))

    up = [(i, i + 1) for i in range(count - 1)]
    down = [(i + 1, i) for i in range(count - 1)]

    def exchange(first, last):
        return lax.ppermute(last, "rows", up), lax.ppermute(first, "rows", down)

    e0, e5 = relayout(edges_body, (0, 5), "edge_rows")
    lo, hi = exchange(e0, e5)
    e1, e2, e3, e4 = relayout(middle_body, (1, 2, 3, 4), "middle_rows")
    f0, f5 = call(step1_edges, [row_shape] * 2, 7, "step1_edges", coef(2), nbytes=8 * row_bytes)(
        e0, e1, e4, e5, lo, hi, flow
    )
    lo, hi = exchange(f0, f5)
    f1, f4, g1, g2, g3, g4, h2, h3 = call(
        inner_steps, [row_shape] * 8, 9, "inner_steps",
        [pltpu.VMEM(row_shape, F32)] * 2 + coef(4), nbytes=16 * row_bytes,
    )(e0, e1, e2, e3, e4, e5, f0, f5, flow)
    g0, g5 = call(functools.partial(pair_step, 0, 5), [row_shape] * 2, 7, "step2_edges", coef(2), nbytes=8 * row_bytes)(
        lo, f0, f1, f4, f5, hi, flow
    )
    lo, hi = exchange(g0, g5)
    h1, h4 = call(functools.partial(pair_step, 1, 4), [row_shape] * 2, 7, "step3_inner", coef(2), nbytes=8 * row_bytes)(
        g0, g1, g2, g3, g4, g5, flow
    )
    depth = levels // mem
    chunk_shape = (rows, depth, members, cells)
    obs = obs_value.size
    *chunks, prof = call(
        last_step, [chunk_shape] * 8 + [(members, obs)], 12, "last_step",
        [pltpu.VMEM((rows,) + row_shape, F32)] + coef(2), smem=1, nbytes=20 * row_bytes,
    )(info, lo, g0, g1, g4, g5, hi, h1, h2, h3, h4, flow)

    def swap(a, k):
        return lax.ppermute(a, "mem", [(i, i ^ k) for i in range(mem)])

    other = swap(prof, 1)
    both = jnp.concatenate([prof, other], axis=0)
    far = [swap(both, 2 * k) for k in (1, 2, 3)]
    moved = [chunks[0]] + [swap(chunks[k], k) for k in range(1, 8)]
    part = call(
        gram_body, (8 * members, 16 * members), 8, "gram",
        [pltpu.VMEM((8 * members, obs), F32), pltpu.VMEM((16 * members, obs), F32)], smem=1, nbytes=1 << 18,
    )(info, prof, other, *far, obs_value.reshape(1, obs), obs_var.reshape(1, obs))

    deep = mem
    wide = count // deep
    total = None
    for dy in range(wide):
        pairs = [
            ((y * deep + z) * mem + m, (((y + dy) % wide) * deep + (z + m) % deep) * mem + m)
            for y in range(wide) for z in range(deep) for m in range(mem)
        ]
        got = lax.ppermute(part, ("rows", "mem"), pairs)
        total = got if total is None else total + got
    total = total + swap(total, 1)
    sums = [swap(total, 2 * k) for k in (1, 2, 3)]
    mixed = call(
        mix_body, [chunk_shape] * 8, 13, "mix",
        [pltpu.VMEM((8 * members, 8 * members), F32)] * 2, smem=1, nbytes=12 * row_bytes,
    )(info, total, *sums, *moved)
    back = [mixed[0]] + [swap(mixed[k], k) for k in range(1, 8)]
    part_spec = pl.BlockSpec((1, depth, members, cells), lambda i: (i, 0, 0, 0))
    placed = pl.pallas_call(
        place_body,
        grid=(rows,),
        out_shape=jax.ShapeDtypeStruct((members, rows, levels, cells), F32),
        in_specs=[SM] + [part_spec] * 8,
        out_specs=pl.BlockSpec((members, 1, levels, cells), lambda i: (0, i, 0, 0)),
        scratch_shapes=[pltpu.VMEM(row_shape, F32)],
        interpret=INTERPRET,
        name="place",
    )(info, *back)
    return jnp.transpose(placed, (0, 2, 1, 3))


def solution(mesh):
    return jax.shard_map(
        per_device,
        mesh=mesh,
        in_specs=(
            P("mem", None, "rows", None),
            P(None, None, "rows", None),
            P("rows"),
            P(None, "rows"),
            P(None, "rows"),
        ),
        out_specs=P("mem", None, "rows", None),
        check_vma=False,
    )
```

time: 192 us -> 196 us (1.021)
  Pallas kernels: 0 us -> 49 us
  starting transfers between devices: 26.1 us -> 68.9 us
  matrix products: 16.3 us -> 0 us
  blocking collectives: 14.6 us -> 0 us
  waiting for transfers between devices: 84.3 us -> 70.1 us
  other arithmetic: 14.8 us -> 0.63 us
  between operations: 14.4 us -> 0.28 us
  local copies, waits for them, and re-layouts: 20.6 us -> 6.56 us
    ppermute x6 -> x32, starting transfers between devices: 15.9 us -> 68.9 us  [the longest x22 40.1 us: swap(): return lax.ppermute(a, 'mem', [(i, i ^ k) for i in range(mem)])]
    pallas_call x0 -> x10, Pallas kernels: none -> 49 us  [the longest x1 12 us: per_device(): call(inner_steps, [row_shape] * 8, 9, 'inner_steps', [pltpu.VMEM(row_shap...]
    ppermute x6 -> x32, waiting for transfers between devices: 28.8 us -> 70.1 us  [the longest x22 56.7 us: swap(): return lax.ppermute(a, 'mem', [(i, i ^ k) for i in range(mem)])]
    all_gather x1 -> x0, waiting for transfers between devices: 40.7 us -> none  [per_device(): lax.all_gather(state_vectors, 'mem', axis=0, tiled=True)]
    dot_general x18 -> x0, matrix products: 16.3 us -> none  [the longest x1 12 us: per_device(): jnp.einsum('jk,jzc->kzc', own_columns, lax.all_gather(state_vectors, 'mem...]
    all_to_all x1 -> x0, waiting for transfers between devices: 14.8 us -> none  [from_everyone(): return lax.all_to_all(copies, axis, split_axis=0, concat_axis=0, tiled=True)]
    all_to_all x1 -> x0, blocking collectives: 14.6 us -> none  [from_everyone(): return lax.all_to_all(copies, axis, split_axis=0, concat_axis=0, tiled=True)]
    add x3 -> x2, other arithmetic: 11.2 us -> 0.02 us  [the longest x1 0.01 us: per_device(): total = got if total is None else total + got]
  transfers between devices with their start and end apart: 8 -> 32, of which waited for: 8 -> 19; matrix products, arithmetic and copies ran while one was open for 11% -> 1% of each run, Pallas kernels for 0% -> 10%
where the time goes in v1:
time: 196 us
  waiting for transfers between devices  70.1 us (36%)
  starting transfers between devices  68.9 us (35%)
  Pallas kernels  49 us (25%)
  local copies, waits for them, and re-layouts  6.56 us (3%)
    ppermute x22, waiting for transfers between devices, swap(): return lax.ppermute(a, 'mem', [(i, i ^ k) for i in range(mem)])  56.7 us
    ppermute x22, starting transfers between devices, swap(): return lax.ppermute(a, 'mem', [(i, i ^ k) for i in range(mem)])  40.1 us
    ppermute x6, starting transfers between devices, exchange(): return (lax.ppermute(last, 'rows', up), lax.ppermute(first, 'rows', down))  17.3 us
    ppermute x6, waiting for transfers between devices, exchange(): return (lax.ppermute(last, 'rows', up), lax.ppermute(first, 'rows', down))  13.4 us
    pallas_call x1, Pallas kernels, per_device(): call(inner_steps, [row_shape] * 8, 9, 'inner_steps', [pltpu.VMEM(row_shap...  12 us
    ppermute x4, starting transfers between devices, per_device(): got = lax.ppermute(part, ('rows', 'mem'), pairs)  11.5 us
    pallas_call x1, Pallas kernels, per_device(): call(last_step, [chunk_shape] * 8 + [(members, obs)], 12, 'last_step', [p...  6.2 us
    pallas_call x1, Pallas kernels, per_device(): call(mix_body, [chunk_shape] * 8, 13, 'mix', [pltpu.VMEM((8 * members, 8...  5.98 us
  transfers between devices with their start and end apart: 32, of which 19 were waited for; matrix products, arithmetic and copies ran while one was open for 1% of the time, Pallas kernels for 10%

profile of v1, /device:TPU:1, one launch (start us, length us, event | category | flops | bytes accessed | tf_op | source)
XLA Modules:
  0.0 195.5 jit_solution(14799384656839632917)
XLA Ops:
  0.0 2.1 %edge_rows.1 = (f32[32,8,384]{2,1,0:T(8,128)}, f32[32,8,384]{2,1,0:T(8,128)}) custom-call(f32[8,6,32,384]{3,2,1,0:T(8,128)} %bitcast.4, f32[8,6,32,384]{3,2,1,0:T(8,128)} %bitcast.5), custom_call_target="tpu_custom_call" | custom-call | tf_op jit(solution)/shard_map/edge_rows/pallas_call | solution.py:262
  2.1 4.4 %collective-permute-start = (f32[32,8,384]{2,1,0:T(8,128)}, f32[32,8,384]{2,1,0:T(8,128)S(1)}, u32[]{:S(2)}, u32[]{:S(2)}) collective-permute-start(f32[32,8,384]{2,1,0:T(8,128)} %get-tuple-element.45.e5), channel_id=1, source_target_pairs={{0,8},{8,16},{16,24},{24,32},{32,40},{40,48},{48,56},{56,64},{64,7... | collective-permute-start | bytes 1179656 | tf_op jit(solution)/shard_map/ppermute | solution.py:276
  6.5 1.3 collective-permute-start.1
  7.8 2.6 %middle_rows.1 = (f32[32,8,384]{2,1,0:T(8,128)}, f32[32,8,384]{2,1,0:T(8,128)}, f32[32,8,384]{2,1,0:T(8,128)}, f32[32,8,384]{2,1,0:T(8,128)}) custom-call(f32[8,6,32,384]{3,2,1,0:T(8,128)} %bitcast.6, f32[8,6,32,384]{3,2,1,0:T(8,128)} %bitcast.7, f32[8,6,32,384]{3,2,1,0:T(8,128)} %bitcast.8, f32[8,6,32,384]{3,2,1,0:T(8,128)} %bitcast.9), custom_call_target="tpu_custom_call" | custom-call | tf_op jit(solution)/shard_map/middle_rows/pallas_call | solution.py:262
  10.4 4.1 %collective-permute-done.lo = f32[32,8,384]{2,1,0:T(8,128)S(1)} collective-permute-done((f32[32,8,384]{2,1,0:T(8,128)}, f32[32,8,384]{2,1,0:T(8,128)S(1)}, u32[]{:S(2)}, u32[]{:S(2)}) %collective-permute-start) | collective-permute-done | bytes 393248 | tf_op jit(solution)/shard_map/ppermute | solution.py:276
  14.5 4.1 %collective-permute-done.1.hi = f32[32,8,384]{2,1,0:T(8,128)S(1)} collective-permute-done((f32[32,8,384]{2,1,0:T(8,128)}, f32[32,8,384]{2,1,0:T(8,128)S(1)}, u32[]{:S(2)}, u32[]{:S(2)}) %collective-permute-start.1) | collective-permute-done | bytes 393248 | tf_op jit(solution)/shard_map/ppermute | solution.py:276
  19.3 4.5 %step1_edges.1 = (f32[32,8,384]{2,1,0:T(8,128)}, f32[32,8,384]{2,1,0:T(8,128)}) custom-call(f32[32,8,384]{2,1,0:T(8,128)} %get-tuple-element.42.e0, f32[32,8,384]{2,1,0:T(8,128)} %get-tuple-element.43.e1, f32[32,8,384]{2,1,0:T(8,128)} %get-tuple-element.44.e4, f32[32,8,384]{2,1,0:T(8,128)} %get-tuple-element.45.e5, f32[32,8,384]{2,1,0:T(8,128)} %copy-done.4, ...), custom_call_target="tpu_custom_call" | custom-call | bytes 3145728 | tf_op jit(solution)/shard_map/step1_edges/pallas_call | solution.py:281
  23.8 3.6 %collective-permute-start.2 = (f32[32,8,384]{2,1,0:T(8,128)}, f32[32,8,384]{2,1,0:T(8,128)S(1)}, u32[]{:S(2)}, u32[]{:S(2)}) collective-permute-start(f32[32,8,384]{2,1,0:T(8,128)} %get-tuple-element.46.f5.hb), channel_id=1, source_target_pairs={{0,8},{8,16},{16,24},{24,32},{32,40},{40,48},{48,56},{56,64},{64,7... | collective-permute-start | bytes 1179656 | tf_op jit(solution)/shard_map/ppermute | solution.py:276
  27.4 1.3 collective-permute-start.3
  28.7 12.0 %inner_steps.1 = (f32[32,8,384]{2,1,0:T(8,128)}, f32[32,8,384]{2,1,0:T(8,128)}, f32[32,8,384]{2,1,0:T(8,128)}, f32[32,8,384]{2,1,0:T(8,128)}, f32[32,8,384]{2,1,...) custom-call(f32[32,8,384]{2,1,0:T(8,128)} %get-tuple-element.42.e0, ...), custom_call_target="tpu_custom_call" | custom-call | bytes 6291456 | tf_op jit(solution)/shard_map/inner_steps/pallas_call | solution.py:285
  41.6 4.5 %step2_edges.1 = (f32[32,8,384]{2,1,0:T(8,128)}, f32[32,8,384]{2,1,0:T(8,128)}) custom-call(f32[32,8,384]{2,1,0:T(8,128)} %copy-done.2, f32[32,8,384]{2,1,0:T(8,128)} %get-tuple-element.47.f0.ha, f32[32,8,384]{2,1,0:T(8,128)} %get-tuple-element.50.aa, f32[32,8,384]{2,1,0:T(8,128)} %get-tuple-element.51.bb, f32[32,8,384]{2,1,0:T(8,128)} %get-tuple-element.46.f5.hb, ...), custom_call_target="tpu_custom_call" | custom-call | bytes 3145728 | tf_op jit(solution)/shard_map/step2_edges/pallas_call | solution.py:289
  46.0 5.5 %collective-permute-start.4 = (f32[32,8,384]{2,1,0:T(8,128)}, f32[32,8,384]{2,1,0:T(8,128)S(1)}, u32[]{:S(2)}, u32[]{:S(2)}) collective-permute-start(f32[32,8,384]{2,1,0:T(8,128)} %get-tuple-element.52.ab.g5), channel_id=1, source_target_pairs={{0,8},{8,16},{16,24},{24,32},{32,40},{40,48},{48,56},{56,64},{64,7... | collective-permute-start | bytes 1179656 | tf_op jit(solution)/shard_map/ppermute | solution.py:276
  51.5 1.3 collective-permute-start.5
  53.4 4.5 %step3_inner.1 = (f32[32,8,384]{2,1,0:T(8,128)}, f32[32,8,384]{2,1,0:T(8,128)}) custom-call(f32[32,8,384]{2,1,0:T(8,128)} %get-tuple-element.53.ba.g0, f32[32,8,384]{2,1,0:T(8,128)} %get-tuple-element.54.ha.g1, f32[32,8,384]{2,1,0:T(8,128)} %get-tuple-element.56.aa, f32[32,8,384]{2,1,0:T(8,128)} %get-tuple-element.57.bb, ...), custom_call_target="tpu_custom_call" | custom-call | bytes 3145728 | tf_op jit(solution)/shard_map/step3_inner/pallas_call | solution.py:293
  58.4 4.7 %collective-permute-done.5.hi = f32[32,8,384]{2,1,0:T(8,128)S(1)} collective-permute-done((f32[32,8,384]{2,1,0:T(8,128)}, f32[32,8,384]{2,1,0:T(8,128)S(1)}, u32[]{:S(2)}, u32[]{:S(2)}) %collective-permute-start.5) | collective-permute-done | bytes 393248 | tf_op jit(solution)/shard_map/ppermute | solution.py:276
  63.9 6.2 %last_step.1 = (f32[6,4,8,384]{3,2,1,0:T(8,128)}, f32[6,4,8,384]{3,2,1,0:T(8,128)}, f32[6,4,8,384]{3,2,1,0:T(8,128)}, f32[6,4,8,384]{3,2,1,0:T(8,128)}, f32[6,4,...) custom-call(s32[17]{0:T(128)} %pad_add_fusion.info, ...), custom_call_target="tpu_custom_call" | custom-call | bytes 7864320 | tf_op jit(solution)/shard_map/last_step/pallas_call | solution.py:299
  70.1 3.0 %collective-permute-start.6 = (f32[8,512]{1,0:T(8,128)}, f32[8,512]{1,0:T(8,128)S(1)}, u32[]{:S(2)}, u32[]{:S(2)}) collective-permute-start(f32[8,512]{1,0:T(8,128)} %get-tuple-element.62.own), channel_id=1, source_target_pairs={{0,1},{1,0},{2,3},{3,2},{4,5},{5,4},{6,7},{7,6},{8,9},{9,8},{10,11... | collective-permute-start | bytes 49160 | tf_op jit(solution)/shard_map/ppermute | solution.py:305
  74.1 1.2 collective-permute-start.7
  75.3 2.5 %collective-permute-start.8 = (f32[16,512]{1,0:T(8,128)S(1)}, f32[16,512]{1,0:T(8,128)S(1)}, u32[]{:S(2)}, u32[]{:S(2)}) collective-permute-start(f32[16,512]{1,0:T(8,128)S(1)} %constant_dynamic-update-slice_fusion), channel_id=1, source_target_pairs={{0,4},{1,5},{2,6},{3,7},{4,0},{5,1},{6,2},{7,3},{8,12},{9,13},{10,... | collective-permute-start | bytes 98312 | tf_op jit(solution)/shard_map/ppermute | solution.py:305
  79.6 2.1 %collective-permute-done.9.r3 = f32[16,512]{1,0:T(8,128)S(1)} collective-permute-done((f32[16,512]{1,0:T(8,128)S(1)}, f32[16,512]{1,0:T(8,128)S(1)}, u32[]{:S(2)}, u32[]{:S(2)}) %collective-permute-start.9) | collective-permute-done | bytes 32800 | tf_op jit(solution)/shard_map/ppermute | solution.py:305
  82.3 1.7 gram.1
  84.1 3.3 %collective-permute-start.10 = (f32[64,128]{1,0:T(8,128)}, f32[64,128]{1,0:T(8,128)S(1)}, u32[]{:S(2)}, u32[]{:S(2)}) collective-permute-start(f32[64,128]{1,0:T(8,128)} %gram.1), channel_id=1, source_target_pairs={{0,0},{1,9},{2,18},{3,27},{4,36},{5,45},{6,54},{7,63},{8,8},{9,17}... | collective-permute-start | bytes 98312 | tf_op jit(solution)/shard_map/ppermute | solution.py:324
  87.4 2.5 %collective-permute-start.11 = (f32[64,128]{1,0:T(8,128)}, f32[64,128]{1,0:T(8,128)S(1)}, u32[]{:S(2)}, u32[]{:S(2)}) collective-permute-start(f32[64,128]{1,0:T(8,128)} %gram.1), channel_id=1, source_target_pairs={{0,64},{1,73},{2,82},{3,91},{4,100},{5,109},{6,118},{7,127},{8,72}... | collective-permute-start | bytes 98312 | tf_op jit(solution)/shard_map/ppermute | solution.py:324
  90.0 4.8 %collective-permute-start.12 = (f32[64,128]{1,0:T(8,128)}, f32[64,128]{1,0:T(8,128)S(1)}, u32[]{:S(2)}, u32[]{:S(2)}) collective-permute-start(f32[64,128]{1,0:T(8,128)} %gram.1), channel_id=1, source_target_pairs={{0,128},{1,137},{2,146},{3,155},{4,164},{5,173},{6,182},{7,191},{8... | collective-permute-start | bytes 98312 | tf_op jit(solution)/shard_map/ppermute | solution.py:324
  95.6 4.3 %collective-permute-start.19 = (f32[6,4,8,384]{3,2,1,0:T(8,128)}, f32[6,4,8,384]{3,2,1,0:T(8,128)S(1)}, u32[]{:S(2)}, u32[]{:S(2)}) collective-permute-start(f32[6,4,8,384]{3,2,1,0:T(8,128)} %get-tuple-element.65), channel_id=1, source_target_pairs={{0,2},{1,3},{2,0},{3,1},{4,6},{5,7},{6,4},{7,5},{8,10},{9,11},{10,... | collective-permute-start | bytes 884744 | tf_op jit(solution)/shard_map/ppermute | solution.py:305
  100.3 0.9 collective-permute-done.14
  101.2 2.7 %collective-permute-start.15 = (f32[64,128]{1,0:T(8,128)S(1)}, f32[64,128]{1,0:T(8,128)S(1)}, u32[]{:S(2)}, u32[]{:S(2)}) collective-permute-start(f32[64,128]{1,0:T(8,128)S(1)} %add.15.own), channel_id=1, source_target_pairs={{0,2},{1,3},{2,0},{3,1},{4,6},{5,7},{6,4},{7,5},{8,10},{9,11},{10,... | collective-permute-start | bytes 98312 | tf_op jit(solution)/shard_map/ppermute | solution.py:305
  104.0 8.2 %collective-permute-start.16 = (f32[64,128]{1,0:T(8,128)S(1)}, f32[64,128]{1,0:T(8,128)S(1)}, u32[]{:S(2)}, u32[]{:S(2)}) collective-permute-start(f32[64,128]{1,0:T(8,128)S(1)} %add.15.own), channel_id=1, source_target_pairs={{0,4},{1,5},{2,6},{3,7},{4,0},{5,1},{6,2},{7,3},{8,12},{9,13},{10,... | collective-permute-start | bytes 98312 | tf_op jit(solution)/shard_map/ppermute | solution.py:305
  112.4 1.7 collective-permute-start.20
  114.1 1.5 collective-permute-done.16.r2
  115.6 1.4 collective-permute-start.21
  117.0 2.3 %collective-permute-start.22 = (f32[6,4,8,384]{3,2,1,0:T(8,128)}, f32[6,4,8,384]{3,2,1,0:T(8,128)S(1)}, u32[]{:S(2)}, u32[]{:S(2)}) collective-permute-start(f32[6,4,8,384]{3,2,1,0:T(8,128)} %get-tuple-element.68), channel_id=1, source_target_pairs={{0,5},{1,4},{2,7},{3,6},{4,1},{5,0},{6,3},{7,2},{8,13},{9,12},{10,... | collective-permute-start | bytes 884744 | tf_op jit(solution)/shard_map/ppermute | solution.py:305
  119.3 2.3 %collective-permute-start.23 = (f32[6,4,8,384]{3,2,1,0:T(8,128)}, f32[6,4,8,384]{3,2,1,0:T(8,128)S(1)}, u32[]{:S(2)}, u32[]{:S(2)}) collective-permute-start(f32[6,4,8,384]{3,2,1,0:T(8,128)} %get-tuple-element.69), channel_id=1, source_target_pairs={{0,6},{1,7},{2,4},{3,5},{4,2},{5,3},{6,0},{7,1},{8,14},{9,15},{10,... | collective-permute-start | bytes 884744 | tf_op jit(solution)/shard_map/ppermute | solution.py:305
  122.1 8.5 %collective-permute-done.21.rest_4_ = f32[6,4,8,384]{3,2,1,0:T(8,128)S(1)} collective-permute-done((f32[6,4,8,384]{3,2,1,0:T(8,128)}, f32[6,4,8,384]{3,2,1,0:T(8,128)S(1)}, u32[]{:S(2)}, u32[]{:S(2)}) %collective-permute-start.21) | collective-permute-done | bytes 294944 | tf_op jit(solution)/shard_map/ppermute | solution.py:305
  130.6 6.5 %collective-permute-done.22.rest_5_ = f32[6,4,8,384]{3,2,1,0:T(8,128)S(1)} collective-permute-done((f32[6,4,8,384]{3,2,1,0:T(8,128)}, f32[6,4,8,384]{3,2,1,0:T(8,128)S(1)}, u32[]{:S(2)}, u32[]{:S(2)}) %collective-permute-start.22) | collective-permute-done | bytes 294944 | tf_op jit(solution)/shard_map/ppermute | solution.py:305
  137.2 5.1 %collective-permute-done.23.rest_6_ = f32[6,4,8,384]{3,2,1,0:T(8,128)S(1)} collective-permute-done((f32[6,4,8,384]{3,2,1,0:T(8,128)}, f32[6,4,8,384]{3,2,1,0:T(8,128)S(1)}, u32[]{:S(2)}, u32[]{:S(2)}) %collective-permute-start.23) | collective-permute-done | bytes 294944 | tf_op jit(solution)/shard_map/ppermute | solution.py:305
  142.3 6.3 %collective-permute-done.24.rest_7_ = f32[6,4,8,384]{3,2,1,0:T(8,128)S(1)} collective-permute-done((f32[6,4,8,384]{3,2,1,0:T(8,128)}, f32[6,4,8,384]{3,2,1,0:T(8,128)S(1)}, u32[]{:S(2)}, u32[]{:S(2)}) %collective-permute-start.24) | collective-permute-done | bytes 294944 | tf_op jit(solution)/shard_map/ppermute | solution.py:305
  149.3 6.0 %mix.1 = (f32[6,4,8,384]{3,2,1,0:T(8,128)}, f32[6,4,8,384]{3,2,1,0:T(8,128)}, f32[6,4,8,384]{3,2,1,0:T(8,128)}, f32[6,4,8,384]{3,2,1,0:T(8,128)}, f32[6,4,8,384]...) custom-call(s32[17]{0:T(128)} %pad_add_fusion.info, ...), custom_call_target="tpu_custom_call" | custom-call | bytes 4718592 | tf_op jit(solution)/shard_map/mix/pallas_call | solution.py:328
  155.7 1.7 collective-permute-start.27
  158.3 2.3 %collective-permute-start.29 = (f32[6,4,8,384]{3,2,1,0:T(8,128)}, f32[6,4,8,384]{3,2,1,0:T(8,128)S(1)}, u32[]{:S(2)}, u32[]{:S(2)}) collective-permute-start(f32[6,4,8,384]{3,2,1,0:T(8,128)} %get-tuple-element.76), channel_id=1, source_target_pairs={{0,5},{1,4},{2,7},{3,6},{4,1},{5,0},{6,3},{7,2},{8,13},{9,12},{10,... | collective-permute-start | bytes 884744 | tf_op jit(solution)/shard_map/ppermute | solution.py:305
  160.7 1.4 collective-permute-start.30
  162.1 2.3 %collective-permute-done.26.rest_2_ = f32[6,4,8,384]{3,2,1,0:T(8,128)S(1)} collective-permute-done((f32[6,4,8,384]{3,2,1,0:T(8,128)}, f32[6,4,8,384]{3,2,1,0:T(8,128)S(1)}, u32[]{:S(2)}, u32[]{:S(2)}) %collective-permute-start.26) | collective-permute-done | bytes 294944 | tf_op jit(solution)/shard_map/ppermute | solution.py:305
  164.3 2.8 %collective-permute-start.31 = (f32[6,4,8,384]{3,2,1,0:T(8,128)}, f32[6,4,8,384]{3,2,1,0:T(8,128)S(1)}, u32[]{:S(2)}, u32[]{:S(2)}) collective-permute-start(f32[6,4,8,384]{3,2,1,0:T(8,128)} %get-tuple-element.78), channel_id=1, source_target_pairs={{0,7},{1,6},{2,5},{3,4},{4,3},{5,2},{6,1},{7,0},{8,15},{9,14},{10,... | collective-permute-start | bytes 884744 | tf_op jit(solution)/shard_map/ppermute | solution.py:305
  167.1 4.7 %collective-permute-done.27.rest_3_ = f32[6,4,8,384]{3,2,1,0:T(8,128)S(1)} collective-permute-done((f32[6,4,8,384]{3,2,1,0:T(8,128)}, f32[6,4,8,384]{3,2,1,0:T(8,128)S(1)}, u32[]{:S(2)}, u32[]{:S(2)}) %collective-permute-start.27) | collective-permute-done | bytes 294944 | tf_op jit(solution)/shard_map/ppermute | solution.py:305
  171.8 6.3 %collective-permute-done.28.rest_4_ = f32[6,4,8,384]{3,2,1,0:T(8,128)S(1)} collective-permute-done((f32[6,4,8,384]{3,2,1,0:T(8,128)}, f32[6,4,8,384]{3,2,1,0:T(8,128)S(1)}, u32[]{:S(2)}, u32[]{:S(2)}) %collective-permute-start.28) | collective-permute-done | bytes 294944 | tf_op jit(solution)/shard_map/ppermute | solution.py:305
  178.1 6.6 %collective-permute-done.29.rest_5_ = f32[6,4,8,384]{3,2,1,0:T(8,128)S(1)} collective-permute-done((f32[6,4,8,384]{3,2,1,0:T(8,128)}, f32[6,4,8,384]{3,2,1,0:T(8,128)S(1)}, u32[]{:S(2)}, u32[]{:S(2)}) %collective-permute-start.29) | collective-permute-done | bytes 294944 | tf_op jit(solution)/shard_map/ppermute | solution.py:305
  184.8 5.0 %collective-permute-done.31.rest_7_ = f32[6,4,8,384]{3,2,1,0:T(8,128)S(1)} collective-permute-done((f32[6,4,8,384]{3,2,1,0:T(8,128)}, f32[6,4,8,384]{3,2,1,0:T(8,128)S(1)}, u32[]{:S(2)}, u32[]{:S(2)}) %collective-permute-start.31) | collective-permute-done | bytes 294944 | tf_op jit(solution)/shard_map/ppermute | solution.py:305
  190.5 5.0 %place.1 = f32[8,6,32,384]{3,2,1,0:T(8,128)} custom-call(s32[17]{0:T(128)} %pad_add_fusion.info, f32[6,4,8,384]{3,2,1,0:T(8,128)} %get-tuple-element.71.rest_0_, f32[6,4,8,384]{3,2,1,0:T(8,128)} %copy-done.6, f32[6,4,8,384]{3,2,1,0:T(8,128)} %copy-done.7, f32[6,4,8,384]{3,2,1,0:T(8,128)} %copy-done.8, f32[6,4,8,384]{3,2,1,0:T(8,128)} %copy-done.9, ...), custom_call_target="tpu_custom_call" | custom-call | tf_op jit(solution)/shard_map/place/pallas_call | solution.py:334
  (98 shorter events, 11.6 us)
Async XLA Ops:
  2.1 12.5 %collective-permute-start = (f32[32,8,384]{2,1,0:T(8,128)}, f32[32,8,384]{2,1,0:T(8,128)S(1)}, u32[]{:S(2)}, u32[]{:S(2)}) collective-permute-start(f32[32,8,384]{2,1,0:T(8,128)} %get-tuple-element.45.e5), channel_id=1, source_target_pairs={{0,8},{8,16},{16,24},{24,32},{32,40},{40,48},{48,56},{56,64},{64,7... | collective-permute-start | bytes 1179656 | tf_op jit(solution)/shard_map/ppermute | solution.py:276
  6.5 12.1 %collective-permute-start.1 = (f32[32,8,384]{2,1,0:T(8,128)}, f32[32,8,384]{2,1,0:T(8,128)S(1)}, u32[]{:S(2)}, u32[]{:S(2)}) collective-permute-start(f32[32,8,384]{2,1,0:T(8,128)} %get-tuple-element.42.e0), channel_id=1, source_target_pairs={{8,0},{16,8},{24,16},{32,24},{40,32},{48,40},{56,48},{64,56},{72,6... | collective-permute-start | bytes 1179656 | tf_op jit(solution)/shard_map/ppermute | solution.py:276
  23.8 16.9 %collective-permute-start.2 = (f32[32,8,384]{2,1,0:T(8,128)}, f32[32,8,384]{2,1,0:T(8,128)S(1)}, u32[]{:S(2)}, u32[]{:S(2)}) collective-permute-start(f32[32,8,384]{2,1,0:T(8,128)} %get-tuple-element.46.f5.hb), channel_id=1, source_target_pairs={{0,8},{8,16},{16,24},{24,32},{32,40},{40,48},{48,56},{56,64},{64,7... | collective-permute-start | bytes 1179656 | tf_op jit(solution)/shard_map/ppermute | solution.py:276
  27.4 13.3 %collective-permute-start.3 = (f32[32,8,384]{2,1,0:T(8,128)}, f32[32,8,384]{2,1,0:T(8,128)S(1)}, u32[]{:S(2)}, u32[]{:S(2)}) collective-permute-start(f32[32,8,384]{2,1,0:T(8,128)} %get-tuple-element.47.f0.ha), channel_id=1, source_target_pairs={{8,0},{16,8},{24,16},{32,24},{40,32},{48,40},{56,48},{64,56},{72,6... | collective-permute-start | bytes 1179656 | tf_op jit(solution)/shard_map/ppermute | solution.py:276
  40.7 12.1 %copy-start.30 = (s32[16]{0:T(128)S(1)}, s32[16]{0:T(128)}, u32[]{:S(2)}) copy-start(s32[16]{0:T(128)} %param.7) | copy-start | bytes 196
  46.0 12.4 %collective-permute-start.4 = (f32[32,8,384]{2,1,0:T(8,128)}, f32[32,8,384]{2,1,0:T(8,128)S(1)}, u32[]{:S(2)}, u32[]{:S(2)}) collective-permute-start(f32[32,8,384]{2,1,0:T(8,128)} %get-tuple-element.52.ab.g5), channel_id=1, source_target_pairs={{0,8},{8,16},{16,24},{24,32},{32,40},{40,48},{48,56},{56,64},{64,7... | collective-permute-start | bytes 1179656 | tf_op jit(solution)/shard_map/ppermute | solution.py:276
  51.5 11.6 %collective-permute-start.5 = (f32[32,8,384]{2,1,0:T(8,128)}, f32[32,8,384]{2,1,0:T(8,128)S(1)}, u32[]{:S(2)}, u32[]{:S(2)}) collective-permute-start(f32[32,8,384]{2,1,0:T(8,128)} %get-tuple-element.53.ba.g0), channel_id=1, source_target_pairs={{8,0},{16,8},{24,16},{32,24},{40,32},{48,40},{56,48},{64,56},{72,6... | collective-permute-start | bytes 1179656 | tf_op jit(solution)/shard_map/ppermute | solution.py:276
  63.9 14.1 %copy-start.28 = (f32[32,16]{0,1:T(8,128)S(1)}, f32[32,16]{0,1:T(8,128)}, u32[]{:S(2)}) copy-start(f32[32,16]{0,1:T(8,128)} %param.8) | copy-start | bytes 6148
  63.9 14.8 %copy-start.29 = (f32[32,16]{0,1:T(8,128)S(1)}, f32[32,16]{0,1:T(8,128)}, u32[]{:S(2)}) copy-start(f32[32,16]{0,1:T(8,128)} %param.9) | copy-start | bytes 6148
  70.1 4.0 %collective-permute-start.6 = (f32[8,512]{1,0:T(8,128)}, f32[8,512]{1,0:T(8,128)S(1)}, u32[]{:S(2)}, u32[]{:S(2)}) collective-permute-start(f32[8,512]{1,0:T(8,128)} %get-tuple-element.62.own), channel_id=1, source_target_pairs={{0,1},{1,0},{2,3},{3,2},{4,5},{5,4},{6,7},{7,6},{8,9},{9,8},{10,11... | collective-permute-start | bytes 49160 | tf_op jit(solution)/shard_map/ppermute | solution.py:305
  74.1 5.4 %collective-permute-start.7 = (f32[16,512]{1,0:T(8,128)S(1)}, f32[16,512]{1,0:T(8,128)S(1)}, u32[]{:S(2)}, u32[]{:S(2)}) collective-permute-start(f32[16,512]{1,0:T(8,128)S(1)} %constant_dynamic-update-slice_fusion), channel_id=1, source_target_pairs={{0,2},{1,3},{2,0},{3,1},{4,6},{5,7},{6,4},{7,5},{8,10},{9,11},{10,... | collective-permute-start | bytes 98312 | tf_op jit(solution)/shard_map/ppermute | solution.py:305
  75.3 4.3 %collective-permute-start.8 = (f32[16,512]{1,0:T(8,128)S(1)}, f32[16,512]{1,0:T(8,128)S(1)}, u32[]{:S(2)}, u32[]{:S(2)}) collective-permute-start(f32[16,512]{1,0:T(8,128)S(1)} %constant_dynamic-update-slice_fusion), channel_id=1, source_target_pairs={{0,4},{1,5},{2,6},{3,7},{4,0},{5,1},{6,2},{7,3},{8,12},{9,13},{10,... | collective-permute-start | bytes 98312 | tf_op jit(solution)/shard_map/ppermute | solution.py:305
  77.8 4.0 %collective-permute-start.9 = (f32[16,512]{1,0:T(8,128)S(1)}, f32[16,512]{1,0:T(8,128)S(1)}, u32[]{:S(2)}, u32[]{:S(2)}) collective-permute-start(f32[16,512]{1,0:T(8,128)S(1)} %constant_dynamic-update-slice_fusion), channel_id=1, source_target_pairs={{0,6},{1,7},{2,4},{3,5},{4,2},{5,3},{6,0},{7,1},{8,14},{9,15},{10,... | collective-permute-start | bytes 98312 | tf_op jit(solution)/shard_map/ppermute | solution.py:305
  84.1 11.5 %collective-permute-start.10 = (f32[64,128]{1,0:T(8,128)}, f32[64,128]{1,0:T(8,128)S(1)}, u32[]{:S(2)}, u32[]{:S(2)}) collective-permute-start(f32[64,128]{1,0:T(8,128)} %gram.1), channel_id=1, source_target_pairs={{0,0},{1,9},{2,18},{3,27},{4,36},{5,45},{6,54},{7,63},{8,8},{9,17}... | collective-permute-start | bytes 98312 | tf_op jit(solution)/shard_map/ppermute | solution.py:324
  87.4 12.4 %collective-permute-start.11 = (f32[64,128]{1,0:T(8,128)}, f32[64,128]{1,0:T(8,128)S(1)}, u32[]{:S(2)}, u32[]{:S(2)}) collective-permute-start(f32[64,128]{1,0:T(8,128)} %gram.1), channel_id=1, source_target_pairs={{0,64},{1,73},{2,82},{3,91},{4,100},{5,109},{6,118},{7,127},{8,72}... | collective-permute-start | bytes 98312 | tf_op jit(solution)/shard_map/ppermute | solution.py:324
  90.0 9.9 %collective-permute-start.12 = (f32[64,128]{1,0:T(8,128)}, f32[64,128]{1,0:T(8,128)S(1)}, u32[]{:S(2)}, u32[]{:S(2)}) collective-permute-start(f32[64,128]{1,0:T(8,128)} %gram.1), channel_id=1, source_target_pairs={{0,128},{1,137},{2,146},{3,155},{4,164},{5,173},{6,182},{7,191},{8... | collective-permute-start | bytes 98312 | tf_op jit(solution)/shard_map/ppermute | solution.py:324
  94.8 5.1 %collective-permute-start.13 = (f32[64,128]{1,0:T(8,128)}, f32[64,128]{1,0:T(8,128)S(1)}, u32[]{:S(2)}, u32[]{:S(2)}) collective-permute-start(f32[64,128]{1,0:T(8,128)} %gram.1), channel_id=1, source_target_pairs={{0,192},{1,201},{2,210},{3,219},{4,228},{5,237},{6,246},{7,255},{8... | collective-permute-start | bytes 98312 | tf_op jit(solution)/shard_map/ppermute | solution.py:324
  95.6 23.7 %collective-permute-start.18 = (f32[6,4,8,384]{3,2,1,0:T(8,128)}, f32[6,4,8,384]{3,2,1,0:T(8,128)S(1)}, u32[]{:S(2)}, u32[]{:S(2)}) collective-permute-start(f32[6,4,8,384]{3,2,1,0:T(8,128)} %get-tuple-element.64), channel_id=1, source_target_pairs={{0,1},{1,0},{2,3},{3,2},{4,5},{5,4},{6,7},{7,6},{8,9},{9,8},{10,11... | collective-permute-start | bytes 884744 | tf_op jit(solution)/shard_map/ppermute | solution.py:305
  95.6 26.1 %collective-permute-start.19 = (f32[6,4,8,384]{3,2,1,0:T(8,128)}, f32[6,4,8,384]{3,2,1,0:T(8,128)S(1)}, u32[]{:S(2)}, u32[]{:S(2)}) collective-permute-start(f32[6,4,8,384]{3,2,1,0:T(8,128)} %get-tuple-element.65), channel_id=1, source_target_pairs={{0,2},{1,3},{2,0},{3,1},{4,6},{5,7},{6,4},{7,5},{8,10},{9,11},{10,... | collective-permute-start | bytes 884744 | tf_op jit(solution)/shard_map/ppermute | solution.py:305
  99.9 1.3 collective-permute-start.14
  101.2 47.4 %copy-start.20 = (f32[64,128]{1,0:T(8,128)}, f32[64,128]{1,0:T(8,128)S(1)}, u32[]{:S(2)}) copy-start(f32[64,128]{1,0:T(8,128)S(1)} %add.15.own) | copy-start | bytes 98308
  101.2 11.2 %collective-permute-start.15 = (f32[64,128]{1,0:T(8,128)S(1)}, f32[64,128]{1,0:T(8,128)S(1)}, u32[]{:S(2)}, u32[]{:S(2)}) collective-permute-start(f32[64,128]{1,0:T(8,128)S(1)} %add.15.own), channel_id=1, source_target_pairs={{0,2},{1,3},{2,0},{3,1},{4,6},{5,7},{6,4},{7,5},{8,10},{9,11},{10,... | collective-permute-start | bytes 98312 | tf_op jit(solution)/shard_map/ppermute | solution.py:305
  104.0 11.6 %collective-permute-start.16 = (f32[64,128]{1,0:T(8,128)S(1)}, f32[64,128]{1,0:T(8,128)S(1)}, u32[]{:S(2)}, u32[]{:S(2)}) collective-permute-start(f32[64,128]{1,0:T(8,128)S(1)} %add.15.own), channel_id=1, source_target_pairs={{0,4},{1,5},{2,6},{3,7},{4,0},{5,1},{6,2},{7,3},{8,12},{9,13},{10,... | collective-permute-start | bytes 98312 | tf_op jit(solution)/shard_map/ppermute | solution.py:305
  112.2 4.8 %collective-permute-start.17 = (f32[64,128]{1,0:T(8,128)S(1)}, f32[64,128]{1,0:T(8,128)S(1)}, u32[]{:S(2)}, u32[]{:S(2)}) collective-permute-start(f32[64,128]{1,0:T(8,128)S(1)} %add.15.own), channel_id=1, source_target_pairs={{0,6},{1,7},{2,4},{3,5},{4,2},{5,3},{6,0},{7,1},{8,14},{9,15},{10,... | collective-permute-start | bytes 98312 | tf_op jit(solution)/shard_map/ppermute | solution.py:305
  112.4 36.2 %copy-start.22 = (f32[64,128]{1,0:T(8,128)}, f32[64,128]{1,0:T(8,128)S(1)}, u32[]{:S(2)}) copy-start(f32[64,128]{1,0:T(8,128)S(1)} %collective-permute-done.15.r1) | copy-start | bytes 98308
  112.4 9.7 %collective-permute-start.20 = (f32[6,4,8,384]{3,2,1,0:T(8,128)}, f32[6,4,8,384]{3,2,1,0:T(8,128)S(1)}, u32[]{:S(2)}, u32[]{:S(2)}) collective-permute-start(f32[6,4,8,384]{3,2,1,0:T(8,128)} %get-tuple-element.66), channel_id=1, source_target_pairs={{0,3},{1,2},{2,1},{3,0},{4,7},{5,6},{6,5},{7,4},{8,11},{9,10},{10,... | collective-permute-start | bytes 884744 | tf_op jit(solution)/shard_map/ppermute | solution.py:305
  115.6 33.0 %copy-start.23 = (f32[64,128]{1,0:T(8,128)}, f32[64,128]{1,0:T(8,128)S(1)}, u32[]{:S(2)}) copy-start(f32[64,128]{1,0:T(8,128)S(1)} %collective-permute-done.16.r2) | copy-start | bytes 98308
  115.6 15.1 %collective-permute-start.21 = (f32[6,4,8,384]{3,2,1,0:T(8,128)}, f32[6,4,8,384]{3,2,1,0:T(8,128)S(1)}, u32[]{:S(2)}, u32[]{:S(2)}) collective-permute-start(f32[6,4,8,384]{3,2,1,0:T(8,128)} %get-tuple-element.67), channel_id=1, source_target_pairs={{0,4},{1,5},{2,6},{3,7},{4,0},{5,1},{6,2},{7,3},{8,12},{9,13},{10,... | collective-permute-start | bytes 884744 | tf_op jit(solution)/shard_map/ppermute | solution.py:305
  117.0 31.6 %copy-start.24 = (f32[64,128]{1,0:T(8,128)}, f32[64,128]{1,0:T(8,128)S(1)}, u32[]{:S(2)}) copy-start(f32[64,128]{1,0:T(8,128)S(1)} %collective-permute-done.17.r3) | copy-start | bytes 98308
  117.0 20.2 %collective-permute-start.22 = (f32[6,4,8,384]{3,2,1,0:T(8,128)}, f32[6,4,8,384]{3,2,1,0:T(8,128)S(1)}, u32[]{:S(2)}, u32[]{:S(2)}) collective-permute-start(f32[6,4,8,384]{3,2,1,0:T(8,128)} %get-tuple-element.68), channel_id=1, source_target_pairs={{0,5},{1,4},{2,7},{3,6},{4,1},{5,0},{6,3},{7,2},{8,13},{9,12},{10,... | collective-permute-start | bytes 884744 | tf_op jit(solution)/shard_map/ppermute | solution.py:305
  119.3 29.3 %copy-start.13 = (f32[6,4,8,384]{3,2,1,0:T(8,128)}, f32[6,4,8,384]{3,2,1,0:T(8,128)S(1)}, u32[]{:S(2)}) copy-start(f32[6,4,8,384]{3,2,1,0:T(8,128)S(1)} %collective-permute-done.18.rest_1_) | copy-start | bytes 884740
  119.3 23.0 %collective-permute-start.23 = (f32[6,4,8,384]{3,2,1,0:T(8,128)}, f32[6,4,8,384]{3,2,1,0:T(8,128)S(1)}, u32[]{:S(2)}, u32[]{:S(2)}) collective-permute-start(f32[6,4,8,384]{3,2,1,0:T(8,128)} %get-tuple-element.69), channel_id=1, source_target_pairs={{0,6},{1,7},{2,4},{3,5},{4,2},{5,3},{6,0},{7,1},{8,14},{9,15},{10,... | collective-permute-start | bytes 884744 | tf_op jit(solution)/shard_map/ppermute | solution.py:305
  121.6 27.0 %copy-start.14 = (f32[6,4,8,384]{3,2,1,0:T(8,128)}, f32[6,4,8,384]{3,2,1,0:T(8,128)S(1)}, u32[]{:S(2)}) copy-start(f32[6,4,8,384]{3,2,1,0:T(8,128)S(1)} %collective-permute-done.19.rest_2_) | copy-start | bytes 884740
  121.6 27.0 %collective-permute-start.24 = (f32[6,4,8,384]{3,2,1,0:T(8,128)}, f32[6,4,8,384]{3,2,1,0:T(8,128)S(1)}, u32[]{:S(2)}, u32[]{:S(2)}) collective-permute-start(f32[6,4,8,384]{3,2,1,0:T(8,128)} %get-tuple-element.70), channel_id=1, source_target_pairs={{0,7},{1,6},{2,5},{3,4},{4,3},{5,2},{6,1},{7,0},{8,15},{9,14},{10,... | collective-permute-start | bytes 884744 | tf_op jit(solution)/shard_map/ppermute | solution.py:305
  122.1 26.5 %copy-start.15 = (f32[6,4,8,384]{3,2,1,0:T(8,128)}, f32[6,4,8,384]{3,2,1,0:T(8,128)S(1)}, u32[]{:S(2)}) copy-start(f32[6,4,8,384]{3,2,1,0:T(8,128)S(1)} %collective-permute-done.20.rest_3_) | copy-start | bytes 884740
  130.6 18.0 %copy-start.16 = (f32[6,4,8,384]{3,2,1,0:T(8,128)}, f32[6,4,8,384]{3,2,1,0:T(8,128)S(1)}, u32[]{:S(2)}) copy-start(f32[6,4,8,384]{3,2,1,0:T(8,128)S(1)} %collective-permute-done.21.rest_4_) | copy-start | bytes 884740
  137.2 11.5 %copy-start.17 = (f32[6,4,8,384]{3,2,1,0:T(8,128)}, f32[6,4,8,384]{3,2,1,0:T(8,128)S(1)}, u32[]{:S(2)}) copy-start(f32[6,4,8,384]{3,2,1,0:T(8,128)S(1)} %collective-permute-done.22.rest_5_) | copy-start | bytes 884740
  155.3 5.4 %collective-permute-start.25 = (f32[6,4,8,384]{3,2,1,0:T(8,128)}, f32[6,4,8,384]{3,2,1,0:T(8,128)S(1)}, u32[]{:S(2)}, u32[]{:S(2)}) collective-permute-start(f32[6,4,8,384]{3,2,1,0:T(8,128)} %get-tuple-element.72), channel_id=1, source_target_pairs={{0,1},{1,0},{2,3},{3,2},{4,5},{5,4},{6,7},{7,6},{8,9},{9,8},{10,11... | collective-permute-start | bytes 884744 | tf_op jit(solution)/shard_map/ppermute | solution.py:305
  155.7 8.7 %collective-permute-start.26 = (f32[6,4,8,384]{3,2,1,0:T(8,128)}, f32[6,4,8,384]{3,2,1,0:T(8,128)S(1)}, u32[]{:S(2)}, u32[]{:S(2)}) collective-permute-start(f32[6,4,8,384]{3,2,1,0:T(8,128)} %get-tuple-element.73), channel_id=1, source_target_pairs={{0,2},{1,3},{2,0},{3,1},{4,6},{5,7},{6,4},{7,5},{8,10},{9,11},{10,... | collective-permute-start | bytes 884744 | tf_op jit(solution)/shard_map/ppermute | solution.py:305
  155.7 16.1 %collective-permute-start.27 = (f32[6,4,8,384]{3,2,1,0:T(8,128)}, f32[6,4,8,384]{3,2,1,0:T(8,128)S(1)}, u32[]{:S(2)}, u32[]{:S(2)}) collective-permute-start(f32[6,4,8,384]{3,2,1,0:T(8,128)} %get-tuple-element.74), channel_id=1, source_target_pairs={{0,3},{1,2},{2,1},{3,0},{4,7},{5,6},{6,5},{7,4},{8,11},{9,10},{10,... | collective-permute-start | bytes 884744 | tf_op jit(solution)/shard_map/ppermute | solution.py:305
  157.4 20.7 %collective-permute-start.28 = (f32[6,4,8,384]{3,2,1,0:T(8,128)}, f32[6,4,8,384]{3,2,1,0:T(8,128)S(1)}, u32[]{:S(2)}, u32[]{:S(2)}) collective-permute-start(f32[6,4,8,384]{3,2,1,0:T(8,128)} %get-tuple-element.75), channel_id=1, source_target_pairs={{0,4},{1,5},{2,6},{3,7},{4,0},{5,1},{6,2},{7,3},{8,12},{9,13},{10,... | collective-permute-start | bytes 884744 | tf_op jit(solution)/shard_map/ppermute | solution.py:305
  158.3 26.5 %collective-permute-start.29 = (f32[6,4,8,384]{3,2,1,0:T(8,128)}, f32[6,4,8,384]{3,2,1,0:T(8,128)S(1)}, u32[]{:S(2)}, u32[]{:S(2)}) collective-permute-start(f32[6,4,8,384]{3,2,1,0:T(8,128)} %get-tuple-element.76), channel_id=1, source_target_pairs={{0,5},{1,4},{2,7},{3,6},{4,1},{5,0},{6,3},{7,2},{8,13},{9,12},{10,... | collective-permute-start | bytes 884744 | tf_op jit(solution)/shard_map/ppermute | solution.py:305
  160.7 29.1 %copy-start.6 = (f32[6,4,8,384]{3,2,1,0:T(8,128)}, f32[6,4,8,384]{3,2,1,0:T(8,128)S(1)}, u32[]{:S(2)}) copy-start(f32[6,4,8,384]{3,2,1,0:T(8,128)S(1)} %collective-permute-done.25.rest_1_) | copy-start | bytes 884740
  160.7 24.1 %collective-permute-start.30 = (f32[6,4,8,384]{3,2,1,0:T(8,128)}, f32[6,4,8,384]{3,2,1,0:T(8,128)S(1)}, u32[]{:S(2)}, u32[]{:S(2)}) collective-permute-start(f32[6,4,8,384]{3,2,1,0:T(8,128)} %get-tuple-element.77), channel_id=1, source_target_pairs={{0,6},{1,7},{2,4},{3,5},{4,2},{5,3},{6,0},{7,1},{8,14},{9,15},{10,... | collective-permute-start | bytes 884744 | tf_op jit(solution)/shard_map/ppermute | solution.py:305
  164.3 25.5 %copy-start.7 = (f32[6,4,8,384]{3,2,1,0:T(8,128)}, f32[6,4,8,384]{3,2,1,0:T(8,128)S(1)}, u32[]{:S(2)}) copy-start(f32[6,4,8,384]{3,2,1,0:T(8,128)S(1)} %collective-permute-done.26.rest_2_) | copy-start | bytes 884740
  164.3 25.5 %collective-permute-start.31 = (f32[6,4,8,384]{3,2,1,0:T(8,128)}, f32[6,4,8,384]{3,2,1,0:T(8,128)S(1)}, u32[]{:S(2)}, u32[]{:S(2)}) collective-permute-start(f32[6,4,8,384]{3,2,1,0:T(8,128)} %get-tuple-element.78), channel_id=1, source_target_pairs={{0,7},{1,6},{2,5},{3,4},{4,3},{5,2},{6,1},{7,0},{8,15},{9,14},{10,... | collective-permute-start | bytes 884744 | tf_op jit(solution)/shard_map/ppermute | solution.py:305
  171.8 18.0 %copy-start.8 = (f32[6,4,8,384]{3,2,1,0:T(8,128)}, f32[6,4,8,384]{3,2,1,0:T(8,128)S(1)}, u32[]{:S(2)}) copy-start(f32[6,4,8,384]{3,2,1,0:T(8,128)S(1)} %collective-permute-done.27.rest_3_) | copy-start | bytes 884740
  178.1 11.7 %copy-start.9 = (f32[6,4,8,384]{3,2,1,0:T(8,128)}, f32[6,4,8,384]{3,2,1,0:T(8,128)S(1)}, u32[]{:S(2)}) copy-start(f32[6,4,8,384]{3,2,1,0:T(8,128)S(1)} %collective-permute-done.28.rest_4_) | copy-start | bytes 884740
  (15 other events, 42.4 us)

commit v2 on v1

v2 whole, which is shorter than its diff:
```python
import functools
import jax
import jax.numpy as jnp
from jax import lax
from jax.experimental import pallas as pl
from jax.experimental.pallas import tpu as pltpu
from jax.sharding import PartitionSpec as P

NS_ITERS = 4
DIFFUSION = 0.05
INTERPRET = False
F32 = jnp.float32
BF16 = jnp.bfloat16
HIGHEST = lax.Precision.HIGHEST
VM = pl.BlockSpec(memory_space=pltpu.VMEM)
SM = pl.BlockSpec(memory_space=pltpu.SMEM)
PARAMS = pltpu.CompilerParams(vmem_limit_bytes=16 * 2**20)
ROUTE = (1, 3, 2)


def call(body, outs, n_in, scratch=(), smem=0, flops=0, nbytes=0):
    single = not isinstance(outs, list)
    shapes = [jax.ShapeDtypeStruct(s, F32) for s in (outs if not single else [outs])]
    return pl.pallas_call(
        body,
        out_shape=shapes[0] if single else shapes,
        in_specs=[SM] * smem + [VM] * (n_in - smem),
        out_specs=VM if single else [VM] * len(shapes),
        scratch_shapes=list(scratch),
        cost_estimate=pl.CostEstimate(flops=flops, transcendentals=0, bytes_accessed=nbytes),
        compiler_params=PARAMS,
        interpret=INTERPRET,
    )


def members_inside(block):
    return jnp.swapaxes(block, 0, 1)


def relayout_row(src, dst):
    for tile in range(src.shape[2] // 8):
        part = pl.ds(8 * tile, 8)
        dst[part] = members_inside(src[:, 0, part, :])


def rows_body(first_ref, last_ref, first_out, last_out):
    relayout_row(first_ref, first_out)
    relayout_row(last_ref, last_out)


def rows_courant_body(first_ref, last_ref, courant, first_out, last_out):
    core = lax.rem(lax.axis_index("mem"), 2)
    levels = first_ref.shape[2]
    for src, dst, row in ((first_ref, first_out, core), (last_ref, last_out, courant.shape[1] - 2 + core)):
        relayout_row(src, dst)
        for d in range(3):
            for tile in range(levels // 8):
                dst[levels + d * (levels // 8) + tile] = courant[d, row, pl.ds(8 * tile, 8), :]


def sum4_body(a, b, c, d, out):
    out[...] = (a[...] + b[...]) + (c[...] + d[...])


def coefficients(coef, slot, tile, levels, speeds, keep=None):
    shape = speeds[0].shape
    lane = lax.broadcasted_iota(jnp.int32, shape, 1)
    level = lax.broadcasted_iota(jnp.int32, shape, 0)
    part = pl.ds(8 * tile, 8)
    total = None
    for d, a in enumerate(speeds):
        low = jnp.maximum(a, 0.0) + DIFFUSION
        high = DIFFUSION - jnp.minimum(a, 0.0)
        both = low + high
        total = both if total is None else total + both
        if d == 1:
            low = jnp.where(lane == 0, 0.0, low)
            high = jnp.where(lane == shape[1] - 1, 0.0, high)
        if d == 2 and tile == 0:
            low = jnp.where(level == 0, 0.0, low)
        if d == 2 and tile == levels // 8 - 1:
            high = jnp.where(level == 7, 0.0, high)
        coef[slot, 2 * d, part] = low if keep is None else low * keep
        coef[slot, 2 * d + 1, part] = high if keep is None else high * keep
    center = 1.0 - total
    coef[slot, 6, part] = center if keep is None else center * keep


def own_coefficients(courant, coef):
    levels = courant.shape[2]
    for row in range(courant.shape[1]):
        for tile in range(levels // 8):
            coefficients(coef, row, tile, levels, [courant[d, row, pl.ds(8 * tile, 8), :] for d in range(3)])


def halo_coefficients(coef, halos):
    core = lax.rem(lax.axis_index("mem"), 2)
    block = lax.axis_index("rows")
    inside = (block > 0, block < lax.axis_size("rows") - 1)
    tiles = halos[0].shape[0] // 11
    levels = 8 * tiles
    for side in range(2):
        keep = jnp.where(inside[side], 1.0, 0.0).astype(F32)
        for part, j in ((halos[2 * side], core), (halos[2 * side + 1], 1 - core)):
            for tile in range(tiles):
                speeds = [part[levels + d * tiles + tile] for d in range(3)]
                coefficients(coef, 2 * side + j, tile, levels, speeds, keep)


def advance_row(dst, below, here, above, coef, slot):
    levels, members, cells = dst.shape

    def level_step(z, carry):
        before, c = carry

        def k(i):
            return jnp.broadcast_to(coef[slot, i, pl.ds(z, 1), :], (members, cells))

        after = here[jnp.minimum(z + 1, levels - 1)]
        new = c * k(6)
        new += k(0) * below[z] + k(1) * above[z]
        new += k(2) * pltpu.roll(c, 1, 1) + k(3) * pltpu.roll(c, cells - 1, 1)
        new += k(4) * before + k(5) * after
        dst[z] = new
        return c, after

    first = here[0]
    lax.fori_loop(0, levels, level_step, (first, first), unroll=32)


def stage_a(lo1, e0, e1, e2, e3, e4, e5, hi1, coef, f0, f1, f4, f5, g1, g2, g3, g4, h2, h3, f2, f3):
    e = [lo1, e0, e1, e2, e3, e4, e5, hi1]
    f = [f0, f1, f2, f3, f4, f5]
    g = [None, g1, g2, g3, g4]
    for row in range(6):
        advance_row(f[row], e[row], e[row + 1], e[row + 2], coef, row)
    for row in (1, 2, 3, 4):
        advance_row(g[row], f[row - 1], f[row], f[row + 1], coef, row)
    for row, h in ((2, h2), (3, h3)):
        advance_row(h, g[row - 1], g[row], g[row + 1], coef, row)


def stage_b(lo2, lo2x, hi2, hi2x, lo1, e0, hi1, e5, f0, f1, f4, f5, g1, g2, g3, g4, coef, *outs):
    fm, fp, g0, g5, h1, h4, side = outs
    halo_coefficients(side, (lo2, lo2x, hi2, hi2x))
    advance_row(fm, lo2, lo1, e0, side, 1)
    advance_row(fp, e5, hi1, hi2, side, 2)
    advance_row(g0, fm, f0, f1, coef, 0)
    advance_row(g5, f4, f5, fp, coef, 5)
    advance_row(h1, g0, g1, g2, coef, 1)
    advance_row(h4, g3, g4, g5, coef, 4)


def stage_c(obs_column, *refs):
    lo3, lo2, lo1, fm, f0, g0, g1, hi3, hi2, hi1, fp, f5, g5, g4, h1, h2, h3, h4, coef, side = refs[:20]
    chunks, prof, one, two, full = refs[20:24], refs[24], refs[25], refs[26], refs[27]
    levels, members, cells = g0.shape
    me = lax.axis_index("mem")
    origin = lax.axis_index("rows") * (6 * cells)
    for row, h in ((1, h1), (2, h2), (3, h3), (4, h4)):
        full[row] = h[...]
    advance_row(one, lo3, lo2, lo1, side, 0)
    advance_row(two, one, fm, f0, side, 1)
    advance_row(full.at[0], two, g0, g1, coef, 0)
    advance_row(one, hi1, hi2, hi3, side, 3)
    advance_row(two, f5, fp, one, side, 2)
    advance_row(full.at[5], g4, g5, two, coef, 5)
    per = prof.shape[1] // levels
    lane = lax.broadcasted_iota(jnp.int32, (members, 128), 1)
    group = 128 // levels
    acc = [jnp.zeros((members, 128), F32) for _ in range(per // group)]
    for p in range(per):
        column = jnp.clip(obs_column[p] - origin, 0, 6 * cells - 1)
        row = lax.div(column, cells)
        y = column - row * cells
        tile = lax.div(y, 128)
        shift = 128 - (y - tile * 128)
        for z in range(levels):
            spot = (p % group) * levels + z
            v = full[row, z, :, pl.ds(pl.multiple_of(tile * 128, 128), 128)]
            v = pltpu.roll(v, lax.rem(shift + spot, 128), 1)
            acc[p // group] = jnp.where(lane == spot, v, acc[p // group])
    for i, a in enumerate(acc):
        prof[:, pl.ds(128 * i, 128)] = a
    depth = levels // 4
    for k in range(4):
        chip = lax.bitwise_xor(lax.div(me, 2), k)
        for row in range(6):
            chunks[k][row] = full[row, pl.ds(chip * depth, depth)]


def flat_rows(ref):
    return jnp.concatenate([ref[pl.ds(p, 1), :] for p in range(ref.shape[0])], axis=1)


def gram_body(*refs):
    profiles, (value, var, out, stack, aug) = refs[:8], refs[8:]
    me = lax.axis_index("mem")
    members = profiles[0].shape[0]
    for k, profile in enumerate(profiles):
        mate = lax.bitwise_xor(me, k)
        stack[pl.ds(pl.multiple_of(mate * members, members), members), :] = profile[...]
    total = stack.shape[0]
    everyone = stack[...]
    center = jnp.sum(everyone, axis=0, keepdims=True) * (1.0 / total)
    variance = flat_rows(var)
    scaling = 1.0 / jnp.sqrt((total - 1.0) * variance)
    scaled = (everyone - center) * scaling
    innovation = (flat_rows(value) - center) / jnp.sqrt(variance)
    aug[pl.ds(0, total), :] = scaled
    first = lax.broadcasted_iota(jnp.int32, everyone.shape, 0) == 0
    aug[pl.ds(total, total), :] = jnp.where(first, jnp.broadcast_to(innovation, everyone.shape), 0.0)
    out[...] = lax.dot_general(
        scaled, aug[...], (((1,), (1,)), ((), ())), precision=HIGHEST, preferred_element_type=F32
    )


def transform_weights(both):
    n = both.shape[0]
    gram = both[:, :n]
    pull = both[:, n:]

    def dot(a, b):
        return jnp.dot(a, b, precision=HIGHEST, preferred_element_type=F32)

    rows = lax.broadcasted_iota(jnp.int32, (n, n), 0)
    cols = lax.broadcasted_iota(jnp.int32, (n, n), 1)
    eye = jnp.where(rows == cols, 1.0, 0.0).astype(F32)
    system = eye + gram
    squares = jnp.sum(jnp.sum(system * system, axis=1, keepdims=True), axis=0, keepdims=True)
    frobenius = jnp.sqrt(squares)
    y = system / frobenius
    z = None
    for i in range(NS_ITERS):
        factor = 0.5 * (3.0 * eye - (y if z is None else dot(z, y)))
        if i < NS_ITERS - 1:
            y = dot(y, factor)
        z = factor if z is None else dot(factor, z)
    root = z / jnp.sqrt(frobenius)
    shift = dot(root, dot(root, pull)) * (1.0 / (n - 1.0) ** 0.5)
    moved = shift[:, :1] + root
    return moved - jnp.sum(moved, axis=0, keepdims=True) * (1.0 / n) + 1.0 / n


def weights_body(own, other, lhs, w_ref, t_ref):
    me = lax.axis_index("mem")
    weights = transform_weights(own[...] + other[...])
    w_ref[...] = weights
    for k in range(8):
        q = lax.bitwise_xor(me, k)
        t_ref[pl.ds(8 * k, 8), :] = w_ref[pl.ds(pl.multiple_of(8 * q, 8), 8), :]
    w_ref[...] = t_ref[...].T
    for k in range(8):
        q = lax.bitwise_xor(me, k)
        t_ref[pl.ds(8 * k, 8), :] = w_ref[pl.ds(pl.multiple_of(8 * q, 8), 8), :]
    left = t_ref[...]
    high = left.astype(BF16).astype(F32)
    lhs[...] = jnp.concatenate([high, left - high, high], axis=1)


def mix_body(left, *rest):
    chunks, outs = rest[:8], rest[8:]
    lhs = left[...].astype(BF16)
    rows, depth = outs[0].shape[1], outs[0].shape[2]
    start = lax.rem(lax.axis_index("mem"), 2) * depth
    for row in range(rows):
        for z in range(depth):
            f = jnp.concatenate([c[row, start + z] for c in chunks], axis=0)
            hi = f.astype(BF16)
            lo = (f - hi.astype(F32)).astype(BF16)
            o = jnp.dot(lhs, jnp.concatenate([hi, hi, lo], axis=0), preferred_element_type=F32)
            for k in range(8):
                outs[k // 2][k % 2, row, z] = o[8 * k : 8 * k + 8]


def place_body(distance, same, cross, *rest):
    out, stack, block, sem = rest[-4:]
    me = lax.axis_index("mem")
    core, chip = lax.rem(me, 2), lax.bitwise_xor(lax.div(me, 2), distance)
    rows, depth = same.shape[1], same.shape[2]
    for row in range(rows):
        stack[pl.ds(core * depth, depth)] = same[0, row]
        stack[pl.ds((1 - core) * depth, depth)] = cross[1, row]
        block[:, row] = members_inside(stack[...])
    levels = pl.ds(pl.multiple_of(chip * 8, 8), 8)
    copy = pltpu.make_async_copy(block, out.at[:, :, levels, :], sem)
    copy.start()
    copy.wait()


def per_device(ensemble, courant, obs_column, obs_value, obs_var):
    members, levels, rows, cells = ensemble.shape
    count = lax.axis_size("rows")
    mem = lax.axis_size("mem")
    field = jnp.transpose(ensemble, (0, 2, 1, 3))
    if not INTERPRET:
        field = pltpu.with_memory_space_constraint(field, pltpu.HBM)
    flow = jnp.transpose(courant, (0, 2, 1, 3))
    row_shape = (levels, members, cells)
    row_bytes = 4 * levels * members * cells

    def row_spec(row):
        return pl.BlockSpec((members, 1, levels, cells), lambda *_: (0, row, 0, 0))

    def relayout(which, with_courant=False):
        full = pl.BlockSpec(row_shape, lambda *_: (0, 0, 0))
        shapes = [jax.ShapeDtypeStruct(row_shape, F32)] * 2
        in_specs, out_specs, args = [row_spec(r) for r in which], [full] * 2, [field, field]
        if with_courant:
            shape = (levels + 3 * levels // 8, members, cells)
            shapes = [jax.ShapeDtypeStruct(shape, F32)] * 2
            in_specs.append(VM)
            out_specs = [pl.BlockSpec(shape, lambda *_: (0, 0, 0))] * 2
            args.append(flow)
        return pl.pallas_call(
            rows_courant_body if with_courant else rows_body,
            grid=(1,),
            out_shape=shapes,
            in_specs=in_specs,
            out_specs=out_specs,
            compiler_params=PARAMS,
            interpret=INTERPRET,
        )(*args)

    up = [(i, i + 1) for i in range(count - 1)]
    down = [(i + 1, i) for i in range(count - 1)]

    def exchange(first, last):
        return lax.ppermute(last, "rows", up), lax.ppermute(first, "rows", down)

    def swap(a, k):
        return lax.ppermute(a, "mem", [(i, i ^ k) for i in range(mem)])

    e0, e5 = relayout((0, 5))
    lo1, hi1 = exchange(e0, e5)
    e1, e4 = relayout((1, 4), True)
    lo2, hi2 = exchange(e1, e4)
    e2, e3 = relayout((2, 3))
    lo3, hi3 = exchange(e2, e3)
    lo2x, hi2x = swap(lo2, 1), swap(hi2, 1)
    coef = call(own_coefficients, (rows, 7, levels, cells), 1, nbytes=7 * row_bytes)(flow)

    f0, f1, f4, f5, g1, g2, g3, g4, h2, h3 = call(
        stage_a, [row_shape] * 10, 9, [pltpu.VMEM(row_shape, F32)] * 2, nbytes=20 * row_bytes,
    )(lo1, e0, e1, e2, e3, e4, e5, hi1, coef)
    fm, fp, g0, g5, h1, h4, side = call(
        stage_b, [row_shape] * 6 + [(4, 7, levels, cells)], 17, nbytes=20 * row_bytes,
    )(lo2, lo2x, hi2, hi2x, lo1, e0, hi1, e5, f0, f1, f4, f5, g1, g2, g3, g4, coef)
    chips = mem // 2
    obs = obs_value.size
    *chunks, prof = call(
        stage_c, [(rows, levels // chips, members, cells)] * chips + [(members, obs)], 21,
        [pltpu.VMEM(row_shape, F32)] * 2 + [pltpu.VMEM((rows,) + row_shape, F32)],
        smem=1, nbytes=30 * row_bytes,
    )(obs_column, lo3, lo2, lo1, fm, f0, g0, g1, hi3, hi2, hi1, fp, f5, g5, g4, h1, h2, h3, h4, coef, side)

    def along_chips(parts):
        got = {0: parts[0]}
        for k in ROUTE:
            got[k] = swap(parts[k], 2 * k)
        return [(got[k], swap(got[k], 1)) for k in (0,) + ROUTE]

    far = [swap(prof, 2 * k) for k in (1, 2, 3)]
    profiles = []
    for a in [prof] + far:
        profiles += [a, swap(a, 1)]
    pairs = dict(zip((0,) + ROUTE, along_chips(chunks)))
    moved = [block for k in range(chips) for block in pairs[k]]
    part = call(
        gram_body, (8 * members, 16 * members), 10,
        [pltpu.VMEM((8 * members, obs), F32), pltpu.VMEM((16 * members, obs), F32)], nbytes=1 << 18,
    )(*profiles, obs_value.T, obs_var.T)

    deep = mem
    wide = count // deep

    def shifted(a, dy, dz):
        pairs = [
            ((y * deep + z) * mem + m, (((y + dy) % wide) * deep + (z + dz[m % 2]) % deep) * mem + m)
            for y in range(wide) for z in range(deep) for m in range(mem)
        ]
        return lax.ppermute(a, ("rows", "mem"), pairs)

    got = [shifted(part, 0, dz) for dz in ((1, -1), (2, -2), (3, -3), (0, 4))]
    sum4 = call(sum4_body, part.shape, 4, nbytes=1 << 17)
    total = sum4(*got)
    if wide == 4:
        total = sum4(total, *[shifted(total, dy, (0, 0)) for dy in range(1, wide)])
    n = 8 * members
    left = call(weights_body, (n, 3 * n), 2, [pltpu.VMEM((n, n), F32)] * 2, nbytes=1 << 17)(total, swap(total, 1))
    mixed = call(mix_body, [(2, rows, levels // mem, members, cells)] * chips, 9, nbytes=18 * row_bytes)(left, *moved)
    placed = None
    shape = (members, rows, levels, cells)
    for k, (same, cross) in zip((0,) + ROUTE, along_chips(mixed)):
        placed = pl.pallas_call(
            functools.partial(place_body, k),
            out_shape=jax.ShapeDtypeStruct(shape, F32),
            in_specs=[VM, VM] + ([] if placed is None else [pl.BlockSpec(memory_space=pl.ANY)]),
            out_specs=pl.BlockSpec(memory_space=pl.ANY),
            scratch_shapes=[
                pltpu.VMEM((8, members, cells), F32),
                pltpu.VMEM((members, rows, 8, cells), F32),
                pltpu.SemaphoreType.DMA,
            ],
            input_output_aliases={} if placed is None else {2: 0},
            compiler_params=PARAMS,
            interpret=INTERPRET,
        )(same, cross, *([] if placed is None else [placed]))
    return jnp.transpose(placed, (0, 2, 1, 3))


def solution(mesh):
    return jax.shard_map(
        per_device,
        mesh=mesh,
        in_specs=(
            P("mem", None, "rows", None),
            P(None, None, "rows", None),
            P("rows"),
            P(None, "rows"),
            P(None, "rows"),
        ),
        out_specs=P("mem", None, "rows", None),
        check_vma=False,
    )
```

time: 196 us -> 179 us (0.913)
  Pallas kernels: 49 us -> 20.6 us
  waiting for transfers between devices: 70.1 us -> 86.6 us
  local copies, waits for them, and re-layouts: 6.56 us -> 1.18 us
    pallas_call x10 -> x16, Pallas kernels: 49 us -> 20.6 us  [the longest x4 3.96 us: per_device(): pl.pallas_call(functools.partial(place_body, k), out_shape=jax.ShapeDtype...]
    ppermute x4 -> x7, waiting for transfers between devices: 0.01 us -> 14.3 us  [shifted(): return lax.ppermute(a, ('rows', 'mem'), pairs)]
    ppermute x4 -> x7, starting transfers between devices: 11.5 us -> 24.6 us  [shifted(): return lax.ppermute(a, ('rows', 'mem'), pairs)]
    ppermute x22 -> x24, starting transfers between devices: 40.1 us -> 28.1 us  [swap(): return lax.ppermute(a, 'mem', [(i, i ^ k) for i in range(mem)])]
    unnamed x65 -> x10, local copies, waits for them, and re-layouts: 5.21 us -> 1.18 us
    ppermute x22 -> x24, waiting for transfers between devices: 56.7 us -> 59.1 us  [swap(): return lax.ppermute(a, 'mem', [(i, i ^ k) for i in range(mem)])]
  transfers between devices with their start and end apart: 32 -> 37, of which waited for: 19 -> 24; matrix products, arithmetic and copies ran while one was open for 1% -> 0% of each run, Pallas kernels for 10% -> 8%
where the time goes in v2:
time: 179 us; the launch traced here: 178 us
  waiting for transfers between devices  86.6 us (48%)
  starting transfers between devices  69.5 us (39%)
  Pallas kernels  20.6 us (12%)
    ppermute x24, waiting for transfers between devices, swap(): return lax.ppermute(a, 'mem', [(i, i ^ k) for i in range(mem)])  59.1 us
    ppermute x24, starting transfers between devices, swap(): return lax.ppermute(a, 'mem', [(i, i ^ k) for i in range(mem)])  28.1 us
    ppermute x7, starting transfers between devices, shifted(): return lax.ppermute(a, ('rows', 'mem'), pairs)  24.6 us
    ppermute x6, starting transfers between devices, exchange(): return (lax.ppermute(last, 'rows', up), lax.ppermute(first, 'rows', down))  16.7 us
    ppermute x7, waiting for transfers between devices, shifted(): return lax.ppermute(a, ('rows', 'mem'), pairs)  14.3 us
    ppermute x6, waiting for transfers between devices, exchange(): return (lax.ppermute(last, 'rows', up), lax.ppermute(first, 'rows', down))  13.1 us
    pallas_call x4, Pallas kernels, per_device(): pl.pallas_call(functools.partial(place_body, k), out_shape=jax.ShapeDtype...  3.96 us
    pallas_call x3, Pallas kernels, relayout(): pl.pallas_call(rows_courant_body if with_courant else rows_body, grid=(1,...  3.79 us
  transfers between devices with their start and end apart: 37, of which 24 were waited for; matrix products, arithmetic and copies ran while one was open for 0% of the time, Pallas kernels for 8%

profile of v2, /device:TPU:1, one launch (start us, length us, event | category | flops | bytes accessed | tf_op | source)
XLA Modules:
  0.0 178.3 jit_solution(4201862479924256004)
XLA Ops:
  0.0 1.2 copy-done
  1.2 1.3 shard_map.56
  2.4 4.4 %collective-permute-start.1 = (f32[44,8,384]{2,1,0:T(8,128)S(1)}, f32[44,8,384]{2,1,0:T(8,128)S(1)}, u32[]{:S(2)}, u32[]{:S(2)}) collective-permute-start(f32[44,8,384]{2,1,0:T(8,128)S(1)} %get-tuple-element.38.e4), channel_id=1, source_target_pairs={{0,8},{8,16},{16,24},{24,32},{32,40},{40,48},{48,56},{56,64},{64,7... | collective-permute-start | bytes 1622024 | tf_op jit(solution)/shard_map/ppermute | solution.py:329
  6.8 1.3 collective-permute-start.4
  8.1 1.3 shard_map.57
  9.4 4.2 %collective-permute-start.2 = (f32[32,8,384]{2,1,0:T(8,128)S(1)}, f32[32,8,384]{2,1,0:T(8,128)S(1)}, u32[]{:S(2)}, u32[]{:S(2)}) collective-permute-start(f32[32,8,384]{2,1,0:T(8,128)S(1)} %get-tuple-element.39.e5), channel_id=1, source_target_pairs={{0,8},{8,16},{16,24},{24,32},{32,40},{40,48},{48,56},{56,64},{64,7... | collective-permute-start | bytes 1179656 | tf_op jit(solution)/shard_map/ppermute | solution.py:329
  13.6 4.2 %collective-permute-done.1.lo2.refs_1_ = f32[44,8,384]{2,1,0:T(8,128)S(1)} collective-permute-done((f32[44,8,384]{2,1,0:T(8,128)S(1)}, f32[44,8,384]{2,1,0:T(8,128)S(1)}, u32[]{:S(2)}, u32[]{:S(2)}) %collective-permute-start.1) | collective-permute-done | bytes 540704 | tf_op jit(solution)/shard_map/ppermute | solution.py:329
  17.7 2.7 %collective-permute-start.3 = (f32[44,8,384]{2,1,0:T(8,128)S(1)}, f32[44,8,384]{2,1,0:T(8,128)S(1)}, u32[]{:S(2)}, u32[]{:S(2)}) collective-permute-start(f32[44,8,384]{2,1,0:T(8,128)S(1)} %collective-permute-done.1.lo2.refs_1_), channel_id=1, source_target_pairs={{0,1},{1,0},{2,3},{3,2},{4,5},{5,4},{6,7},{7,6},{8,9},{9,8},{10,11... | collective-permute-start | bytes 1622024 | tf_op jit(solution)/shard_map/ppermute | solution.py:332
  20.4 1.5 collective-permute-done.4.hi2.refs_8_
  21.9 1.7 collective-permute-start.5
  23.6 1.4 collective-permute-start.6
  25.0 1.3 shard_map.55
  26.3 4.2 %collective-permute-start = (f32[32,8,384]{2,1,0:T(8,128)S(1)}, f32[32,8,384]{2,1,0:T(8,128)S(1)}, u32[]{:S(2)}, u32[]{:S(2)}) collective-permute-start(f32[32,8,384]{2,1,0:T(8,128)S(1)} %get-tuple-element.37.e3), channel_id=1, source_target_pairs={{0,8},{8,16},{16,24},{24,32},{32,40},{40,48},{48,56},{56,64},{64,7... | collective-permute-start | bytes 1179656 | tf_op jit(solution)/shard_map/ppermute | solution.py:329
  30.5 1.3 collective-permute-start.7
  32.0 4.6 %collective-permute-done.6.hi1.refs_9_ = f32[32,8,384]{2,1,0:T(8,128)S(1)} collective-permute-done((f32[32,8,384]{2,1,0:T(8,128)S(1)}, f32[32,8,384]{2,1,0:T(8,128)S(1)}, u32[]{:S(2)}, u32[]{:S(2)}) %collective-permute-start.6) | collective-permute-done | bytes 393248 | tf_op jit(solution)/shard_map/ppermute | solution.py:329
  36.6 3.3 %shard_map.59 = (f32[32,8,384]{2,1,0:T(8,128)S(1)}, f32[32,8,384]{2,1,0:T(8,128)S(1)}, f32[32,8,384]{2,1,0:T(8,128)S(1)}, f32[32,8,384]{2,1,0:T(8,128)S(1)}, f32...) custom-call(f32[32,8,384]{2,1,0:T(8,128)S(1)} %collective-permute-do, ...), custom_call_target="tpu_custom_call" | custom-call | bytes 7864320 | tf_op jit(solution)/shard_map/pallas_call | solution.py:343
  40.0 2.2 %shard_map.60 = (f32[32,8,384]{2,1,0:T(8,128)S(1)}, f32[32,8,384]{2,1,0:T(8,128)S(1)}, f32[32,8,384]{2,1,0:T(8,128)S(1)}, f32[32,8,384]{2,1,0:T(8,128)S(1)}, f32...) custom-call(f32[44,8,384]{2,1,0:T(8,128)S(1)} %collective-permute-done.1.lo2.refs_1_, ...), custom_call_target="tpu_custom_call" | custom-call | bytes 7864320 | tf_op jit(solution)/shard_map/pallas_call | solution.py:346
  42.2 2.8 %collective-permute-done.7.refs_7_ = f32[32,8,384]{2,1,0:T(8,128)S(1)} collective-permute-done((f32[32,8,384]{2,1,0:T(8,128)S(1)}, f32[32,8,384]{2,1,0:T(8,128)S(1)}, u32[]{:S(2)}, u32[]{:S(2)}) %collective-permute-start.7) | collective-permute-done | bytes 393248 | tf_op jit(solution)/shard_map/ppermute | solution.py:329
  45.1 3.8 %shard_map.61 = (f32[6,8,8,384]{3,2,1,0:T(8,128)S(1)}, f32[6,8,8,384]{3,2,1,0:T(8,128)S(1)}, f32[6,8,8,384]{3,2,1,0:T(8,128)S(1)}, f32[6,8,8,384]{3,2,1,0:T(8,128)S(1)}, f32[8,512]{1,0:T(8,128)S(1)}) custom-call(s32[16]{0:T(128)S(1)} %copy-done.4, f32[32,8,384]{2,1,0:T(8,128)S(1)} %collective-permute-done.refs_0_, ...), custom_call_target="tpu_custom_call" | custom-call | bytes 11796480 | tf_op jit(solution)/shard_map/pallas_call | solution.py:351
  48.8 1.3 collective-permute-start.24
  50.1 2.5 %collective-permute-start.26 = (f32[6,8,8,384]{3,2,1,0:T(8,128)S(1)}, f32[6,8,8,384]{3,2,1,0:T(8,128)S(1)}, u32[]{:S(2)}, u32[]{:S(2)}) collective-permute-start(f32[6,8,8,384]{3,2,1,0:T(8,128)S(1)} %get-tuple-element.63), channel_id=1, source_target_pairs={{0,4},{1,5},{2,6},{3,7},{4,0},{5,1},{6,2},{7,3},{8,12},{9,13},{10,... | collective-permute-start | bytes 1769480 | tf_op jit(solution)/shard_map/ppermute | solution.py:332
  52.8 1.5 collective-permute-start.23
  54.3 8.8 %collective-permute-done.24.rest_2_ = f32[6,8,8,384]{3,2,1,0:T(8,128)S(1)} collective-permute-done((f32[6,8,8,384]{3,2,1,0:T(8,128)S(1)}, f32[6,8,8,384]{3,2,1,0:T(8,128)S(1)}, u32[]{:S(2)}, u32[]{:S(2)}) %collective-permute-start.24) | collective-permute-done | bytes 589856 | tf_op jit(solution)/shard_map/ppermute | solution.py:332
  63.1 2.7 %collective-permute-start.25 = (f32[6,8,8,384]{3,2,1,0:T(8,128)S(1)}, f32[6,8,8,384]{3,2,1,0:T(8,128)S(1)}, u32[]{:S(2)}, u32[]{:S(2)}) collective-permute-start(f32[6,8,8,384]{3,2,1,0:T(8,128)S(1)} %collective-permute-done.24.rest_2_), channel_id=1, source_target_pairs={{0,1},{1,0},{2,3},{3,2},{4,5},{5,4},{6,7},{7,6},{8,9},{9,8},{10,11... | collective-permute-start | bytes 1769480 | tf_op jit(solution)/shard_map/ppermute | solution.py:332
  65.8 12.2 %collective-permute-done.26.rest_4_ = f32[6,8,8,384]{3,2,1,0:T(8,128)S(1)} collective-permute-done((f32[6,8,8,384]{3,2,1,0:T(8,128)S(1)}, f32[6,8,8,384]{3,2,1,0:T(8,128)S(1)}, u32[]{:S(2)}, u32[]{:S(2)}) %collective-permute-start.26) | collective-permute-done | bytes 589856 | tf_op jit(solution)/shard_map/ppermute | solution.py:332
  78.0 1.6 collective-permute-start.27
  80.1 2.1 %collective-permute-start.29 = (f32[6,8,8,384]{3,2,1,0:T(8,128)S(1)}, f32[6,8,8,384]{3,2,1,0:T(8,128)S(1)}, u32[]{:S(2)}, u32[]{:S(2)}) collective-permute-start(f32[6,8,8,384]{3,2,1,0:T(8,128)S(1)} %collective-permute-done.28.rest_6_), channel_id=1, source_target_pairs={{0,1},{1,0},{2,3},{3,2},{4,5},{5,4},{6,7},{7,6},{8,9},{9,8},{10,11... | collective-permute-start | bytes 1769480 | tf_op jit(solution)/shard_map/ppermute | solution.py:332
  82.4 3.6 %collective-permute-done.13.refs_6_ = f32[8,512]{1,0:T(8,128)S(1)} collective-permute-done((f32[8,512]{1,0:T(8,128)S(1)}, f32[8,512]{1,0:T(8,128)S(1)}, u32[]{:S(2)}, u32[]{:S(2)}) %collective-permute-start.13) | collective-permute-done | bytes 16416 | tf_op jit(solution)/shard_map/ppermute | solution.py:332
  86.0 4.1 %collective-permute-done.11.refs_4_ = f32[8,512]{1,0:T(8,128)S(1)} collective-permute-done((f32[8,512]{1,0:T(8,128)S(1)}, f32[8,512]{1,0:T(8,128)S(1)}, u32[]{:S(2)}, u32[]{:S(2)}) %collective-permute-start.11) | collective-permute-done | bytes 16416 | tf_op jit(solution)/shard_map/ppermute | solution.py:332
  90.1 2.6 %collective-permute-done.9.refs_2_ = f32[8,512]{1,0:T(8,128)S(1)} collective-permute-done((f32[8,512]{1,0:T(8,128)S(1)}, f32[8,512]{1,0:T(8,128)S(1)}, u32[]{:S(2)}, u32[]{:S(2)}) %collective-permute-start.9) | collective-permute-done | bytes 16416 | tf_op jit(solution)/shard_map/ppermute | solution.py:332
  92.6 3.5 %collective-permute-start.8 = (f32[8,512]{1,0:T(8,128)S(1)}, f32[8,512]{1,0:T(8,128)S(1)}, u32[]{:S(2)}, u32[]{:S(2)}) collective-permute-start(f32[8,512]{1,0:T(8,128)S(1)} %get-tuple-element.60.refs_0_), channel_id=1, source_target_pairs={{0,1},{1,0},{2,3},{3,2},{4,5},{5,4},{6,7},{7,6},{8,9},{9,8},{10,11... | collective-permute-start | bytes 49160 | tf_op jit(solution)/shard_map/ppermute | solution.py:332
  100.9 8.3 %collective-permute-start.18 = (f32[64,128]{1,0:T(8,128)S(1)}, f32[64,128]{1,0:T(8,128)S(1)}, u32[]{:S(2)}, u32[]{:S(2)}) collective-permute-start(f32[64,128]{1,0:T(8,128)S(1)} %shard_map.62), channel_id=1, source_target_pairs={{0,0},{1,33},{2,2},{3,35},{4,4},{5,37},{6,6},{7,39},{8,8},{9,41},{... | collective-permute-start | bytes 98312 | tf_op jit(solution)/shard_map/ppermute | solution.py:382
  109.2 1.3 collective-permute-done.18.d
  110.5 4.0 %collective-permute-start.17 = (f32[64,128]{1,0:T(8,128)S(1)}, f32[64,128]{1,0:T(8,128)S(1)}, u32[]{:S(2)}, u32[]{:S(2)}) collective-permute-start(f32[64,128]{1,0:T(8,128)S(1)} %shard_map.62), channel_id=1, source_target_pairs={{0,24},{1,41},{2,26},{3,43},{4,28},{5,45},{6,30},{7,47},{8,32},{9,... | collective-permute-start | bytes 98312 | tf_op jit(solution)/shard_map/ppermute | solution.py:382
  114.5 3.8 %collective-permute-done.17.c = f32[64,128]{1,0:T(8,128)S(1)} collective-permute-done((f32[64,128]{1,0:T(8,128)S(1)}, f32[64,128]{1,0:T(8,128)S(1)}, u32[]{:S(2)}, u32[]{:S(2)}) %collective-permute-start.17) | collective-permute-done | bytes 32800 | tf_op jit(solution)/shard_map/ppermute | solution.py:382
  118.2 2.5 %collective-permute-start.16 = (f32[64,128]{1,0:T(8,128)S(1)}, f32[64,128]{1,0:T(8,128)S(1)}, u32[]{:S(2)}, u32[]{:S(2)}) collective-permute-start(f32[64,128]{1,0:T(8,128)S(1)} %shard_map.62), channel_id=1, source_target_pairs={{0,16},{1,49},{2,18},{3,51},{4,20},{5,53},{6,22},{7,55},{8,24},{9,... | collective-permute-start | bytes 98312 | tf_op jit(solution)/shard_map/ppermute | solution.py:382
  120.7 1.4 collective-permute-done.16.b
  122.2 5.2 %collective-permute-start.15 = (f32[64,128]{1,0:T(8,128)S(1)}, f32[64,128]{1,0:T(8,128)S(1)}, u32[]{:S(2)}, u32[]{:S(2)}) collective-permute-start(f32[64,128]{1,0:T(8,128)S(1)} %shard_map.62), channel_id=1, source_target_pairs={{0,8},{1,57},{2,10},{3,59},{4,12},{5,61},{6,14},{7,63},{8,16},{9,1... | collective-permute-start | bytes 98312 | tf_op jit(solution)/shard_map/ppermute | solution.py:382
  128.7 2.6 %collective-permute-done.21.d = f32[64,128]{1,0:T(8,128)S(1)} collective-permute-done((f32[64,128]{1,0:T(8,128)S(1)}, f32[64,128]{1,0:T(8,128)S(1)}, u32[]{:S(2)}, u32[]{:S(2)}) %collective-permute-start.21) | collective-permute-done | bytes 32800 | tf_op jit(solution)/shard_map/ppermute | solution.py:382
  131.3 3.2 %collective-permute-start.20 = (f32[64,128]{1,0:T(8,128)S(1)}, f32[64,128]{1,0:T(8,128)S(1)}, u32[]{:S(2)}, u32[]{:S(2)}) collective-permute-start(f32[64,128]{1,0:T(8,128)S(1)} %shard_map.63.a), channel_id=1, source_target_pairs={{0,128},{1,129},{2,130},{3,131},{4,132},{5,133},{6,134},{7,135},{8... | collective-permute-start | bytes 98312 | tf_op jit(solution)/shard_map/ppermute | solution.py:382
  134.5 1.3 collective-permute-done.20.c
  136.8 3.0 %collective-permute-done.19.b = f32[64,128]{1,0:T(8,128)S(1)} collective-permute-done((f32[64,128]{1,0:T(8,128)S(1)}, f32[64,128]{1,0:T(8,128)S(1)}, u32[]{:S(2)}, u32[]{:S(2)}) %collective-permute-start.19) | collective-permute-done | bytes 32800 | tf_op jit(solution)/shard_map/ppermute | solution.py:382
  140.1 1.2 collective-permute-done.22.other
  141.3 1.9 %shard_map.65.left = f32[64,192]{1,0:T(8,128)S(1)} custom-call(f32[64,128]{1,0:T(8,128)S(1)} %shard_map.64.own, f32[64,128]{1,0:T(8,128)S(1)} %collective-permute-done.22.other), custom_call_target="tpu_custom_call" | custom-call | bytes 131072 | tf_op jit(solution)/shard_map/pallas_call | solution.py:390
  144.7 3.0 %collective-permute-start.30 = (f32[2,6,4,8,384]{4,3,2,1,0:T(8,128)S(1)}, f32[2,6,4,8,384]{4,3,2,1,0:T(8,128)S(1)}, u32[]{:S(2)}, u32[]{:S(2)}) collective-permute-start(f32[2,6,4,8,384]{4,3,2,1,0:T(8,128)S(1)} %get-tuple-element.65), channel_id=1, source_target_pairs={{0,4},{1,5},{2,6},{3,7},{4,0},{5,1},{6,2},{7,3},{8,12},{9,13},{10,... | collective-permute-start | bytes 1769480 | tf_op jit(solution)/shard_map/ppermute | solution.py:332
  148.7 10.5 %collective-permute-done.34.same = f32[2,6,4,8,384]{4,3,2,1,0:T(8,128)S(1)} collective-permute-done((f32[2,6,4,8,384]{4,3,2,1,0:T(8,128)S(1)}, f32[2,6,4,8,384]{4,3,2,1,0:T(8,128)S(1)}, u32[]{:S(2)}, u32[]{:S(2)}) %collective-permute-start.34) | collective-permute-done | bytes 589856 | tf_op jit(solution)/shard_map/ppermute | solution.py:332
  159.1 1.6 collective-permute-start.35
  160.8 12.3 %collective-permute-done.32.same = f32[2,6,4,8,384]{4,3,2,1,0:T(8,128)S(1)} collective-permute-done((f32[2,6,4,8,384]{4,3,2,1,0:T(8,128)S(1)}, f32[2,6,4,8,384]{4,3,2,1,0:T(8,128)S(1)}, u32[]{:S(2)}, u32[]{:S(2)}) %collective-permute-start.32) | collective-permute-done | bytes 589856 | tf_op jit(solution)/shard_map/ppermute | solution.py:332
  (52 shorter events, 15.9 us)
Async XLA Ops:
  0.0 1.2 copy-start
  2.4 15.3 %collective-permute-start.1 = (f32[44,8,384]{2,1,0:T(8,128)S(1)}, f32[44,8,384]{2,1,0:T(8,128)S(1)}, u32[]{:S(2)}, u32[]{:S(2)}) collective-permute-start(f32[44,8,384]{2,1,0:T(8,128)S(1)} %get-tuple-element.38.e4), channel_id=1, source_target_pairs={{0,8},{8,16},{16,24},{24,32},{32,40},{40,48},{48,56},{56,64},{64,7... | collective-permute-start | bytes 1622024 | tf_op jit(solution)/shard_map/ppermute | solution.py:329
  6.8 15.1 %collective-permute-start.4 = (f32[44,8,384]{2,1,0:T(8,128)S(1)}, f32[44,8,384]{2,1,0:T(8,128)S(1)}, u32[]{:S(2)}, u32[]{:S(2)}) collective-permute-start(f32[44,8,384]{2,1,0:T(8,128)S(1)} %get-tuple-element.40.e1), channel_id=1, source_target_pairs={{8,0},{16,8},{24,16},{32,24},{40,32},{48,40},{56,48},{64,56},{72,6... | collective-permute-start | bytes 1622024 | tf_op jit(solution)/shard_map/ppermute | solution.py:329
  9.4 21.1 %collective-permute-start.2 = (f32[32,8,384]{2,1,0:T(8,128)S(1)}, f32[32,8,384]{2,1,0:T(8,128)S(1)}, u32[]{:S(2)}, u32[]{:S(2)}) collective-permute-start(f32[32,8,384]{2,1,0:T(8,128)S(1)} %get-tuple-element.39.e5), channel_id=1, source_target_pairs={{0,8},{8,16},{16,24},{24,32},{32,40},{40,48},{48,56},{56,64},{64,7... | collective-permute-start | bytes 1179656 | tf_op jit(solution)/shard_map/ppermute | solution.py:329
  17.7 22.2 %collective-permute-start.3 = (f32[44,8,384]{2,1,0:T(8,128)S(1)}, f32[44,8,384]{2,1,0:T(8,128)S(1)}, u32[]{:S(2)}, u32[]{:S(2)}) collective-permute-start(f32[44,8,384]{2,1,0:T(8,128)S(1)} %collective-permute-done.1.lo2.refs_1_), channel_id=1, source_target_pairs={{0,1},{1,0},{2,3},{3,2},{4,5},{5,4},{6,7},{7,6},{8,9},{9,8},{10,11... | collective-permute-start | bytes 1622024 | tf_op jit(solution)/shard_map/ppermute | solution.py:332
  21.9 18.1 %collective-permute-start.5 = (f32[44,8,384]{2,1,0:T(8,128)S(1)}, f32[44,8,384]{2,1,0:T(8,128)S(1)}, u32[]{:S(2)}, u32[]{:S(2)}) collective-permute-start(f32[44,8,384]{2,1,0:T(8,128)S(1)} %collective-permute-done.4.hi2.refs_8_), channel_id=1, source_target_pairs={{0,1},{1,0},{2,3},{3,2},{4,5},{5,4},{6,7},{7,6},{8,9},{9,8},{10,11... | collective-permute-start | bytes 1622024 | tf_op jit(solution)/shard_map/ppermute | solution.py:332
  23.6 8.2 %copy-start.1 = (f32[3,32,6,384]{3,1,2,0:T(8,128)S(1)}, f32[3,32,6,384]{3,1,2,0:T(8,128)}, u32[]{:S(2)}) copy-start(f32[3,32,6,384]{3,1,2,0:T(8,128)} %param.6) | copy-start | bytes 2654212
  23.6 13.0 %collective-permute-start.6 = (f32[32,8,384]{2,1,0:T(8,128)S(1)}, f32[32,8,384]{2,1,0:T(8,128)S(1)}, u32[]{:S(2)}, u32[]{:S(2)}) collective-permute-start(f32[32,8,384]{2,1,0:T(8,128)S(1)} %get-tuple-element.41.e0), channel_id=1, source_target_pairs={{8,0},{16,8},{24,16},{32,24},{40,32},{48,40},{56,48},{64,56},{72,6... | collective-permute-start | bytes 1179656 | tf_op jit(solution)/shard_map/ppermute | solution.py:329
  26.3 16.0 %collective-permute-start = (f32[32,8,384]{2,1,0:T(8,128)S(1)}, f32[32,8,384]{2,1,0:T(8,128)S(1)}, u32[]{:S(2)}, u32[]{:S(2)}) collective-permute-start(f32[32,8,384]{2,1,0:T(8,128)S(1)} %get-tuple-element.37.e3), channel_id=1, source_target_pairs={{0,8},{8,16},{16,24},{24,32},{32,40},{40,48},{48,56},{56,64},{64,7... | collective-permute-start | bytes 1179656 | tf_op jit(solution)/shard_map/ppermute | solution.py:329
  30.5 14.6 %collective-permute-start.7 = (f32[32,8,384]{2,1,0:T(8,128)S(1)}, f32[32,8,384]{2,1,0:T(8,128)S(1)}, u32[]{:S(2)}, u32[]{:S(2)}) collective-permute-start(f32[32,8,384]{2,1,0:T(8,128)S(1)} %get-tuple-element.42.e2), channel_id=1, source_target_pairs={{8,0},{16,8},{24,16},{32,24},{40,32},{48,40},{56,48},{64,56},{72,6... | collective-permute-start | bytes 1179656 | tf_op jit(solution)/shard_map/ppermute | solution.py:329
  40.0 5.1 %copy-start.4 = (s32[16]{0:T(128)S(1)}, s32[16]{0:T(128)}, u32[]{:S(2)}) copy-start(s32[16]{0:T(128)} %obs_column.1) | copy-start | bytes 196
  45.0 55.4 %copy-start.2 = (f32[32,16]{0,1:T(8,128)S(1)}, f32[32,16]{0,1:T(8,128)}, u32[]{:S(2)}) copy-start(f32[32,16]{0,1:T(8,128)} %param.8) | copy-start | bytes 6148
  45.1 55.4 %copy-start.3 = (f32[32,16]{0,1:T(8,128)S(1)}, f32[32,16]{0,1:T(8,128)}, u32[]{:S(2)}) copy-start(f32[32,16]{0,1:T(8,128)} %param.9) | copy-start | bytes 6148
  48.8 14.3 %collective-permute-start.24 = (f32[6,8,8,384]{3,2,1,0:T(8,128)S(1)}, f32[6,8,8,384]{3,2,1,0:T(8,128)S(1)}, u32[]{:S(2)}, u32[]{:S(2)}) collective-permute-start(f32[6,8,8,384]{3,2,1,0:T(8,128)S(1)} %get-tuple-element.62), channel_id=1, source_target_pairs={{0,2},{1,3},{2,0},{3,1},{4,6},{5,7},{6,4},{7,5},{8,10},{9,11},{10,... | collective-permute-start | bytes 1769480 | tf_op jit(solution)/shard_map/ppermute | solution.py:332
  50.1 27.9 %collective-permute-start.26 = (f32[6,8,8,384]{3,2,1,0:T(8,128)S(1)}, f32[6,8,8,384]{3,2,1,0:T(8,128)S(1)}, u32[]{:S(2)}, u32[]{:S(2)}) collective-permute-start(f32[6,8,8,384]{3,2,1,0:T(8,128)S(1)} %get-tuple-element.63), channel_id=1, source_target_pairs={{0,4},{1,5},{2,6},{3,7},{4,0},{5,1},{6,2},{7,3},{8,12},{9,13},{10,... | collective-permute-start | bytes 1769480 | tf_op jit(solution)/shard_map/ppermute | solution.py:332
  52.6 27.5 %collective-permute-start.28 = (f32[6,8,8,384]{3,2,1,0:T(8,128)S(1)}, f32[6,8,8,384]{3,2,1,0:T(8,128)S(1)}, u32[]{:S(2)}, u32[]{:S(2)}) collective-permute-start(f32[6,8,8,384]{3,2,1,0:T(8,128)S(1)} %get-tuple-element.64), channel_id=1, source_target_pairs={{0,6},{1,7},{2,4},{3,5},{4,2},{5,3},{6,0},{7,1},{8,14},{9,15},{10,... | collective-permute-start | bytes 1769480 | tf_op jit(solution)/shard_map/ppermute | solution.py:332
  52.8 90.5 %collective-permute-start.23 = (f32[6,8,8,384]{3,2,1,0:T(8,128)S(1)}, f32[6,8,8,384]{3,2,1,0:T(8,128)S(1)}, u32[]{:S(2)}, u32[]{:S(2)}) collective-permute-start(f32[6,8,8,384]{3,2,1,0:T(8,128)S(1)} %get-tuple-element.61.rest_0_), channel_id=1, source_target_pairs={{0,1},{1,0},{2,3},{3,2},{4,5},{5,4},{6,7},{7,6},{8,9},{9,8},{10,11... | collective-permute-start | bytes 1769480 | tf_op jit(solution)/shard_map/ppermute | solution.py:332
  63.1 80.2 %collective-permute-start.25 = (f32[6,8,8,384]{3,2,1,0:T(8,128)S(1)}, f32[6,8,8,384]{3,2,1,0:T(8,128)S(1)}, u32[]{:S(2)}, u32[]{:S(2)}) collective-permute-start(f32[6,8,8,384]{3,2,1,0:T(8,128)S(1)} %collective-permute-done.24.rest_2_), channel_id=1, source_target_pairs={{0,1},{1,0},{2,3},{3,2},{4,5},{5,4},{6,7},{7,6},{8,9},{9,8},{10,11... | collective-permute-start | bytes 1769480 | tf_op jit(solution)/shard_map/ppermute | solution.py:332
  78.0 65.3 %collective-permute-start.27 = (f32[6,8,8,384]{3,2,1,0:T(8,128)S(1)}, f32[6,8,8,384]{3,2,1,0:T(8,128)S(1)}, u32[]{:S(2)}, u32[]{:S(2)}) collective-permute-start(f32[6,8,8,384]{3,2,1,0:T(8,128)S(1)} %collective-permute-done.26.rest_4_), channel_id=1, source_target_pairs={{0,1},{1,0},{2,3},{3,2},{4,5},{5,4},{6,7},{7,6},{8,9},{9,8},{10,11... | collective-permute-start | bytes 1769480 | tf_op jit(solution)/shard_map/ppermute | solution.py:332
  80.1 63.2 %collective-permute-start.29 = (f32[6,8,8,384]{3,2,1,0:T(8,128)S(1)}, f32[6,8,8,384]{3,2,1,0:T(8,128)S(1)}, u32[]{:S(2)}, u32[]{:S(2)}) collective-permute-start(f32[6,8,8,384]{3,2,1,0:T(8,128)S(1)} %collective-permute-done.28.rest_6_), channel_id=1, source_target_pairs={{0,1},{1,0},{2,3},{3,2},{4,5},{5,4},{6,7},{7,6},{8,9},{9,8},{10,11... | collective-permute-start | bytes 1769480 | tf_op jit(solution)/shard_map/ppermute | solution.py:332
  82.2 3.8 %collective-permute-start.13 = (f32[8,512]{1,0:T(8,128)S(1)}, f32[8,512]{1,0:T(8,128)S(1)}, u32[]{:S(2)}, u32[]{:S(2)}) collective-permute-start(f32[8,512]{1,0:T(8,128)S(1)} %get-tuple-element.60.refs_0_), channel_id=1, source_target_pairs={{0,6},{1,7},{2,4},{3,5},{4,2},{5,3},{6,0},{7,1},{8,14},{9,15},{10,... | collective-permute-start | bytes 49160 | tf_op jit(solution)/shard_map/ppermute | solution.py:332
  86.0 4.1 %collective-permute-start.11 = (f32[8,512]{1,0:T(8,128)S(1)}, f32[8,512]{1,0:T(8,128)S(1)}, u32[]{:S(2)}, u32[]{:S(2)}) collective-permute-start(f32[8,512]{1,0:T(8,128)S(1)} %get-tuple-element.60.refs_0_), channel_id=1, source_target_pairs={{0,4},{1,5},{2,6},{3,7},{4,0},{5,1},{6,2},{7,3},{8,12},{9,13},{10,... | collective-permute-start | bytes 49160 | tf_op jit(solution)/shard_map/ppermute | solution.py:332
  90.1 2.6 %collective-permute-start.9 = (f32[8,512]{1,0:T(8,128)S(1)}, f32[8,512]{1,0:T(8,128)S(1)}, u32[]{:S(2)}, u32[]{:S(2)}) collective-permute-start(f32[8,512]{1,0:T(8,128)S(1)} %get-tuple-element.60.refs_0_), channel_id=1, source_target_pairs={{0,2},{1,3},{2,0},{3,1},{4,6},{5,7},{6,4},{7,5},{8,10},{9,11},{10,... | collective-permute-start | bytes 49160 | tf_op jit(solution)/shard_map/ppermute | solution.py:332
  92.6 4.3 %collective-permute-start.8 = (f32[8,512]{1,0:T(8,128)S(1)}, f32[8,512]{1,0:T(8,128)S(1)}, u32[]{:S(2)}, u32[]{:S(2)}) collective-permute-start(f32[8,512]{1,0:T(8,128)S(1)} %get-tuple-element.60.refs_0_), channel_id=1, source_target_pairs={{0,1},{1,0},{2,3},{3,2},{4,5},{5,4},{6,7},{7,6},{8,9},{9,8},{10,11... | collective-permute-start | bytes 49160 | tf_op jit(solution)/shard_map/ppermute | solution.py:332
  96.9 1.2 collective-permute-start.14
  98.1 1.2 collective-permute-start.12
  99.3 1.2 collective-permute-start.10
  100.9 9.6 %collective-permute-start.18 = (f32[64,128]{1,0:T(8,128)S(1)}, f32[64,128]{1,0:T(8,128)S(1)}, u32[]{:S(2)}, u32[]{:S(2)}) collective-permute-start(f32[64,128]{1,0:T(8,128)S(1)} %shard_map.62), channel_id=1, source_target_pairs={{0,0},{1,33},{2,2},{3,35},{4,4},{5,37},{6,6},{7,39},{8,8},{9,41},{... | collective-permute-start | bytes 98312 | tf_op jit(solution)/shard_map/ppermute | solution.py:382
  110.5 7.7 %collective-permute-start.17 = (f32[64,128]{1,0:T(8,128)S(1)}, f32[64,128]{1,0:T(8,128)S(1)}, u32[]{:S(2)}, u32[]{:S(2)}) collective-permute-start(f32[64,128]{1,0:T(8,128)S(1)} %shard_map.62), channel_id=1, source_target_pairs={{0,24},{1,41},{2,26},{3,43},{4,28},{5,45},{6,30},{7,47},{8,32},{9,... | collective-permute-start | bytes 98312 | tf_op jit(solution)/shard_map/ppermute | solution.py:382
  118.2 4.0 %collective-permute-start.16 = (f32[64,128]{1,0:T(8,128)S(1)}, f32[64,128]{1,0:T(8,128)S(1)}, u32[]{:S(2)}, u32[]{:S(2)}) collective-permute-start(f32[64,128]{1,0:T(8,128)S(1)} %shard_map.62), channel_id=1, source_target_pairs={{0,16},{1,49},{2,18},{3,51},{4,20},{5,53},{6,22},{7,55},{8,24},{9,... | collective-permute-start | bytes 98312 | tf_op jit(solution)/shard_map/ppermute | solution.py:382
  122.2 6.2 %collective-permute-start.15 = (f32[64,128]{1,0:T(8,128)S(1)}, f32[64,128]{1,0:T(8,128)S(1)}, u32[]{:S(2)}, u32[]{:S(2)}) collective-permute-start(f32[64,128]{1,0:T(8,128)S(1)} %shard_map.62), channel_id=1, source_target_pairs={{0,8},{1,57},{2,10},{3,59},{4,12},{5,61},{6,14},{7,63},{8,16},{9,1... | collective-permute-start | bytes 98312 | tf_op jit(solution)/shard_map/ppermute | solution.py:382
  128.4 2.8 %collective-permute-start.21 = (f32[64,128]{1,0:T(8,128)S(1)}, f32[64,128]{1,0:T(8,128)S(1)}, u32[]{:S(2)}, u32[]{:S(2)}) collective-permute-start(f32[64,128]{1,0:T(8,128)S(1)} %shard_map.63.a), channel_id=1, source_target_pairs={{0,192},{1,193},{2,194},{3,195},{4,196},{5,197},{6,198},{7,199},{8... | collective-permute-start | bytes 98312 | tf_op jit(solution)/shard_map/ppermute | solution.py:382
  131.3 4.5 %collective-permute-start.20 = (f32[64,128]{1,0:T(8,128)S(1)}, f32[64,128]{1,0:T(8,128)S(1)}, u32[]{:S(2)}, u32[]{:S(2)}) collective-permute-start(f32[64,128]{1,0:T(8,128)S(1)} %shard_map.63.a), channel_id=1, source_target_pairs={{0,128},{1,129},{2,130},{3,131},{4,132},{5,133},{6,134},{7,135},{8... | collective-permute-start | bytes 98312 | tf_op jit(solution)/shard_map/ppermute | solution.py:382
  135.8 4.0 %collective-permute-start.19 = (f32[64,128]{1,0:T(8,128)S(1)}, f32[64,128]{1,0:T(8,128)S(1)}, u32[]{:S(2)}, u32[]{:S(2)}) collective-permute-start(f32[64,128]{1,0:T(8,128)S(1)} %shard_map.63.a), channel_id=1, source_target_pairs={{0,64},{1,65},{2,66},{3,67},{4,68},{5,69},{6,70},{7,71},{8,72},{9,... | collective-permute-start | bytes 98312 | tf_op jit(solution)/shard_map/ppermute | solution.py:382
  139.8 1.5 collective-permute-start.22
  144.3 14.8 %collective-permute-start.34 = (f32[2,6,4,8,384]{4,3,2,1,0:T(8,128)S(1)}, f32[2,6,4,8,384]{4,3,2,1,0:T(8,128)S(1)}, u32[]{:S(2)}, u32[]{:S(2)}) collective-permute-start(f32[2,6,4,8,384]{4,3,2,1,0:T(8,128)S(1)} %get-tuple-element.67), channel_id=1, source_target_pairs={{0,2},{1,3},{2,0},{3,1},{4,6},{5,7},{6,4},{7,5},{8,10},{9,11},{10,... | collective-permute-start | bytes 1769480 | tf_op jit(solution)/shard_map/ppermute | solution.py:332
  144.4 28.7 %collective-permute-start.32 = (f32[2,6,4,8,384]{4,3,2,1,0:T(8,128)S(1)}, f32[2,6,4,8,384]{4,3,2,1,0:T(8,128)S(1)}, u32[]{:S(2)}, u32[]{:S(2)}) collective-permute-start(f32[2,6,4,8,384]{4,3,2,1,0:T(8,128)S(1)} %get-tuple-element.66), channel_id=1, source_target_pairs={{0,6},{1,7},{2,4},{3,5},{4,2},{5,3},{6,0},{7,1},{8,14},{9,15},{10,... | collective-permute-start | bytes 1769480 | tf_op jit(solution)/shard_map/ppermute | solution.py:332
  144.7 29.4 %collective-permute-start.30 = (f32[2,6,4,8,384]{4,3,2,1,0:T(8,128)S(1)}, f32[2,6,4,8,384]{4,3,2,1,0:T(8,128)S(1)}, u32[]{:S(2)}, u32[]{:S(2)}) collective-permute-start(f32[2,6,4,8,384]{4,3,2,1,0:T(8,128)S(1)} %get-tuple-element.65), channel_id=1, source_target_pairs={{0,4},{1,5},{2,6},{3,7},{4,0},{5,1},{6,2},{7,3},{8,12},{9,13},{10,... | collective-permute-start | bytes 1769480 | tf_op jit(solution)/shard_map/ppermute | solution.py:332
  147.7 26.5 %collective-permute-start.36 = (f32[2,6,4,8,384]{4,3,2,1,0:T(8,128)S(1)}, f32[2,6,4,8,384]{4,3,2,1,0:T(8,128)S(1)}, u32[]{:S(2)}, u32[]{:S(2)}) collective-permute-start(f32[2,6,4,8,384]{4,3,2,1,0:T(8,128)S(1)} %get-tuple-element.68.same), channel_id=1, source_target_pairs={{0,1},{1,0},{2,3},{3,2},{4,5},{5,4},{6,7},{7,6},{8,9},{9,8},{10,11... | collective-permute-start | bytes 1769480 | tf_op jit(solution)/shard_map/ppermute | solution.py:332
  159.1 16.0 %collective-permute-start.35 = (f32[2,6,4,8,384]{4,3,2,1,0:T(8,128)S(1)}, f32[2,6,4,8,384]{4,3,2,1,0:T(8,128)S(1)}, u32[]{:S(2)}, u32[]{:S(2)}) collective-permute-start(f32[2,6,4,8,384]{4,3,2,1,0:T(8,128)S(1)} %collective-permute-done.34.same), channel_id=1, source_target_pairs={{0,1},{1,0},{2,3},{3,2},{4,5},{5,4},{6,7},{7,6},{8,9},{9,8},{10,11... | collective-permute-start | bytes 1769480 | tf_op jit(solution)/shard_map/ppermute | solution.py:332
  173.1 3.0 %collective-permute-start.33 = (f32[2,6,4,8,384]{4,3,2,1,0:T(8,128)S(1)}, f32[2,6,4,8,384]{4,3,2,1,0:T(8,128)S(1)}, u32[]{:S(2)}, u32[]{:S(2)}) collective-permute-start(f32[2,6,4,8,384]{4,3,2,1,0:T(8,128)S(1)} %collective-permute-done.32.same), channel_id=1, source_target_pairs={{0,1},{1,0},{2,3},{3,2},{4,5},{5,4},{6,7},{7,6},{8,9},{9,8},{10,11... | collective-permute-start | bytes 1769480 | tf_op jit(solution)/shard_map/ppermute | solution.py:332
  174.1 3.0 %collective-permute-start.31 = (f32[2,6,4,8,384]{4,3,2,1,0:T(8,128)S(1)}, f32[2,6,4,8,384]{4,3,2,1,0:T(8,128)S(1)}, u32[]{:S(2)}, u32[]{:S(2)}) collective-permute-start(f32[2,6,4,8,384]{4,3,2,1,0:T(8,128)S(1)} %collective-permute-done.30.same), channel_id=1, source_target_pairs={{0,1},{1,0},{2,3},{3,2},{4,5},{5,4},{6,7},{7,6},{8,9},{9,8},{10,11... | collective-permute-start | bytes 1769480 | tf_op jit(solution)/shard_map/ppermute | solution.py:332

commit v3 on v2

--- a/solution.py
+++ b/solution.py
@@ -16,6 +16,7 @@
 SM = pl.BlockSpec(memory_space=pltpu.SMEM)
 PARAMS = pltpu.CompilerParams(vmem_limit_bytes=16 * 2**20)
 ROUTE = (1, 3, 2)
+OUTER = (0, 1, 4, 5)
 
 
 def call(body, outs, n_in, scratch=(), smem=0, flops=0, nbytes=0):
@@ -56,6 +57,15 @@
         for d in range(3):
             for tile in range(levels // 8):
                 dst[levels + d * (levels // 8) + tile] = courant[d, row, pl.ds(8 * tile, 8), :]
+
+
+def pick_body(one, three, out):
+    core = lax.rem(lax.axis_index("mem"), 2)
+    for value, ref in ((0, one), (1, three)):
+
+        @pl.when(core == value)
+        def _():
+            out[...] = ref[...]
 
 
 def sum4_body(a, b, c, d, out):
@@ -128,7 +138,7 @@
     lax.fori_loop(0, levels, level_step, (first, first), unroll=32)
 
 
-def stage_a(lo1, e0, e1, e2, e3, e4, e5, hi1, coef, f0, f1, f4, f5, g1, g2, g3, g4, h2, h3, f2, f3):
+def stage_a(lo1, e0, e1, e2, e3, e4, e5, hi1, coef, f0, f1, f4, f5, g1, g2, g3, g4, h23, f2, f3):
     e = [lo1, e0, e1, e2, e3, e4, e5, hi1]
     f = [f0, f1, f2, f3, f4, f5]
     g = [None, g1, g2, g3, g4]
@@ -136,8 +146,8 @@
         advance_row(f[row], e[row], e[row + 1], e[row + 2], coef, row)
     for row in (1, 2, 3, 4):
         advance_row(g[row], f[row - 1], f[row], f[row + 1], coef, row)
-    for row, h in ((2, h2), (3, h3)):
-        advance_row(h, g[row - 1], g[row], g[row + 1], coef, row)
+    for row in (2, 3):
+        advance_row(h23.at[row - 2], g[row - 1], g[row], g[row + 1], coef, row)
 
 
 def stage_b(lo2, lo2x, hi2, hi2x, lo1, e0, hi1, e5, f0, f1, f4, f5, g1, g2, g3, g4, coef, *outs):
@@ -152,13 +162,14 @@
 
 
 def stage_c(obs_column, *refs):
-    lo3, lo2, lo1, fm, f0, g0, g1, hi3, hi2, hi1, fp, f5, g5, g4, h1, h2, h3, h4, coef, side = refs[:20]
-    chunks, prof, one, two, full = refs[20:24], refs[24], refs[25], refs[26], refs[27]
+    lo3, lo2, lo1, fm, f0, g0, g1, hi3, hi2, hi1, fp, f5, g5, g4, h1, h23, h4, coef, side = refs[:19]
+    chunks, prof, one, two, full = refs[19:23], refs[23], refs[24], refs[25], refs[26]
     levels, members, cells = g0.shape
     me = lax.axis_index("mem")
     origin = lax.axis_index("rows") * (6 * cells)
-    for row, h in ((1, h1), (2, h2), (3, h3), (4, h4)):
-        full[row] = h[...]
+    full[1] = h1[...]
+    full[pl.ds(2, 2)] = h23[...]
+    full[4] = h4[...]
     advance_row(one, lo3, lo2, lo1, side, 0)
     advance_row(two, one, fm, f0, side, 1)
     advance_row(full.at[0], two, g0, g1, coef, 0)
@@ -185,8 +196,8 @@
     depth = levels // 4
     for k in range(4):
         chip = lax.bitwise_xor(lax.div(me, 2), k)
-        for row in range(6):
-            chunks[k][row] = full[row, pl.ds(chip * depth, depth)]
+        for i, row in enumerate(OUTER):
+            chunks[k][i] = full[row, pl.ds(chip * depth, depth)]
 
 
 def flat_rows(ref):
@@ -258,6 +269,13 @@
     lhs[...] = jnp.concatenate([high, left - high, high], axis=1)
 
 
+def mixed_levels(lhs, blocks):
+    f = jnp.concatenate(blocks, axis=0)
+    hi = f.astype(BF16)
+    lo = (f - hi.astype(F32)).astype(BF16)
+    return jnp.dot(lhs, jnp.concatenate([hi, hi, lo], axis=0), preferred_element_type=F32)
+
+
 def mix_body(left, *rest):
     chunks, outs = rest[:8], rest[8:]
     lhs = left[...].astype(BF16)
@@ -265,16 +283,32 @@
     start = lax.rem(lax.axis_index("mem"), 2) * depth
     for row in range(rows):
         for z in range(depth):
-            f = jnp.concatenate([c[row, start + z] for c in chunks], axis=0)
-            hi = f.astype(BF16)
-            lo = (f - hi.astype(F32)).astype(BF16)
-            o = jnp.dot(lhs, jnp.concatenate([hi, hi, lo], axis=0), preferred_element_type=F32)
+            o = mixed_levels(lhs, [c[row, start + z] for c in chunks])
             for k in range(8):
                 outs[k // 2][k % 2, row, z] = o[8 * k : 8 * k + 8]
 
 
+def inner_body(left, *rest):
+    fields, (out, stack, block, sem) = rest[:8], rest[-4:]
+    members = stack.shape[1]
+    lhs = left[pl.ds(0, 2 * members), :].astype(BF16)
+    for row in range(2):
+
+        def tile(t, carry):
+            for z in range(8):
+                o = mixed_levels(lhs, [f[row, 8 * t + z] for f in fields])
+                stack[z] = o[:members]
+            block[:, row, pl.ds(pl.multiple_of(8 * t, 8), 8), :] = members_inside(stack[...])
+            return carry
+
+        lax.fori_loop(0, fields[0].shape[1] // 8, tile, 0)
+    copy = pltpu.make_async_copy(block, out.at[:, pl.ds(2, 2)], sem)
+    copy.start()
+    copy.wait()
+
+
 def place_body(distance, same, cross, *rest):
-    out, stack, block, sem = rest[-4:]
+    out, stack, block, sems = rest[-4:]
     me = lax.axis_index("mem")
     core, chip = lax.rem(me, 2), lax.bitwise_xor(lax.div(me, 2), distance)
     rows, depth = same.shape[1], same.shape[2]
@@ -283,9 +317,14 @@
         stack[pl.ds((1 - core) * depth, depth)] = cross[1, row]
         block[:, row] = members_inside(stack[...])
     levels = pl.ds(pl.multiple_of(chip * 8, 8), 8)
-    copy = pltpu.make_async_copy(block, out.at[:, :, levels, :], sem)
-    copy.start()
-    copy.wait()
+    copies = [
+        pltpu.make_async_copy(block.at[:, pl.ds(2 * i, 2)], out.at[:, pl.ds(4 * i, 2), levels, :], sems.at[i])
+        for i in range(2)
+    ]
+    for copy in copies:
+        copy.start()
+    for copy in copies:
+        copy.wait()
 
 
 def per_device(ensemble, courant, obs_column, obs_value, obs_var):
@@ -340,8 +379,8 @@
     lo2x, hi2x = swap(lo2, 1), swap(hi2, 1)
     coef = call(own_coefficients, (rows, 7, levels, cells), 1, nbytes=7 * row_bytes)(flow)
 
-    f0, f1, f4, f5, g1, g2, g3, g4, h2, h3 = call(
-        stage_a, [row_shape] * 10, 9, [pltpu.VMEM(row_shape, F32)] * 2, nbytes=20 * row_bytes,
+    f0, f1, f4, f5, g1, g2, g3, g4, h23 = call(
+        stage_a, [row_shape] * 8 + [(2,) + row_shape], 9, [pltpu.VMEM(row_shape, F32)] * 2, nbytes=20 * row_bytes,
     )(lo1, e0, e1, e2, e3, e4, e5, hi1, coef)
     fm, fp, g0, g5, h1, h4, side = call(
         stage_b, [row_shape] * 6 + [(4, 7, levels, cells)], 17, nbytes=20 * row_bytes,
@@ -349,23 +388,32 @@
     chips = mem // 2
     obs = obs_value.size
     *chunks, prof = call(
-        stage_c, [(rows, levels // chips, members, cells)] * chips + [(members, obs)], 21,
+        stage_c, [(len(OUTER), levels // chips, members, cells)] * chips + [(members, obs)], 20,
         [pltpu.VMEM(row_shape, F32)] * 2 + [pltpu.VMEM((rows,) + row_shape, F32)],
         smem=1, nbytes=30 * row_bytes,
-    )(obs_column, lo3, lo2, lo1, fm, f0, g0, g1, hi3, hi2, hi1, fp, f5, g5, g4, h1, h2, h3, h4, coef, side)
+    )(obs_column, lo3, lo2, lo1, fm, f0, g0, g1, hi3, hi2, hi1, fp, f5, g5, g4, h1, h23, h4, coef, side)
 
     def along_chips(parts):
         got = {0: parts[0]}
         for k in ROUTE:
             got[k] = swap(parts[k], 2 * k)
-        return [(got[k], swap(got[k], 1)) for k in (0,) + ROUTE]
+        return shown(got)
+
+    def shown(got):
+        return {k: (got[k], swap(got[k], 1)) for k in got}
+
+    def in_order(pairs):
+        return [block for k in range(chips) for block in pairs[k]]
 
     far = [swap(prof, 2 * k) for k in (1, 2, 3)]
     profiles = []
     for a in [prof] + far:
         profiles += [a, swap(a, 1)]
-    pairs = dict(zip((0,) + ROUTE, along_chips(chunks)))
-    moved = [block for k in range(chips) for block in pairs[k]]
+    moved = in_order(along_chips(chunks))
+    near = {0: h23, 1: swap(h23, 2), 3: swap(h23, 6)}
+    onward = call(pick_body, h23.shape, 2, nbytes=4 * row_bytes)(near[1], near[3])
+    near[2] = lax.ppermute(onward, "mem", [(i, i ^ (2 if i % 2 else 6)) for i in range(mem)])
+    inner = in_order(shown(near))
     part = call(
         gram_body, (8 * members, 16 * members), 10,
         [pltpu.VMEM((8 * members, obs), F32), pltpu.VMEM((16 * members, obs), F32)], nbytes=1 << 18,
@@ -388,24 +436,40 @@
         total = sum4(total, *[shifted(total, dy, (0, 0)) for dy in range(1, wide)])
     n = 8 * members
     left = call(weights_body, (n, 3 * n), 2, [pltpu.VMEM((n, n), F32)] * 2, nbytes=1 << 17)(total, swap(total, 1))
-    mixed = call(mix_body, [(2, rows, levels // mem, members, cells)] * chips, 9, nbytes=18 * row_bytes)(left, *moved)
-    placed = None
-    shape = (members, rows, levels, cells)
-    for k, (same, cross) in zip((0,) + ROUTE, along_chips(mixed)):
+    mixed = call(
+        mix_body, [(2, len(OUTER), levels // mem, members, cells)] * chips, 9, nbytes=18 * row_bytes,
+    )(left, *moved)
+    result = jax.ShapeDtypeStruct((members, rows, levels, cells), F32)
+    anywhere = pl.BlockSpec(memory_space=pl.ANY)
+    placed = pl.pallas_call(
+        inner_body,
+        out_shape=result,
+        in_specs=[VM] * 9,
+        out_specs=anywhere,
+        scratch_shapes=[
+            pltpu.VMEM((8, members, cells), F32),
+            pltpu.VMEM((members, 2, levels, cells), F32),
+            pltpu.SemaphoreType.DMA,
+        ],
+        compiler_params=PARAMS,
+        interpret=INTERPRET,
+        name="inner",
+    )(left, *inner)
+    for k, (same, cross) in along_chips(mixed).items():
         placed = pl.pallas_call(
             functools.partial(place_body, k),
-            out_shape=jax.ShapeDtypeStruct(shape, F32),
-            in_specs=[VM, VM] + ([] if placed is None else [pl.BlockSpec(memory_space=pl.ANY)]),
-            out_specs=pl.BlockSpec(memory_space=pl.ANY),
+            out_shape=result,
+            in_specs=[VM, VM, anywhere],
+            out_specs=anywhere,
             scratch_shapes=[
                 pltpu.VMEM((8, members, cells), F32),
-                pltpu.VMEM((members, rows, 8, cells), F32),
-                pltpu.SemaphoreType.DMA,
+                pltpu.VMEM((members, len(OUTER), 8, cells), F32),
+                pltpu.SemaphoreType.DMA((2,)),
             ],
-            input_output_aliases={} if placed is None else {2: 0},
+            input_output_aliases={2: 0},
             compiler_params=PARAMS,
             interpret=INTERPRET,
-        )(same, cross, *([] if placed is None else [placed]))
+        )(same, cross, placed)
     return jnp.transpose(placed, (0, 2, 1, 3))
 
 

time: 179 us -> 149 us (0.83)
  waiting for transfers between devices: 86.6 us -> 49.9 us
  starting transfers between devices: 69.5 us -> 75 us
    ppermute x24 -> x30, waiting for transfers between devices: 59.1 us -> 25.4 us  [swap(): return lax.ppermute(a, 'mem', [(i, i ^ k) for i in range(mem)])]
    ppermute x24 -> x30, starting transfers between devices: 28.1 us -> 39.9 us  [swap(): return lax.ppermute(a, 'mem', [(i, i ^ k) for i in range(mem)])]
    ppermute x7, waiting for transfers between devices: 14.3 us -> 2.6 us  [shifted(): return lax.ppermute(a, ('rows', 'mem'), pairs)]
    ppermute x6, waiting for transfers between devices: 13.1 us -> 21.8 us  [exchange(): return (lax.ppermute(last, 'rows', up), lax.ppermute(first, 'rows', down))]
    ppermute x7, starting transfers between devices: 24.6 us -> 17.5 us  [shifted(): return lax.ppermute(a, ('rows', 'mem'), pairs)]
    pallas_call x7 -> x9, Pallas kernels: 12.1 us -> 13.8 us  [the longest x1 3.55 us: per_device(): pl.pallas_call(inner_body, out_shape=result, in_specs=[VM] * 9, out_specs...]
  transfers between devices with their start and end apart: 37 -> 44, of which waited for: 24 -> 16; matrix products, arithmetic and copies ran while one was open for 0% -> 0% of each run, Pallas kernels for 8% -> 13%
where the time goes in v3:
time: 149 us
  starting transfers between devices  75 us (50%)
  waiting for transfers between devices  49.9 us (33%)
  Pallas kernels  22 us (15%)
    ppermute x30, starting transfers between devices, swap(): return lax.ppermute(a, 'mem', [(i, i ^ k) for i in range(mem)])  39.9 us
    ppermute x30, waiting for transfers between devices, swap(): return lax.ppermute(a, 'mem', [(i, i ^ k) for i in range(mem)])  25.4 us
    ppermute x6, waiting for transfers between devices, exchange(): return (lax.ppermute(last, 'rows', up), lax.ppermute(first, 'rows', down))  21.8 us
    ppermute x7, starting transfers between devices, shifted(): return lax.ppermute(a, ('rows', 'mem'), pairs)  17.5 us
    ppermute x6, starting transfers between devices, exchange(): return (lax.ppermute(last, 'rows', up), lax.ppermute(first, 'rows', down))  16.1 us
    pallas_call x3, Pallas kernels, relayout(): pl.pallas_call(rows_courant_body if with_courant else rows_body, grid=(1,...  3.78 us
    pallas_call x1, Pallas kernels, per_device(): pl.pallas_call(inner_body, out_shape=result, in_specs=[VM] * 9, out_specs...  3.55 us
    pallas_call x4, Pallas kernels, per_device(): pl.pallas_call(functools.partial(place_body, k), out_shape=result, in_spe...  3.49 us
  transfers between devices with their start and end apart: 44, of which 16 were waited for; matrix products, arithmetic and copies ran while one was open for 0% of the time, Pallas kernels for 13%

profile of v3, /device:TPU:1, one launch (start us, length us, event | category | flops | bytes accessed | tf_op | source)
XLA Modules:
  0.0 148.5 jit_solution(12459948345537890984)
XLA Ops:
  0.0 1.2 copy-done
  1.2 1.3 shard_map.56
  2.4 4.4 %collective-permute-start.1 = (f32[44,8,384]{2,1,0:T(8,128)S(1)}, f32[44,8,384]{2,1,0:T(8,128)S(1)}, u32[]{:S(2)}, u32[]{:S(2)}) collective-permute-start(f32[44,8,384]{2,1,0:T(8,128)S(1)} %get-tuple-element.37.e4), channel_id=1, source_target_pairs={{0,8},{8,16},{16,24},{24,32},{32,40},{40,48},{48,56},{56,64},{64,7... | collective-permute-start | bytes 1622024 | tf_op jit(solution)/shard_map/ppermute | solution.py:368
  6.8 1.3 collective-permute-start.4
  8.1 1.3 shard_map.57
  9.4 4.2 %collective-permute-start.2 = (f32[32,8,384]{2,1,0:T(8,128)S(1)}, f32[32,8,384]{2,1,0:T(8,128)S(1)}, u32[]{:S(2)}, u32[]{:S(2)}) collective-permute-start(f32[32,8,384]{2,1,0:T(8,128)S(1)} %get-tuple-element.38.e5), channel_id=1, source_target_pairs={{0,8},{8,16},{16,24},{24,32},{32,40},{40,48},{48,56},{56,64},{64,7... | collective-permute-start | bytes 1179656 | tf_op jit(solution)/shard_map/ppermute | solution.py:368
  13.6 1.4 collective-permute-start.6
  15.0 2.7 %collective-permute-done.1.lo2.refs_1_ = f32[44,8,384]{2,1,0:T(8,128)S(1)} collective-permute-done((f32[44,8,384]{2,1,0:T(8,128)S(1)}, f32[44,8,384]{2,1,0:T(8,128)S(1)}, u32[]{:S(2)}, u32[]{:S(2)}) %collective-permute-start.1) | collective-permute-done | bytes 540704 | tf_op jit(solution)/shard_map/ppermute | solution.py:368
  17.7 2.7 %collective-permute-start.3 = (f32[44,8,384]{2,1,0:T(8,128)S(1)}, f32[44,8,384]{2,1,0:T(8,128)S(1)}, u32[]{:S(2)}, u32[]{:S(2)}) collective-permute-start(f32[44,8,384]{2,1,0:T(8,128)S(1)} %collective-permute-done.1.lo2.refs_1_), channel_id=1, source_target_pairs={{0,1},{1,0},{2,3},{3,2},{4,5},{5,4},{6,7},{7,6},{8,9},{9,8},{10,11... | collective-permute-start | bytes 1622024 | tf_op jit(solution)/shard_map/ppermute | solution.py:371
  20.4 1.3 shard_map.55
  21.9 4.3 %collective-permute-done.2.lo1.refs_2_ = f32[32,8,384]{2,1,0:T(8,128)S(1)} collective-permute-done((f32[32,8,384]{2,1,0:T(8,128)S(1)}, f32[32,8,384]{2,1,0:T(8,128)S(1)}, u32[]{:S(2)}, u32[]{:S(2)}) %collective-permute-start.2) | collective-permute-done | bytes 393248 | tf_op jit(solution)/shard_map/ppermute | solution.py:368
  26.2 4.2 %collective-permute-done.6.hi1.refs_9_ = f32[32,8,384]{2,1,0:T(8,128)S(1)} collective-permute-done((f32[32,8,384]{2,1,0:T(8,128)S(1)}, f32[32,8,384]{2,1,0:T(8,128)S(1)}, u32[]{:S(2)}, u32[]{:S(2)}) %collective-permute-start.6) | collective-permute-done | bytes 393248 | tf_op jit(solution)/shard_map/ppermute | solution.py:368
  30.3 2.5 %shard_map.59 = (f32[32,8,384]{2,1,0:T(8,128)S(1)}, f32[32,8,384]{2,1,0:T(8,128)S(1)}, f32[32,8,384]{2,1,0:T(8,128)S(1)}, f32[32,8,384]{2,1,0:T(8,128)S(1)}, f32...) custom-call(f32[32,8,384]{2,1,0:T(8,128)S(1)} %collective-permute-do, ...), custom_call_target="tpu_custom_call" | custom-call | bytes 7864320 | tf_op jit(solution)/shard_map/pallas_call | solution.py:382
  32.9 2.6 %collective-permute-start.40 = (f32[2,32,8,384]{3,2,1,0:T(8,128)S(1)}, f32[2,32,8,384]{3,2,1,0:T(8,128)S(1)}, u32[]{:S(2)}, u32[]{:S(2)}) collective-permute-start(f32[2,32,8,384]{3,2,1,0:T(8,128)S(1)} %get-tuple-element.55.refs_15_.rest_0_), channel_id=1, source_target_pairs={{0,6},{1,7},{2,4},{3,5},{4,2},{5,3},{6,0},{7,1},{8,14},{9,15},{10,... | collective-permute-start | bytes 2359304 | tf_op jit(solution)/shard_map/ppermute | solution.py:371
  35.5 1.9 %collective-permute-start.5 = (f32[44,8,384]{2,1,0:T(8,128)S(1)}, f32[44,8,384]{2,1,0:T(8,128)S(1)}, u32[]{:S(2)}, u32[]{:S(2)}) collective-permute-start(f32[44,8,384]{2,1,0:T(8,128)S(1)} %collective-permute-done.4.hi2.refs_8_), channel_id=1, source_target_pairs={{0,1},{1,0},{2,3},{3,2},{4,5},{5,4},{6,7},{7,6},{8,9},{9,8},{10,11... | collective-permute-start | bytes 1622024 | tf_op jit(solution)/shard_map/ppermute | solution.py:371
  37.4 3.6 %collective-permute-start = (f32[32,8,384]{2,1,0:T(8,128)S(1)}, f32[32,8,384]{2,1,0:T(8,128)S(1)}, u32[]{:S(2)}, u32[]{:S(2)}) collective-permute-start(f32[32,8,384]{2,1,0:T(8,128)S(1)} %get-tuple-element.36.e3), channel_id=1, source_target_pairs={{0,8},{8,16},{16,24},{24,32},{32,40},{40,48},{48,56},{56,64},{64,7... | collective-permute-start | bytes 1179656 | tf_op jit(solution)/shard_map/ppermute | solution.py:368
  41.0 1.3 collective-permute-start.7
  42.4 1.9 %shard_map.60 = (f32[32,8,384]{2,1,0:T(8,128)S(1)}, f32[32,8,384]{2,1,0:T(8,128)S(1)}, f32[32,8,384]{2,1,0:T(8,128)S(1)}, f32[32,8,384]{2,1,0:T(8,128)S(1)}, f32...) custom-call(f32[44,8,384]{2,1,0:T(8,128)S(1)} %collective-permute-done.1.lo2.refs_1_, ...), custom_call_target="tpu_custom_call" | custom-call | bytes 7864320 | tf_op jit(solution)/shard_map/pallas_call | solution.py:385
  44.3 5.1 %collective-permute-done.refs_0_ = f32[32,8,384]{2,1,0:T(8,128)S(1)} collective-permute-done((f32[32,8,384]{2,1,0:T(8,128)S(1)}, f32[32,8,384]{2,1,0:T(8,128)S(1)}, u32[]{:S(2)}, u32[]{:S(2)}) %collective-permute-start) | collective-permute-done | bytes 393248 | tf_op jit(solution)/shard_map/ppermute | solution.py:368
  49.4 5.5 %collective-permute-done.7.refs_7_ = f32[32,8,384]{2,1,0:T(8,128)S(1)} collective-permute-done((f32[32,8,384]{2,1,0:T(8,128)S(1)}, f32[32,8,384]{2,1,0:T(8,128)S(1)}, u32[]{:S(2)}, u32[]{:S(2)}) %collective-permute-start.7) | collective-permute-done | bytes 393248 | tf_op jit(solution)/shard_map/ppermute | solution.py:368
  54.9 3.5 %shard_map.61 = (f32[4,8,8,384]{3,2,1,0:T(8,128)S(1)}, f32[4,8,8,384]{3,2,1,0:T(8,128)S(1)}, f32[4,8,8,384]{3,2,1,0:T(8,128)S(1)}, f32[4,8,8,384]{3,2,1,0:T(8,128)S(1)}, f32[8,512]{1,0:T(8,128)S(1)}) custom-call(s32[16]{0:T(128)S(1)} %copy-done.4, f32[32,8,384]{2,1,0:T(8,128)S(1)} %collective-permute-done.refs_0_, ...), custom_call_target="tpu_custom_call" | custom-call | bytes 11796480 | tf_op jit(solution)/shard_map/pallas_call | solution.py:390
  58.7 1.5 %collective-permute-start.11 = (f32[8,512]{1,0:T(8,128)S(1)}, f32[8,512]{1,0:T(8,128)S(1)}, u32[]{:S(2)}, u32[]{:S(2)}) collective-permute-start(f32[8,512]{1,0:T(8,128)S(1)} %get-tuple-element.58.refs_0_), channel_id=1, source_target_pairs={{0,4},{1,5},{2,6},{3,7},{4,0},{5,1},{6,2},{7,3},{8,12},{9,13},{10,... | collective-permute-start | bytes 49160 | tf_op jit(solution)/shard_map/ppermute | solution.py:371
  60.2 1.5 %collective-permute-start.9 = (f32[8,512]{1,0:T(8,128)S(1)}, f32[8,512]{1,0:T(8,128)S(1)}, u32[]{:S(2)}, u32[]{:S(2)}) collective-permute-start(f32[8,512]{1,0:T(8,128)S(1)} %get-tuple-element.58.refs_0_), channel_id=1, source_target_pairs={{0,2},{1,3},{2,0},{3,1},{4,6},{5,7},{6,4},{7,5},{8,10},{9,11},{10,... | collective-permute-start | bytes 49160 | tf_op jit(solution)/shard_map/ppermute | solution.py:371
  62.3 2.0 %collective-permute-start.8 = (f32[8,512]{1,0:T(8,128)S(1)}, f32[8,512]{1,0:T(8,128)S(1)}, u32[]{:S(2)}, u32[]{:S(2)}) collective-permute-start(f32[8,512]{1,0:T(8,128)S(1)} %get-tuple-element.58.refs_0_), channel_id=1, source_target_pairs={{0,1},{1,0},{2,3},{3,2},{4,5},{5,4},{6,7},{7,6},{8,9},{9,8},{10,11... | collective-permute-start | bytes 49160 | tf_op jit(solution)/shard_map/ppermute | solution.py:371
  66.9 7.5 %collective-permute-start.18 = (f32[64,128]{1,0:T(8,128)S(1)}, f32[64,128]{1,0:T(8,128)S(1)}, u32[]{:S(2)}, u32[]{:S(2)}) collective-permute-start(f32[64,128]{1,0:T(8,128)S(1)} %shard_map.62), channel_id=1, source_target_pairs={{0,0},{1,33},{2,2},{3,35},{4,4},{5,37},{6,6},{7,39},{8,8},{9,41},{... | collective-permute-start | bytes 98312 | tf_op jit(solution)/shard_map/ppermute | solution.py:430
  74.4 1.3 collective-permute-start.17
  75.8 3.5 %collective-permute-start.16 = (f32[64,128]{1,0:T(8,128)S(1)}, f32[64,128]{1,0:T(8,128)S(1)}, u32[]{:S(2)}, u32[]{:S(2)}) collective-permute-start(f32[64,128]{1,0:T(8,128)S(1)} %shard_map.62), channel_id=1, source_target_pairs={{0,16},{1,49},{2,18},{3,51},{4,20},{5,53},{6,22},{7,55},{8,24},{9,... | collective-permute-start | bytes 98312 | tf_op jit(solution)/shard_map/ppermute | solution.py:430
  79.3 1.4 collective-permute-start.15
  80.6 1.4 collective-permute-done.15.a
  82.0 2.3 %collective-permute-start.21 = (f32[64,128]{1,0:T(8,128)S(1)}, f32[64,128]{1,0:T(8,128)S(1)}, u32[]{:S(2)}, u32[]{:S(2)}) collective-permute-start(f32[64,128]{1,0:T(8,128)S(1)} %shard_map.63.a), channel_id=1, source_target_pairs={{0,192},{1,193},{2,194},{3,195},{4,196},{5,197},{6,198},{7,199},{8... | collective-permute-start | bytes 98312 | tf_op jit(solution)/shard_map/ppermute | solution.py:430
  85.9 1.5 %collective-permute-start.24 = (f32[4,8,8,384]{3,2,1,0:T(8,128)S(1)}, f32[4,8,8,384]{3,2,1,0:T(8,128)S(1)}, u32[]{:S(2)}, u32[]{:S(2)}) collective-permute-start(f32[4,8,8,384]{3,2,1,0:T(8,128)S(1)} %get-tuple-element.60), channel_id=1, source_target_pairs={{0,2},{1,3},{2,0},{3,1},{4,6},{5,7},{6,4},{7,5},{8,10},{9,11},{10,... | collective-permute-start | bytes 1179656 | tf_op jit(solution)/shard_map/ppermute | solution.py:371
  87.4 1.2 collective-permute-done.20.c
  88.6 1.6 %collective-permute-start.26 = (f32[4,8,8,384]{3,2,1,0:T(8,128)S(1)}, f32[4,8,8,384]{3,2,1,0:T(8,128)S(1)}, u32[]{:S(2)}, u32[]{:S(2)}) collective-permute-start(f32[4,8,8,384]{3,2,1,0:T(8,128)S(1)} %get-tuple-element.61), channel_id=1, source_target_pairs={{0,4},{1,5},{2,6},{3,7},{4,0},{5,1},{6,2},{7,3},{8,12},{9,13},{10,... | collective-permute-start | bytes 1179656 | tf_op jit(solution)/shard_map/ppermute | solution.py:371
  90.2 1.3 collective-permute-start.28
  91.5 0.9 collective-permute-start.23
  92.7 4.4 %collective-permute-done.24.rest_2_ = f32[4,8,8,384]{3,2,1,0:T(8,128)S(1)} collective-permute-done((f32[4,8,8,384]{3,2,1,0:T(8,128)S(1)}, f32[4,8,8,384]{3,2,1,0:T(8,128)S(1)}, u32[]{:S(2)}, u32[]{:S(2)}) %collective-permute-start.24) | collective-permute-done | bytes 393248 | tf_op jit(solution)/shard_map/ppermute | solution.py:371
  97.1 1.5 collective-permute-start.41
  98.6 8.2 %collective-permute-done.26.rest_4_ = f32[4,8,8,384]{3,2,1,0:T(8,128)S(1)} collective-permute-done((f32[4,8,8,384]{3,2,1,0:T(8,128)S(1)}, f32[4,8,8,384]{3,2,1,0:T(8,128)S(1)}, u32[]{:S(2)}, u32[]{:S(2)}) %collective-permute-start.26) | collective-permute-done | bytes 393248 | tf_op jit(solution)/shard_map/ppermute | solution.py:371
  106.8 3.7 %collective-permute-done.28.rest_6_ = f32[4,8,8,384]{3,2,1,0:T(8,128)S(1)} collective-permute-done((f32[4,8,8,384]{3,2,1,0:T(8,128)S(1)}, f32[4,8,8,384]{3,2,1,0:T(8,128)S(1)}, u32[]{:S(2)}, u32[]{:S(2)}) %collective-permute-start.28) | collective-permute-done | bytes 393248 | tf_op jit(solution)/shard_map/ppermute | solution.py:371
  112.0 1.9 %shard_map.65.left = f32[64,192]{1,0:T(8,128)S(1)} custom-call(f32[64,128]{1,0:T(8,128)S(1)} %shard_map.64.own, f32[64,128]{1,0:T(8,128)S(1)} %collective-permute-done.22.other), custom_call_target="tpu_custom_call" | custom-call | bytes 131072 | tf_op jit(solution)/shard_map/pallas_call | solution.py:438
  114.0 1.1 collective-permute-done.29.rest_7_
  115.7 4.1 %collective-permute-start.42 = (f32[2,32,8,384]{3,2,1,0:T(8,128)S(1)}, f32[2,32,8,384]{3,2,1,0:T(8,128)S(1)}, u32[]{:S(2)}, u32[]{:S(2)}) collective-permute-start(f32[2,32,8,384]{3,2,1,0:T(8,128)S(1)} %collective-permute-done.41.rest_4_), channel_id=1, source_target_pairs={{0,1},{1,0},{2,3},{3,2},{4,5},{5,4},{6,7},{7,6},{8,9},{9,8},{10,11... | collective-permute-start | bytes 2359304 | tf_op jit(solution)/shard_map/ppermute | solution.py:371
  120.1 1.1 collective-permute-start.32
  121.1 2.0 %collective-permute-start.30 = (f32[2,4,4,8,384]{4,3,2,1,0:T(8,128)S(1)}, f32[2,4,4,8,384]{4,3,2,1,0:T(8,128)S(1)}, u32[]{:S(2)}, u32[]{:S(2)}) collective-permute-start(f32[2,4,4,8,384]{4,3,2,1,0:T(8,128)S(1)} %get-tuple-element.63), channel_id=1, source_target_pairs={{0,4},{1,5},{2,6},{3,7},{4,0},{5,1},{6,2},{7,3},{8,12},{9,13},{10,... | collective-permute-start | bytes 1179656 | tf_op jit(solution)/shard_map/ppermute | solution.py:371
  124.0 6.6 %collective-permute-done.34.same = f32[2,4,4,8,384]{4,3,2,1,0:T(8,128)S(1)} collective-permute-done((f32[2,4,4,8,384]{4,3,2,1,0:T(8,128)S(1)}, f32[2,4,4,8,384]{4,3,2,1,0:T(8,128)S(1)}, u32[]{:S(2)}, u32[]{:S(2)}) %collective-permute-start.34) | collective-permute-done | bytes 393248 | tf_op jit(solution)/shard_map/ppermute | solution.py:371
  130.5 1.3 collective-permute-start.35
  131.8 9.4 %collective-permute-start.33 = (f32[2,4,4,8,384]{4,3,2,1,0:T(8,128)S(1)}, f32[2,4,4,8,384]{4,3,2,1,0:T(8,128)S(1)}, u32[]{:S(2)}, u32[]{:S(2)}) collective-permute-start(f32[2,4,4,8,384]{4,3,2,1,0:T(8,128)S(1)} %collective-permute-done.32.same), channel_id=1, source_target_pairs={{0,1},{1,0},{2,3},{3,2},{4,5},{5,4},{6,7},{7,6},{8,9},{9,8},{10,11... | collective-permute-start | bytes 1179656 | tf_op jit(solution)/shard_map/ppermute | solution.py:371
  141.2 3.5 %inner.1.rest_0_ = f32[8,6,32,384]{3,2,1,0:T(8,128)} custom-call(f32[64,192]{1,0:T(8,128)S(1)} %shard_map.65.left, f32[2,32,8,384]{3,2,1,0:T(8,128)S(1)} %get-tuple-element.55.refs_15_.rest_0_, f32[2,32,8,384]{3,2,1,0:T(8,128)S(1)} %collective-permute-done.37.rest_1_, f32[2,32,8,384]{3,2,1,0:T(8,128)S(1)} %collective-permute-done.38.one.rest_2_, ...), custom_call_target="tpu_custom_call" | custom-call | tf_op jit(solution)/shard_map/inner/pallas_call | solution.py:444
  (68 shorter events, 12.5 us)
Async XLA Ops:
  2.4 15.3 %collective-permute-start.1 = (f32[44,8,384]{2,1,0:T(8,128)S(1)}, f32[44,8,384]{2,1,0:T(8,128)S(1)}, u32[]{:S(2)}, u32[]{:S(2)}) collective-permute-start(f32[44,8,384]{2,1,0:T(8,128)S(1)} %get-tuple-element.37.e4), channel_id=1, source_target_pairs={{0,8},{8,16},{16,24},{24,32},{32,40},{40,48},{48,56},{56,64},{64,7... | collective-permute-start | bytes 1622024 | tf_op jit(solution)/shard_map/ppermute | solution.py:368
  6.8 28.6 %collective-permute-start.4 = (f32[44,8,384]{2,1,0:T(8,128)S(1)}, f32[44,8,384]{2,1,0:T(8,128)S(1)}, u32[]{:S(2)}, u32[]{:S(2)}) collective-permute-start(f32[44,8,384]{2,1,0:T(8,128)S(1)} %get-tuple-element.39.e1), channel_id=1, source_target_pairs={{8,0},{16,8},{24,16},{32,24},{40,32},{48,40},{56,48},{64,56},{72,6... | collective-permute-start | bytes 1622024 | tf_op jit(solution)/shard_map/ppermute | solution.py:368
  9.4 16.8 %collective-permute-start.2 = (f32[32,8,384]{2,1,0:T(8,128)S(1)}, f32[32,8,384]{2,1,0:T(8,128)S(1)}, u32[]{:S(2)}, u32[]{:S(2)}) collective-permute-start(f32[32,8,384]{2,1,0:T(8,128)S(1)} %get-tuple-element.38.e5), channel_id=1, source_target_pairs={{0,8},{8,16},{16,24},{24,32},{32,40},{40,48},{48,56},{56,64},{64,7... | collective-permute-start | bytes 1179656 | tf_op jit(solution)/shard_map/ppermute | solution.py:368
  13.6 8.1 %copy-start.1 = (f32[3,32,6,384]{3,1,2,0:T(8,128)S(1)}, f32[3,32,6,384]{3,1,2,0:T(8,128)}, u32[]{:S(2)}) copy-start(f32[3,32,6,384]{3,1,2,0:T(8,128)} %param.6) | copy-start | bytes 2654212
  13.6 16.8 %collective-permute-start.6 = (f32[32,8,384]{2,1,0:T(8,128)S(1)}, f32[32,8,384]{2,1,0:T(8,128)S(1)}, u32[]{:S(2)}, u32[]{:S(2)}) collective-permute-start(f32[32,8,384]{2,1,0:T(8,128)S(1)} %get-tuple-element.40.e0), channel_id=1, source_target_pairs={{8,0},{16,8},{24,16},{32,24},{40,32},{48,40},{56,48},{64,56},{72,6... | collective-permute-start | bytes 1179656 | tf_op jit(solution)/shard_map/ppermute | solution.py:368
  17.7 24.5 %collective-permute-start.3 = (f32[44,8,384]{2,1,0:T(8,128)S(1)}, f32[44,8,384]{2,1,0:T(8,128)S(1)}, u32[]{:S(2)}, u32[]{:S(2)}) collective-permute-start(f32[44,8,384]{2,1,0:T(8,128)S(1)} %collective-permute-done.1.lo2.refs_1_), channel_id=1, source_target_pairs={{0,1},{1,0},{2,3},{3,2},{4,5},{5,4},{6,7},{7,6},{8,9},{9,8},{10,11... | collective-permute-start | bytes 1622024 | tf_op jit(solution)/shard_map/ppermute | solution.py:371
  32.9 58.6 %collective-permute-start.40 = (f32[2,32,8,384]{3,2,1,0:T(8,128)S(1)}, f32[2,32,8,384]{3,2,1,0:T(8,128)S(1)}, u32[]{:S(2)}, u32[]{:S(2)}) collective-permute-start(f32[2,32,8,384]{3,2,1,0:T(8,128)S(1)} %get-tuple-element.55.refs_15_.rest_0_), channel_id=1, source_target_pairs={{0,6},{1,7},{2,4},{3,5},{4,2},{5,3},{6,0},{7,1},{8,14},{9,15},{10,... | collective-permute-start | bytes 2359304 | tf_op jit(solution)/shard_map/ppermute | solution.py:371
  35.5 6.9 %collective-permute-start.5 = (f32[44,8,384]{2,1,0:T(8,128)S(1)}, f32[44,8,384]{2,1,0:T(8,128)S(1)}, u32[]{:S(2)}, u32[]{:S(2)}) collective-permute-start(f32[44,8,384]{2,1,0:T(8,128)S(1)} %collective-permute-done.4.hi2.refs_8_), channel_id=1, source_target_pairs={{0,1},{1,0},{2,3},{3,2},{4,5},{5,4},{6,7},{7,6},{8,9},{9,8},{10,11... | collective-permute-start | bytes 1622024 | tf_op jit(solution)/shard_map/ppermute | solution.py:371
  37.4 12.0 %collective-permute-start = (f32[32,8,384]{2,1,0:T(8,128)S(1)}, f32[32,8,384]{2,1,0:T(8,128)S(1)}, u32[]{:S(2)}, u32[]{:S(2)}) collective-permute-start(f32[32,8,384]{2,1,0:T(8,128)S(1)} %get-tuple-element.36.e3), channel_id=1, source_target_pairs={{0,8},{8,16},{16,24},{24,32},{32,40},{40,48},{48,56},{56,64},{64,7... | collective-permute-start | bytes 1179656 | tf_op jit(solution)/shard_map/ppermute | solution.py:368
  41.0 13.9 %collective-permute-start.7 = (f32[32,8,384]{2,1,0:T(8,128)S(1)}, f32[32,8,384]{2,1,0:T(8,128)S(1)}, u32[]{:S(2)}, u32[]{:S(2)}) collective-permute-start(f32[32,8,384]{2,1,0:T(8,128)S(1)} %get-tuple-element.41.e2), channel_id=1, source_target_pairs={{8,0},{16,8},{24,16},{32,24},{40,32},{48,40},{56,48},{64,56},{72,6... | collective-permute-start | bytes 1179656 | tf_op jit(solution)/shard_map/ppermute | solution.py:368
  42.3 50.2 %collective-permute-start.38 = (f32[2,32,8,384]{3,2,1,0:T(8,128)S(1)}, f32[2,32,8,384]{3,2,1,0:T(8,128)S(1)}, u32[]{:S(2)}, u32[]{:S(2)}) collective-permute-start(f32[2,32,8,384]{3,2,1,0:T(8,128)S(1)} %get-tuple-element.55.refs_15_.rest_0_), channel_id=1, source_target_pairs={{0,2},{1,3},{2,0},{3,1},{4,6},{5,7},{6,4},{7,5},{8,10},{9,11},{10,... | collective-permute-start | bytes 2359304 | tf_op jit(solution)/shard_map/ppermute | solution.py:371
  42.4 12.5 %copy-start.4 = (s32[16]{0:T(128)S(1)}, s32[16]{0:T(128)}, u32[]{:S(2)}) copy-start(s32[16]{0:T(128)} %obs_column.1) | copy-start | bytes 196
  54.9 11.6 %copy-start.2 = (f32[32,16]{0,1:T(8,128)S(1)}, f32[32,16]{0,1:T(8,128)}, u32[]{:S(2)}) copy-start(f32[32,16]{0,1:T(8,128)} %param.8) | copy-start | bytes 6148
  54.9 11.6 %copy-start.3 = (f32[32,16]{0,1:T(8,128)S(1)}, f32[32,16]{0,1:T(8,128)}, u32[]{:S(2)}) copy-start(f32[32,16]{0,1:T(8,128)} %param.9) | copy-start | bytes 6148
  58.4 3.9 %collective-permute-start.13 = (f32[8,512]{1,0:T(8,128)S(1)}, f32[8,512]{1,0:T(8,128)S(1)}, u32[]{:S(2)}, u32[]{:S(2)}) collective-permute-start(f32[8,512]{1,0:T(8,128)S(1)} %get-tuple-element.58.refs_0_), channel_id=1, source_target_pairs={{0,6},{1,7},{2,4},{3,5},{4,2},{5,3},{6,0},{7,1},{8,14},{9,15},{10,... | collective-permute-start | bytes 49160 | tf_op jit(solution)/shard_map/ppermute | solution.py:371
  58.7 5.6 %collective-permute-start.11 = (f32[8,512]{1,0:T(8,128)S(1)}, f32[8,512]{1,0:T(8,128)S(1)}, u32[]{:S(2)}, u32[]{:S(2)}) collective-permute-start(f32[8,512]{1,0:T(8,128)S(1)} %get-tuple-element.58.refs_0_), channel_id=1, source_target_pairs={{0,4},{1,5},{2,6},{3,7},{4,0},{5,1},{6,2},{7,3},{8,12},{9,13},{10,... | collective-permute-start | bytes 49160 | tf_op jit(solution)/shard_map/ppermute | solution.py:371
  60.2 4.9 %collective-permute-start.9 = (f32[8,512]{1,0:T(8,128)S(1)}, f32[8,512]{1,0:T(8,128)S(1)}, u32[]{:S(2)}, u32[]{:S(2)}) collective-permute-start(f32[8,512]{1,0:T(8,128)S(1)} %get-tuple-element.58.refs_0_), channel_id=1, source_target_pairs={{0,2},{1,3},{2,0},{3,1},{4,6},{5,7},{6,4},{7,5},{8,10},{9,11},{10,... | collective-permute-start | bytes 49160 | tf_op jit(solution)/shard_map/ppermute | solution.py:371
  62.3 3.1 %collective-permute-start.8 = (f32[8,512]{1,0:T(8,128)S(1)}, f32[8,512]{1,0:T(8,128)S(1)}, u32[]{:S(2)}, u32[]{:S(2)}) collective-permute-start(f32[8,512]{1,0:T(8,128)S(1)} %get-tuple-element.58.refs_0_), channel_id=1, source_target_pairs={{0,1},{1,0},{2,3},{3,2},{4,5},{5,4},{6,7},{7,6},{8,9},{9,8},{10,11... | collective-permute-start | bytes 49160 | tf_op jit(solution)/shard_map/ppermute | solution.py:371
  64.3 1.6 %collective-permute-start.14 = (f32[8,512]{1,0:T(8,128)S(1)}, f32[8,512]{1,0:T(8,128)S(1)}, u32[]{:S(2)}, u32[]{:S(2)}) collective-permute-start(f32[8,512]{1,0:T(8,128)S(1)} %collective-permute-done.13.refs_6_), channel_id=1, source_target_pairs={{0,1},{1,0},{2,3},{3,2},{4,5},{5,4},{6,7},{7,6},{8,9},{9,8},{10,11... | collective-permute-start | bytes 49160 | tf_op jit(solution)/shard_map/ppermute | solution.py:371
  65.1 1.2 collective-permute-start.12
  65.4 1.2 collective-permute-start.10
  66.9 12.3 %collective-permute-start.18 = (f32[64,128]{1,0:T(8,128)S(1)}, f32[64,128]{1,0:T(8,128)S(1)}, u32[]{:S(2)}, u32[]{:S(2)}) collective-permute-start(f32[64,128]{1,0:T(8,128)S(1)} %shard_map.62), channel_id=1, source_target_pairs={{0,0},{1,33},{2,2},{3,35},{4,4},{5,37},{6,6},{7,39},{8,8},{9,41},{... | collective-permute-start | bytes 98312 | tf_op jit(solution)/shard_map/ppermute | solution.py:430
  74.4 6.2 %collective-permute-start.17 = (f32[64,128]{1,0:T(8,128)S(1)}, f32[64,128]{1,0:T(8,128)S(1)}, u32[]{:S(2)}, u32[]{:S(2)}) collective-permute-start(f32[64,128]{1,0:T(8,128)S(1)} %shard_map.62), channel_id=1, source_target_pairs={{0,24},{1,41},{2,26},{3,43},{4,28},{5,45},{6,30},{7,47},{8,32},{9,... | collective-permute-start | bytes 98312 | tf_op jit(solution)/shard_map/ppermute | solution.py:430
  75.8 4.8 %collective-permute-start.16 = (f32[64,128]{1,0:T(8,128)S(1)}, f32[64,128]{1,0:T(8,128)S(1)}, u32[]{:S(2)}, u32[]{:S(2)}) collective-permute-start(f32[64,128]{1,0:T(8,128)S(1)} %shard_map.62), channel_id=1, source_target_pairs={{0,16},{1,49},{2,18},{3,51},{4,20},{5,53},{6,22},{7,55},{8,24},{9,... | collective-permute-start | bytes 98312 | tf_op jit(solution)/shard_map/ppermute | solution.py:430
  79.3 2.8 %collective-permute-start.15 = (f32[64,128]{1,0:T(8,128)S(1)}, f32[64,128]{1,0:T(8,128)S(1)}, u32[]{:S(2)}, u32[]{:S(2)}) collective-permute-start(f32[64,128]{1,0:T(8,128)S(1)} %shard_map.62), channel_id=1, source_target_pairs={{0,8},{1,57},{2,10},{3,59},{4,12},{5,61},{6,14},{7,63},{8,16},{9,1... | collective-permute-start | bytes 98312 | tf_op jit(solution)/shard_map/ppermute | solution.py:430
  82.0 3.9 %collective-permute-start.21 = (f32[64,128]{1,0:T(8,128)S(1)}, f32[64,128]{1,0:T(8,128)S(1)}, u32[]{:S(2)}, u32[]{:S(2)}) collective-permute-start(f32[64,128]{1,0:T(8,128)S(1)} %shard_map.63.a), channel_id=1, source_target_pairs={{0,192},{1,193},{2,194},{3,195},{4,196},{5,197},{6,198},{7,199},{8... | collective-permute-start | bytes 98312 | tf_op jit(solution)/shard_map/ppermute | solution.py:430
  84.3 4.3 %collective-permute-start.20 = (f32[64,128]{1,0:T(8,128)S(1)}, f32[64,128]{1,0:T(8,128)S(1)}, u32[]{:S(2)}, u32[]{:S(2)}) collective-permute-start(f32[64,128]{1,0:T(8,128)S(1)} %shard_map.63.a), channel_id=1, source_target_pairs={{0,128},{1,129},{2,130},{3,131},{4,132},{5,133},{6,134},{7,135},{8... | collective-permute-start | bytes 98312 | tf_op jit(solution)/shard_map/ppermute | solution.py:430
  85.2 5.0 %collective-permute-start.19 = (f32[64,128]{1,0:T(8,128)S(1)}, f32[64,128]{1,0:T(8,128)S(1)}, u32[]{:S(2)}, u32[]{:S(2)}) collective-permute-start(f32[64,128]{1,0:T(8,128)S(1)} %shard_map.63.a), channel_id=1, source_target_pairs={{0,64},{1,65},{2,66},{3,67},{4,68},{5,69},{6,70},{7,71},{8,72},{9,... | collective-permute-start | bytes 98312 | tf_op jit(solution)/shard_map/ppermute | solution.py:430
  85.9 11.2 %collective-permute-start.24 = (f32[4,8,8,384]{3,2,1,0:T(8,128)S(1)}, f32[4,8,8,384]{3,2,1,0:T(8,128)S(1)}, u32[]{:S(2)}, u32[]{:S(2)}) collective-permute-start(f32[4,8,8,384]{3,2,1,0:T(8,128)S(1)} %get-tuple-element.60), channel_id=1, source_target_pairs={{0,2},{1,3},{2,0},{3,1},{4,6},{5,7},{6,4},{7,5},{8,10},{9,11},{10,... | collective-permute-start | bytes 1179656 | tf_op jit(solution)/shard_map/ppermute | solution.py:371
  88.6 18.1 %collective-permute-start.26 = (f32[4,8,8,384]{3,2,1,0:T(8,128)S(1)}, f32[4,8,8,384]{3,2,1,0:T(8,128)S(1)}, u32[]{:S(2)}, u32[]{:S(2)}) collective-permute-start(f32[4,8,8,384]{3,2,1,0:T(8,128)S(1)} %get-tuple-element.61), channel_id=1, source_target_pairs={{0,4},{1,5},{2,6},{3,7},{4,0},{5,1},{6,2},{7,3},{8,12},{9,13},{10,... | collective-permute-start | bytes 1179656 | tf_op jit(solution)/shard_map/ppermute | solution.py:371
  90.2 20.2 %collective-permute-start.28 = (f32[4,8,8,384]{3,2,1,0:T(8,128)S(1)}, f32[4,8,8,384]{3,2,1,0:T(8,128)S(1)}, u32[]{:S(2)}, u32[]{:S(2)}) collective-permute-start(f32[4,8,8,384]{3,2,1,0:T(8,128)S(1)} %get-tuple-element.62), channel_id=1, source_target_pairs={{0,6},{1,7},{2,4},{3,5},{4,2},{5,3},{6,0},{7,1},{8,14},{9,15},{10,... | collective-permute-start | bytes 1179656 | tf_op jit(solution)/shard_map/ppermute | solution.py:371
  91.5 19.9 %collective-permute-start.23 = (f32[4,8,8,384]{3,2,1,0:T(8,128)S(1)}, f32[4,8,8,384]{3,2,1,0:T(8,128)S(1)}, u32[]{:S(2)}, u32[]{:S(2)}) collective-permute-start(f32[4,8,8,384]{3,2,1,0:T(8,128)S(1)} %get-tuple-element.59.rest_0_), channel_id=1, source_target_pairs={{0,1},{1,0},{2,3},{3,2},{4,5},{5,4},{6,7},{7,6},{8,9},{9,8},{10,11... | collective-permute-start | bytes 1179656 | tf_op jit(solution)/shard_map/ppermute | solution.py:371
  92.5 4.6 %collective-permute-start.22 = (f32[64,128]{1,0:T(8,128)S(1)}, f32[64,128]{1,0:T(8,128)S(1)}, u32[]{:S(2)}, u32[]{:S(2)}) collective-permute-start(f32[64,128]{1,0:T(8,128)S(1)} %shard_map.64.own), channel_id=1, source_target_pairs={{0,1},{1,0},{2,3},{3,2},{4,5},{5,4},{6,7},{7,6},{8,9},{9,8},{10,11... | collective-permute-start | bytes 98312 | tf_op jit(solution)/shard_map/ppermute | solution.py:371
  97.1 14.3 %collective-permute-start.25 = (f32[4,8,8,384]{3,2,1,0:T(8,128)S(1)}, f32[4,8,8,384]{3,2,1,0:T(8,128)S(1)}, u32[]{:S(2)}, u32[]{:S(2)}) collective-permute-start(f32[4,8,8,384]{3,2,1,0:T(8,128)S(1)} %collective-permute-done.24.rest_2_), channel_id=1, source_target_pairs={{0,1},{1,0},{2,3},{3,2},{4,5},{5,4},{6,7},{7,6},{8,9},{9,8},{10,11... | collective-permute-start | bytes 1179656 | tf_op jit(solution)/shard_map/ppermute | solution.py:371
  97.1 18.6 %collective-permute-start.41 = (f32[2,32,8,384]{3,2,1,0:T(8,128)S(1)}, f32[2,32,8,384]{3,2,1,0:T(8,128)S(1)}, u32[]{:S(2)}, u32[]{:S(2)}) collective-permute-start(f32[2,32,8,384]{3,2,1,0:T(8,128)S(1)} %shard_map.67), channel_id=1, source_target_pairs={{0,6},{1,3},{2,4},{3,1},{4,2},{5,7},{6,0},{7,5},{8,14},{9,11},{10,... | collective-permute-start | bytes 2359304 | tf_op jit(solution)/shard_map/ppermute | solution.py:415
  106.7 5.2 %collective-permute-start.27 = (f32[4,8,8,384]{3,2,1,0:T(8,128)S(1)}, f32[4,8,8,384]{3,2,1,0:T(8,128)S(1)}, u32[]{:S(2)}, u32[]{:S(2)}) collective-permute-start(f32[4,8,8,384]{3,2,1,0:T(8,128)S(1)} %collective-permute-done.26.rest_4_), channel_id=1, source_target_pairs={{0,1},{1,0},{2,3},{3,2},{4,5},{5,4},{6,7},{7,6},{8,9},{9,8},{10,11... | collective-permute-start | bytes 1179656 | tf_op jit(solution)/shard_map/ppermute | solution.py:371
  110.5 9.6 %collective-permute-start.37 = (f32[2,32,8,384]{3,2,1,0:T(8,128)S(1)}, f32[2,32,8,384]{3,2,1,0:T(8,128)S(1)}, u32[]{:S(2)}, u32[]{:S(2)}) collective-permute-start(f32[2,32,8,384]{3,2,1,0:T(8,128)S(1)} %get-tuple-element.55.refs_15_.rest_0_), channel_id=1, source_target_pairs={{0,1},{1,0},{2,3},{3,2},{4,5},{5,4},{6,7},{7,6},{8,9},{9,8},{10,11... | collective-permute-start | bytes 2359304 | tf_op jit(solution)/shard_map/ppermute | solution.py:371
  111.4 9.7 %collective-permute-start.43 = (f32[2,32,8,384]{3,2,1,0:T(8,128)S(1)}, f32[2,32,8,384]{3,2,1,0:T(8,128)S(1)}, u32[]{:S(2)}, u32[]{:S(2)}) collective-permute-start(f32[2,32,8,384]{3,2,1,0:T(8,128)S(1)} %collective-permute-done.40.three.rest_6_), channel_id=1, source_target_pairs={{0,1},{1,0},{2,3},{3,2},{4,5},{5,4},{6,7},{7,6},{8,9},{9,8},{10,11... | collective-permute-start | bytes 2359304 | tf_op jit(solution)/shard_map/ppermute | solution.py:371
  111.4 3.6 %collective-permute-start.29 = (f32[4,8,8,384]{3,2,1,0:T(8,128)S(1)}, f32[4,8,8,384]{3,2,1,0:T(8,128)S(1)}, u32[]{:S(2)}, u32[]{:S(2)}) collective-permute-start(f32[4,8,8,384]{3,2,1,0:T(8,128)S(1)} %collective-permute-done.28.rest_6_), channel_id=1, source_target_pairs={{0,1},{1,0},{2,3},{3,2},{4,5},{5,4},{6,7},{7,6},{8,9},{9,8},{10,11... | collective-permute-start | bytes 1179656 | tf_op jit(solution)/shard_map/ppermute | solution.py:371
  111.9 11.2 %collective-permute-start.39 = (f32[2,32,8,384]{3,2,1,0:T(8,128)S(1)}, f32[2,32,8,384]{3,2,1,0:T(8,128)S(1)}, u32[]{:S(2)}, u32[]{:S(2)}) collective-permute-start(f32[2,32,8,384]{3,2,1,0:T(8,128)S(1)} %collective-permute-done.38.one.rest_2_), channel_id=1, source_target_pairs={{0,1},{1,0},{2,3},{3,2},{4,5},{5,4},{6,7},{7,6},{8,9},{9,8},{10,11... | collective-permute-start | bytes 2359304 | tf_op jit(solution)/shard_map/ppermute | solution.py:371
  115.7 25.5 %collective-permute-start.42 = (f32[2,32,8,384]{3,2,1,0:T(8,128)S(1)}, f32[2,32,8,384]{3,2,1,0:T(8,128)S(1)}, u32[]{:S(2)}, u32[]{:S(2)}) collective-permute-start(f32[2,32,8,384]{3,2,1,0:T(8,128)S(1)} %collective-permute-done.41.rest_4_), channel_id=1, source_target_pairs={{0,1},{1,0},{2,3},{3,2},{4,5},{5,4},{6,7},{7,6},{8,9},{9,8},{10,11... | collective-permute-start | bytes 2359304 | tf_op jit(solution)/shard_map/ppermute | solution.py:371
  119.8 10.7 %collective-permute-start.34 = (f32[2,4,4,8,384]{4,3,2,1,0:T(8,128)S(1)}, f32[2,4,4,8,384]{4,3,2,1,0:T(8,128)S(1)}, u32[]{:S(2)}, u32[]{:S(2)}) collective-permute-start(f32[2,4,4,8,384]{4,3,2,1,0:T(8,128)S(1)} %get-tuple-element.65), channel_id=1, source_target_pairs={{0,2},{1,3},{2,0},{3,1},{4,6},{5,7},{6,4},{7,5},{8,10},{9,11},{10,... | collective-permute-start | bytes 1179656 | tf_op jit(solution)/shard_map/ppermute | solution.py:371
  120.1 11.8 %collective-permute-start.32 = (f32[2,4,4,8,384]{4,3,2,1,0:T(8,128)S(1)}, f32[2,4,4,8,384]{4,3,2,1,0:T(8,128)S(1)}, u32[]{:S(2)}, u32[]{:S(2)}) collective-permute-start(f32[2,4,4,8,384]{4,3,2,1,0:T(8,128)S(1)} %get-tuple-element.64), channel_id=1, source_target_pairs={{0,6},{1,7},{2,4},{3,5},{4,2},{5,3},{6,0},{7,1},{8,14},{9,15},{10,... | collective-permute-start | bytes 1179656 | tf_op jit(solution)/shard_map/ppermute | solution.py:371
  121.1 20.1 %collective-permute-start.30 = (f32[2,4,4,8,384]{4,3,2,1,0:T(8,128)S(1)}, f32[2,4,4,8,384]{4,3,2,1,0:T(8,128)S(1)}, u32[]{:S(2)}, u32[]{:S(2)}) collective-permute-start(f32[2,4,4,8,384]{4,3,2,1,0:T(8,128)S(1)} %get-tuple-element.63), channel_id=1, source_target_pairs={{0,4},{1,5},{2,6},{3,7},{4,0},{5,1},{6,2},{7,3},{8,12},{9,13},{10,... | collective-permute-start | bytes 1179656 | tf_op jit(solution)/shard_map/ppermute | solution.py:371
  123.1 21.7 %collective-permute-start.36 = (f32[2,4,4,8,384]{4,3,2,1,0:T(8,128)S(1)}, f32[2,4,4,8,384]{4,3,2,1,0:T(8,128)S(1)}, u32[]{:S(2)}, u32[]{:S(2)}) collective-permute-start(f32[2,4,4,8,384]{4,3,2,1,0:T(8,128)S(1)} %get-tuple-element.66.same), channel_id=1, source_target_pairs={{0,1},{1,0},{2,3},{3,2},{4,5},{5,4},{6,7},{7,6},{8,9},{9,8},{10,11... | collective-permute-start | bytes 1179656 | tf_op jit(solution)/shard_map/ppermute | solution.py:371
  130.5 15.2 %collective-permute-start.35 = (f32[2,4,4,8,384]{4,3,2,1,0:T(8,128)S(1)}, f32[2,4,4,8,384]{4,3,2,1,0:T(8,128)S(1)}, u32[]{:S(2)}, u32[]{:S(2)}) collective-permute-start(f32[2,4,4,8,384]{4,3,2,1,0:T(8,128)S(1)} %collective-permute-done.34.same), channel_id=1, source_target_pairs={{0,1},{1,0},{2,3},{3,2},{4,5},{5,4},{6,7},{7,6},{8,9},{9,8},{10,11... | collective-permute-start | bytes 1179656 | tf_op jit(solution)/shard_map/ppermute | solution.py:371
  131.8 14.7 %collective-permute-start.33 = (f32[2,4,4,8,384]{4,3,2,1,0:T(8,128)S(1)}, f32[2,4,4,8,384]{4,3,2,1,0:T(8,128)S(1)}, u32[]{:S(2)}, u32[]{:S(2)}) collective-permute-start(f32[2,4,4,8,384]{4,3,2,1,0:T(8,128)S(1)} %collective-permute-done.32.same), channel_id=1, source_target_pairs={{0,1},{1,0},{2,3},{3,2},{4,5},{5,4},{6,7},{7,6},{8,9},{9,8},{10,11... | collective-permute-start | bytes 1179656 | tf_op jit(solution)/shard_map/ppermute | solution.py:371
  141.2 6.2 %collective-permute-start.31 = (f32[2,4,4,8,384]{4,3,2,1,0:T(8,128)S(1)}, f32[2,4,4,8,384]{4,3,2,1,0:T(8,128)S(1)}, u32[]{:S(2)}, u32[]{:S(2)}) collective-permute-start(f32[2,4,4,8,384]{4,3,2,1,0:T(8,128)S(1)} %collective-permute-done.30.same), channel_id=1, source_target_pairs={{0,1},{1,0},{2,3},{3,2},{4,5},{5,4},{6,7},{7,6},{8,9},{9,8},{10,11... | collective-permute-start | bytes 1179656 | tf_op jit(solution)/shard_map/ppermute | solution.py:371
  (1 other events, 1.2 us)

commit v4 on v3

--- a/solution.py
+++ b/solution.py
@@ -52,11 +52,13 @@
 def rows_courant_body(first_ref, last_ref, courant, first_out, last_out):
     core = lax.rem(lax.axis_index("mem"), 2)
     levels = first_ref.shape[2]
-    for src, dst, row in ((first_ref, first_out, core), (last_ref, last_out, courant.shape[1] - 2 + core)):
+    tiles = levels // 16
+    for src, dst, row in ((first_ref, first_out, 0), (last_ref, last_out, courant.shape[1] - 1)):
         relayout_row(src, dst)
         for d in range(3):
-            for tile in range(levels // 8):
-                dst[levels + d * (levels // 8) + tile] = courant[d, row, pl.ds(8 * tile, 8), :]
+            for tile in range(tiles):
+                part = pl.ds(pl.multiple_of(8 * (core * tiles + tile), 8), 8)
+                dst[levels + d * tiles + tile] = courant[d, row, part, :]
 
 
 def pick_body(one, three, out):
@@ -75,8 +77,8 @@
 def coefficients(coef, slot, tile, levels, speeds, keep=None):
     shape = speeds[0].shape
     lane = lax.broadcasted_iota(jnp.int32, shape, 1)
-    level = lax.broadcasted_iota(jnp.int32, shape, 0)
-    part = pl.ds(8 * tile, 8)
+    level = lax.broadcasted_iota(jnp.int32, shape, 0) + 8 * tile
+    part = pl.ds(8 * tile if isinstance(tile, int) else pl.multiple_of(8 * tile, 8), 8)
     total = None
     for d, a in enumerate(speeds):
         low = jnp.maximum(a, 0.0) + DIFFUSION
@@ -86,10 +88,9 @@
         if d == 1:
             low = jnp.where(lane == 0, 0.0, low)
             high = jnp.where(lane == shape[1] - 1, 0.0, high)
-        if d == 2 and tile == 0:
+        if d == 2:
             low = jnp.where(level == 0, 0.0, low)
-        if d == 2 and tile == levels // 8 - 1:
-            high = jnp.where(level == 7, 0.0, high)
+            high = jnp.where(level == levels - 1, 0.0, high)
         coef[slot, 2 * d, part] = low if keep is None else low * keep
         coef[slot, 2 * d + 1, part] = high if keep is None else high * keep
     center = 1.0 - total
@@ -103,18 +104,17 @@
             coefficients(coef, row, tile, levels, [courant[d, row, pl.ds(8 * tile, 8), :] for d in range(3)])
 
 
-def halo_coefficients(coef, halos):
+def halo_coefficients(coef, halos, levels):
     core = lax.rem(lax.axis_index("mem"), 2)
     block = lax.axis_index("rows")
     inside = (block > 0, block < lax.axis_size("rows") - 1)
-    tiles = halos[0].shape[0] // 11
-    levels = 8 * tiles
+    tiles = levels // 16
     for side in range(2):
         keep = jnp.where(inside[side], 1.0, 0.0).astype(F32)
-        for part, j in ((halos[2 * side], core), (halos[2 * side + 1], 1 - core)):
+        for part, half in ((halos[2 * side], core), (halos[2 * side + 1], 1 - core)):
             for tile in range(tiles):
                 speeds = [part[levels + d * tiles + tile] for d in range(3)]
-                coefficients(coef, 2 * side + j, tile, levels, speeds, keep)
+                coefficients(coef, side, half * tiles + tile, levels, speeds, keep)
 
 
 def advance_row(dst, below, here, above, coef, slot):
@@ -152,9 +152,9 @@
 
 def stage_b(lo2, lo2x, hi2, hi2x, lo1, e0, hi1, e5, f0, f1, f4, f5, g1, g2, g3, g4, coef, *outs):
     fm, fp, g0, g5, h1, h4, side = outs
-    halo_coefficients(side, (lo2, lo2x, hi2, hi2x))
-    advance_row(fm, lo2, lo1, e0, side, 1)
-    advance_row(fp, e5, hi1, hi2, side, 2)
+    halo_coefficients(side, (lo2, lo2x, hi2, hi2x), e0.shape[0])
+    advance_row(fm, lo2, lo1, e0, side, 0)
+    advance_row(fp, e5, hi1, hi2, side, 1)
     advance_row(g0, fm, f0, f1, coef, 0)
     advance_row(g5, f4, f5, fp, coef, 5)
     advance_row(h1, g0, g1, g2, coef, 1)
@@ -162,20 +162,17 @@
 
 
 def stage_c(obs_column, *refs):
-    lo3, lo2, lo1, fm, f0, g0, g1, hi3, hi2, hi1, fp, f5, g5, g4, h1, h23, h4, coef, side = refs[:19]
-    chunks, prof, one, two, full = refs[19:23], refs[23], refs[24], refs[25], refs[26]
+    lo3, fm, f0, g0, g1, hi3, fp, f5, g5, g4, h1, h23, h4, coef, side = refs[:15]
+    prof, full, low, high = refs[15:]
     levels, members, cells = g0.shape
-    me = lax.axis_index("mem")
     origin = lax.axis_index("rows") * (6 * cells)
     full[1] = h1[...]
     full[pl.ds(2, 2)] = h23[...]
     full[4] = h4[...]
-    advance_row(one, lo3, lo2, lo1, side, 0)
-    advance_row(two, one, fm, f0, side, 1)
-    advance_row(full.at[0], two, g0, g1, coef, 0)
-    advance_row(one, hi1, hi2, hi3, side, 3)
-    advance_row(two, f5, fp, one, side, 2)
-    advance_row(full.at[5], g4, g5, two, coef, 5)
+    advance_row(low, lo3, fm, f0, side, 0)
+    advance_row(full.at[0], low, g0, g1, coef, 0)
+    advance_row(high, f5, fp, hi3, side, 1)
+    advance_row(full.at[5], g4, g5, high, coef, 5)
     per = prof.shape[1] // levels
     lane = lax.broadcasted_iota(jnp.int32, (members, 128), 1)
     group = 128 // levels
@@ -193,11 +190,14 @@
             acc[p // group] = jnp.where(lane == spot, v, acc[p // group])
     for i, a in enumerate(acc):
         prof[:, pl.ds(128 * i, 128)] = a
-    depth = levels // 4
-    for k in range(4):
-        chip = lax.bitwise_xor(lax.div(me, 2), k)
+
+
+def emit_body(full, *chunks):
+    depth = chunks[0].shape[1]
+    for k, chunk in enumerate(chunks):
+        chip = lax.bitwise_xor(lax.div(lax.axis_index("mem"), 2), k)
         for i, row in enumerate(OUTER):
-            chunks[k][i] = full[row, pl.ds(chip * depth, depth)]
+            chunk[i] = full[row, pl.ds(chip * depth, depth)]
 
 
 def flat_rows(ref):
@@ -307,22 +307,23 @@
     copy.wait()
 
 
-def place_body(distance, same, cross, *rest):
-    out, stack, block, sems = rest[-4:]
+def place_body(distances, *refs):
+    pairs, (out, stack, block, sems) = refs[: 2 * len(distances)], refs[-4:]
     me = lax.axis_index("mem")
-    core, chip = lax.rem(me, 2), lax.bitwise_xor(lax.div(me, 2), distance)
-    rows, depth = same.shape[1], same.shape[2]
-    for row in range(rows):
-        stack[pl.ds(core * depth, depth)] = same[0, row]
-        stack[pl.ds((1 - core) * depth, depth)] = cross[1, row]
-        block[:, row] = members_inside(stack[...])
-    levels = pl.ds(pl.multiple_of(chip * 8, 8), 8)
-    copies = [
-        pltpu.make_async_copy(block.at[:, pl.ds(2 * i, 2)], out.at[:, pl.ds(4 * i, 2), levels, :], sems.at[i])
-        for i in range(2)
-    ]
-    for copy in copies:
-        copy.start()
+    core = lax.rem(me, 2)
+    copies = []
+    for n, distance in enumerate(distances):
+        same, cross = pairs[2 * n], pairs[2 * n + 1]
+        rows, depth = same.shape[1], same.shape[2]
+        for row in range(rows):
+            stack[pl.ds(core * depth, depth)] = same[0, row]
+            stack[pl.ds((1 - core) * depth, depth)] = cross[1, row]
+            block[n, :, row] = members_inside(stack[...])
+        levels = pl.ds(pl.multiple_of(lax.bitwise_xor(lax.div(me, 2), distance) * 8, 8), 8)
+        for i in range(2):
+            here = block.at[n, :, pl.ds(2 * i, 2)]
+            copies.append(pltpu.make_async_copy(here, out.at[:, pl.ds(4 * i, 2), levels, :], sems.at[2 * n + i]))
+            copies[-1].start()
     for copy in copies:
         copy.wait()
 
@@ -346,7 +347,7 @@
         shapes = [jax.ShapeDtypeStruct(row_shape, F32)] * 2
         in_specs, out_specs, args = [row_spec(r) for r in which], [full] * 2, [field, field]
         if with_courant:
-            shape = (levels + 3 * levels // 8, members, cells)
+            shape = (levels + 3 * levels // 16, members, cells)
             shapes = [jax.ShapeDtypeStruct(shape, F32)] * 2
             in_specs.append(VM)
             out_specs = [pl.BlockSpec(shape, lambda *_: (0, 0, 0))] * 2
@@ -375,23 +376,23 @@
     e1, e4 = relayout((1, 4), True)
     lo2, hi2 = exchange(e1, e4)
     e2, e3 = relayout((2, 3))
-    lo3, hi3 = exchange(e2, e3)
     lo2x, hi2x = swap(lo2, 1), swap(hi2, 1)
     coef = call(own_coefficients, (rows, 7, levels, cells), 1, nbytes=7 * row_bytes)(flow)
 
     f0, f1, f4, f5, g1, g2, g3, g4, h23 = call(
         stage_a, [row_shape] * 8 + [(2,) + row_shape], 9, [pltpu.VMEM(row_shape, F32)] * 2, nbytes=20 * row_bytes,
     )(lo1, e0, e1, e2, e3, e4, e5, hi1, coef)
+    lo3, hi3 = exchange(f1, f4)
     fm, fp, g0, g5, h1, h4, side = call(
-        stage_b, [row_shape] * 6 + [(4, 7, levels, cells)], 17, nbytes=20 * row_bytes,
+        stage_b, [row_shape] * 6 + [(2, 7, levels, cells)], 17, nbytes=20 * row_bytes,
     )(lo2, lo2x, hi2, hi2x, lo1, e0, hi1, e5, f0, f1, f4, f5, g1, g2, g3, g4, coef)
     chips = mem // 2
     obs = obs_value.size
-    *chunks, prof = call(
-        stage_c, [(len(OUTER), levels // chips, members, cells)] * chips + [(members, obs)], 20,
-        [pltpu.VMEM(row_shape, F32)] * 2 + [pltpu.VMEM((rows,) + row_shape, F32)],
+    prof, full = call(
+        stage_c, [(members, obs), (rows,) + row_shape], 16, [pltpu.VMEM(row_shape, F32)] * 2,
         smem=1, nbytes=30 * row_bytes,
-    )(obs_column, lo3, lo2, lo1, fm, f0, g0, g1, hi3, hi2, hi1, fp, f5, g5, g4, h1, h23, h4, coef, side)
+    )(obs_column, lo3, fm, f0, g0, g1, hi3, fp, f5, g5, g4, h1, h23, h4, coef, side)
+    chunks = call(emit_body, [(len(OUTER), levels // chips, members, cells)] * chips, 1, nbytes=8 * row_bytes)(full)
 
     def along_chips(parts):
         got = {0: parts[0]}
@@ -455,21 +456,23 @@
         interpret=INTERPRET,
         name="inner",
     )(left, *inner)
-    for k, (same, cross) in along_chips(mixed).items():
+    back = along_chips(mixed)
+    for distances in ((0,), ROUTE):
+        count = len(distances)
         placed = pl.pallas_call(
-            functools.partial(place_body, k),
+            functools.partial(place_body, distances),
             out_shape=result,
-            in_specs=[VM, VM, anywhere],
+            in_specs=[VM] * (2 * count) + [anywhere],
             out_specs=anywhere,
             scratch_shapes=[
                 pltpu.VMEM((8, members, cells), F32),
-                pltpu.VMEM((members, len(OUTER), 8, cells), F32),
-                pltpu.SemaphoreType.DMA((2,)),
+                pltpu.VMEM((count, members, len(OUTER), 8, cells), F32),
+                pltpu.SemaphoreType.DMA((2 * count,)),
             ],
-            input_output_aliases={2: 0},
+            input_output_aliases={2 * count: 0},
             compiler_params=PARAMS,
             interpret=INTERPRET,
-        )(same, cross, placed)
+        )(*[block for k in distances for block in back[k]], placed)
     return jnp.transpose(placed, (0, 2, 1, 3))
 
 

time: 149 us -> 144 us (0.966)
  starting transfers between devices: 75 us -> 71 us
  Pallas kernels: 22 us -> 20 us
    ppermute x6, waiting for transfers between devices: 21.8 us -> 10.8 us  [exchange(): return (lax.ppermute(last, 'rows', up), lax.ppermute(first, 'rows', down))]
    ppermute x30, waiting for transfers between devices: 25.4 us -> 36.2 us  [swap(): return lax.ppermute(a, 'mem', [(i, i ^ k) for i in range(mem)])]
    ppermute x30, starting transfers between devices: 39.9 us -> 30.6 us  [swap(): return lax.ppermute(a, 'mem', [(i, i ^ k) for i in range(mem)])]
    ppermute x7, starting transfers between devices: 17.5 us -> 23.5 us  [shifted(): return lax.ppermute(a, ('rows', 'mem'), pairs)]
    pallas_call x6 -> x5, Pallas kernels: 8.82 us -> 6.59 us  [the longest x1 2.89 us: per_device(): call(stage_c, [(members, obs), (rows,) + row_shape], 16, [pltpu.VMEM(row_...]
    ppermute x7, waiting for transfers between devices: 2.6 us -> 4.15 us  [shifted(): return lax.ppermute(a, ('rows', 'mem'), pairs)]
  transfers between devices with their start and end apart: 44 -> 44, of which waited for: 16 -> 15; matrix products, arithmetic and copies ran while one was open for 0% -> 0% of each run, Pallas kernels for 13% -> 12%
where the time goes in v4:
time: 144 us
  starting transfers between devices  71 us (49%)
  waiting for transfers between devices  51.2 us (36%)
  Pallas kernels  20 us (14%)
    ppermute x30, waiting for transfers between devices, swap(): return lax.ppermute(a, 'mem', [(i, i ^ k) for i in range(mem)])  36.2 us
    ppermute x30, starting transfers between devices, swap(): return lax.ppermute(a, 'mem', [(i, i ^ k) for i in range(mem)])  30.6 us
    ppermute x7, starting transfers between devices, shifted(): return lax.ppermute(a, ('rows', 'mem'), pairs)  23.5 us
    ppermute x6, starting transfers between devices, exchange(): return (lax.ppermute(last, 'rows', up), lax.ppermute(first, 'rows', down))  16.8 us
    ppermute x6, waiting for transfers between devices, exchange(): return (lax.ppermute(last, 'rows', up), lax.ppermute(first, 'rows', down))  10.8 us
    ppermute x7, waiting for transfers between devices, shifted(): return lax.ppermute(a, ('rows', 'mem'), pairs)  4.15 us
    pallas_call x3, Pallas kernels, relayout(): pl.pallas_call(rows_courant_body if with_courant else rows_body, grid=(1,...  3.78 us
    pallas_call x1, Pallas kernels, per_device(): pl.pallas_call(inner_body, out_shape=result, in_specs=[VM] * 9, out_specs...  3.55 us
  transfers between devices with their start and end apart: 44, of which 15 were waited for; matrix products, arithmetic and copies ran while one was open for 0% of the time, Pallas kernels for 12%

profile of v4, /device:TPU:1, one launch (start us, length us, event | category | flops | bytes accessed | tf_op | source)
XLA Modules:
  0.0 143.8 jit_solution(5301529895271794761)
XLA Ops:
  0.0 1.2 copy-done
  1.2 1.3 shard_map.56
  2.4 1.3 collective-permute-start.5
  3.7 1.3 shard_map.55
  5.0 5.0 %collective-permute-start = (f32[32,8,384]{2,1,0:T(8,128)S(1)}, f32[32,8,384]{2,1,0:T(8,128)S(1)}, u32[]{:S(2)}, u32[]{:S(2)}) collective-permute-start(f32[32,8,384]{2,1,0:T(8,128)S(1)} %get-tuple-element.37.e5), channel_id=1, source_target_pairs={{0,8},{8,16},{16,24},{24,32},{32,40},{40,48},{48,56},{56,64},{64,7... | collective-permute-start | bytes 1179656 | tf_op jit(solution)/shard_map/ppermute | solution.py:369
  10.0 1.3 collective-permute-start.1
  11.3 4.3 %collective-permute-start.3 = (f32[38,8,384]{2,1,0:T(8,128)S(1)}, f32[38,8,384]{2,1,0:T(8,128)S(1)}, u32[]{:S(2)}, u32[]{:S(2)}) collective-permute-start(f32[38,8,384]{2,1,0:T(8,128)S(1)} %get-tuple-element.42.e4), channel_id=1, source_target_pairs={{0,8},{8,16},{16,24},{24,32},{32,40},{40,48},{48,56},{56,64},{64,7... | collective-permute-start | bytes 1400840 | tf_op jit(solution)/shard_map/ppermute | solution.py:369
  15.7 5.4 %collective-permute-start.6 = (f32[38,8,384]{2,1,0:T(8,128)S(1)}, f32[38,8,384]{2,1,0:T(8,128)S(1)}, u32[]{:S(2)}, u32[]{:S(2)}) collective-permute-start(f32[38,8,384]{2,1,0:T(8,128)S(1)} %collective-permute-done.5.hi2), channel_id=1, source_target_pairs={{0,1},{1,0},{2,3},{3,2},{4,5},{5,4},{6,7},{7,6},{8,9},{9,8},{10,11... | collective-permute-start | bytes 1400840 | tf_op jit(solution)/shard_map/ppermute | solution.py:372
  21.1 1.3 shard_map.57
  22.6 1.2 collective-permute-done.1.hi1
  23.8 2.8 %shard_map.59 = (f32[32,8,384]{2,1,0:T(8,128)S(1)}, f32[32,8,384]{2,1,0:T(8,128)S(1)}, f32[32,8,384]{2,1,0:T(8,128)S(1)}, f32[32,8,384]{2,1,0:T(8,128)S(1)}, f32...) custom-call(f32[32,8,384]{2,1,0:T(8,128)S(1)} %collective-permute-do, ...), custom_call_target="tpu_custom_call" | custom-call | bytes 7864320 | tf_op jit(solution)/shard_map/pallas_call | solution.py:382
  26.6 4.3 %collective-permute-start.40 = (f32[2,32,8,384]{3,2,1,0:T(8,128)S(1)}, f32[2,32,8,384]{3,2,1,0:T(8,128)S(1)}, u32[]{:S(2)}, u32[]{:S(2)}) collective-permute-start(f32[2,32,8,384]{3,2,1,0:T(8,128)S(1)} %get-tuple-element.56.refs_11_.rest_0_), channel_id=1, source_target_pairs={{0,6},{1,7},{2,4},{3,5},{4,2},{5,3},{6,0},{7,1},{8,14},{9,15},{10,... | collective-permute-start | bytes 2359304 | tf_op jit(solution)/shard_map/ppermute | solution.py:372
  30.9 1.6 %collective-permute-start.4 = (f32[38,8,384]{2,1,0:T(8,128)S(1)}, f32[38,8,384]{2,1,0:T(8,128)S(1)}, u32[]{:S(2)}, u32[]{:S(2)}) collective-permute-start(f32[38,8,384]{2,1,0:T(8,128)S(1)} %collective-permute-done.3.lo2), channel_id=1, source_target_pairs={{0,1},{1,0},{2,3},{3,2},{4,5},{5,4},{6,7},{7,6},{8,9},{9,8},{10,11... | collective-permute-start | bytes 1400840 | tf_op jit(solution)/shard_map/ppermute | solution.py:372
  32.5 3.6 %collective-permute-start.2 = (f32[32,8,384]{2,1,0:T(8,128)S(1)}, f32[32,8,384]{2,1,0:T(8,128)S(1)}, u32[]{:S(2)}, u32[]{:S(2)}) collective-permute-start(f32[32,8,384]{2,1,0:T(8,128)S(1)} %get-tuple-element.43.f4), channel_id=1, source_target_pairs={{0,8},{8,16},{16,24},{24,32},{32,40},{40,48},{48,56},{56,64},{64,7... | collective-permute-start | bytes 1179656 | tf_op jit(solution)/shard_map/ppermute | solution.py:369
  36.1 1.3 collective-permute-start.7
  37.5 1.6 %shard_map.60 = (f32[32,8,384]{2,1,0:T(8,128)S(1)}, f32[32,8,384]{2,1,0:T(8,128)S(1)}, f32[32,8,384]{2,1,0:T(8,128)S(1)}, f32[32,8,384]{2,1,0:T(8,128)S(1)}, f32...) custom-call(f32[38,8,384]{2,1,0:T(8,128)S(1)} %collective-permute-done.3.lo2, ...), custom_call_target="tpu_custom_call" | custom-call | bytes 7864320 | tf_op jit(solution)/shard_map/pallas_call | solution.py:386
  39.1 5.4 %collective-permute-done.2.refs_0_ = f32[32,8,384]{2,1,0:T(8,128)S(1)} collective-permute-done((f32[32,8,384]{2,1,0:T(8,128)S(1)}, f32[32,8,384]{2,1,0:T(8,128)S(1)}, u32[]{:S(2)}, u32[]{:S(2)}) %collective-permute-start.2) | collective-permute-done | bytes 393248 | tf_op jit(solution)/shard_map/ppermute | solution.py:369
  44.5 4.2 %collective-permute-done.7.refs_5_ = f32[32,8,384]{2,1,0:T(8,128)S(1)} collective-permute-done((f32[32,8,384]{2,1,0:T(8,128)S(1)}, f32[32,8,384]{2,1,0:T(8,128)S(1)}, u32[]{:S(2)}, u32[]{:S(2)}) %collective-permute-start.7) | collective-permute-done | bytes 393248 | tf_op jit(solution)/shard_map/ppermute | solution.py:369
  48.7 2.9 %shard_map.61 = (f32[8,512]{1,0:T(8,128)S(1)}, f32[6,32,8,384]{3,2,1,0:T(8,128)S(1)}) custom-call(s32[16]{0:T(128)S(1)} %copy-done.4, f32[32,8,384]{2,1,0:T(8,128)S(1)} %collective-permute-done.2.refs_0_, f32[32,8,384]{2,1,0:T(8,128)S(1)} %get-tuple-element.51.refs_1_, f32[32,8,384]{2,1,0:T(8,128)S(1)} %get-tuple-element.44.f0.refs_2_, ...), custom_call_target="tpu_custom_call" | custom-call | bytes 11796480 | tf_op jit(solution)/shard_map/pallas_call | solution.py:391
  51.9 1.5 %collective-permute-start.11 = (f32[8,512]{1,0:T(8,128)S(1)}, f32[8,512]{1,0:T(8,128)S(1)}, u32[]{:S(2)}, u32[]{:S(2)}) collective-permute-start(f32[8,512]{1,0:T(8,128)S(1)} %get-tuple-element.59.refs_0_), channel_id=1, source_target_pairs={{0,4},{1,5},{2,6},{3,7},{4,0},{5,1},{6,2},{7,3},{8,12},{9,13},{10,... | collective-permute-start | bytes 49160 | tf_op jit(solution)/shard_map/ppermute | solution.py:372
  53.4 1.5 %collective-permute-start.9 = (f32[8,512]{1,0:T(8,128)S(1)}, f32[8,512]{1,0:T(8,128)S(1)}, u32[]{:S(2)}, u32[]{:S(2)}) collective-permute-start(f32[8,512]{1,0:T(8,128)S(1)} %get-tuple-element.59.refs_0_), channel_id=1, source_target_pairs={{0,2},{1,3},{2,0},{3,1},{4,6},{5,7},{6,4},{7,5},{8,10},{9,11},{10,... | collective-permute-start | bytes 49160 | tf_op jit(solution)/shard_map/ppermute | solution.py:372
  55.5 2.1 %collective-permute-start.8 = (f32[8,512]{1,0:T(8,128)S(1)}, f32[8,512]{1,0:T(8,128)S(1)}, u32[]{:S(2)}, u32[]{:S(2)}) collective-permute-start(f32[8,512]{1,0:T(8,128)S(1)} %get-tuple-element.59.refs_0_), channel_id=1, source_target_pairs={{0,1},{1,0},{2,3},{3,2},{4,5},{5,4},{6,7},{7,6},{8,9},{9,8},{10,11... | collective-permute-start | bytes 49160 | tf_op jit(solution)/shard_map/ppermute | solution.py:372
  57.6 0.8 collective-permute-start.14
  60.3 10.7 %collective-permute-start.18 = (f32[64,128]{1,0:T(8,128)S(1)}, f32[64,128]{1,0:T(8,128)S(1)}, u32[]{:S(2)}, u32[]{:S(2)}) collective-permute-start(f32[64,128]{1,0:T(8,128)S(1)} %shard_map.62), channel_id=1, source_target_pairs={{0,0},{1,33},{2,2},{3,35},{4,4},{5,37},{6,6},{7,39},{8,8},{9,41},{... | collective-permute-start | bytes 98312 | tf_op jit(solution)/shard_map/ppermute | solution.py:431
  71.0 7.6 %collective-permute-start.16 = (f32[64,128]{1,0:T(8,128)S(1)}, f32[64,128]{1,0:T(8,128)S(1)}, u32[]{:S(2)}, u32[]{:S(2)}) collective-permute-start(f32[64,128]{1,0:T(8,128)S(1)} %shard_map.62), channel_id=1, source_target_pairs={{0,16},{1,49},{2,18},{3,51},{4,20},{5,53},{6,22},{7,55},{8,24},{9,... | collective-permute-start | bytes 98312 | tf_op jit(solution)/shard_map/ppermute | solution.py:431
  78.7 1.3 collective-permute-start.15
  80.0 1.5 %collective-permute-done.15.a = f32[64,128]{1,0:T(8,128)S(1)} collective-permute-done((f32[64,128]{1,0:T(8,128)S(1)}, f32[64,128]{1,0:T(8,128)S(1)}, u32[]{:S(2)}, u32[]{:S(2)}) %collective-permute-start.15) | collective-permute-done | bytes 32800 | tf_op jit(solution)/shard_map/ppermute | solution.py:431
  81.4 2.5 %collective-permute-start.21 = (f32[64,128]{1,0:T(8,128)S(1)}, f32[64,128]{1,0:T(8,128)S(1)}, u32[]{:S(2)}, u32[]{:S(2)}) collective-permute-start(f32[64,128]{1,0:T(8,128)S(1)} %shard_map.63.a), channel_id=1, source_target_pairs={{0,192},{1,193},{2,194},{3,195},{4,196},{5,197},{6,198},{7,199},{8... | collective-permute-start | bytes 98312 | tf_op jit(solution)/shard_map/ppermute | solution.py:431
  83.9 0.7 collective-permute-start.20
  84.6 0.7 collective-permute-start.19
  85.5 2.7 %collective-permute-done.20.c = f32[64,128]{1,0:T(8,128)S(1)} collective-permute-done((f32[64,128]{1,0:T(8,128)S(1)}, f32[64,128]{1,0:T(8,128)S(1)}, u32[]{:S(2)}, u32[]{:S(2)}) %collective-permute-start.20) | collective-permute-done | bytes 32800 | tf_op jit(solution)/shard_map/ppermute | solution.py:431
  88.2 0.6 collective-permute-start.26
  88.8 1.7 %collective-permute-start.28 = (f32[4,8,8,384]{3,2,1,0:T(8,128)S(1)}, f32[4,8,8,384]{3,2,1,0:T(8,128)S(1)}, u32[]{:S(2)}, u32[]{:S(2)}) collective-permute-start(f32[4,8,8,384]{3,2,1,0:T(8,128)S(1)} %get-tuple-element.64), channel_id=1, source_target_pairs={{0,6},{1,7},{2,4},{3,5},{4,2},{5,3},{6,0},{7,1},{8,14},{9,15},{10,... | collective-permute-start | bytes 1179656 | tf_op jit(solution)/shard_map/ppermute | solution.py:372
  91.1 5.5 %collective-permute-done.24.rest_2_ = f32[4,8,8,384]{3,2,1,0:T(8,128)S(1)} collective-permute-done((f32[4,8,8,384]{3,2,1,0:T(8,128)S(1)}, f32[4,8,8,384]{3,2,1,0:T(8,128)S(1)}, u32[]{:S(2)}, u32[]{:S(2)}) %collective-permute-start.24) | collective-permute-done | bytes 393248 | tf_op jit(solution)/shard_map/ppermute | solution.py:372
  96.7 5.6 %collective-permute-done.26.rest_4_ = f32[4,8,8,384]{3,2,1,0:T(8,128)S(1)} collective-permute-done((f32[4,8,8,384]{3,2,1,0:T(8,128)S(1)}, f32[4,8,8,384]{3,2,1,0:T(8,128)S(1)}, u32[]{:S(2)}, u32[]{:S(2)}) %collective-permute-start.26) | collective-permute-done | bytes 393248 | tf_op jit(solution)/shard_map/ppermute | solution.py:372
  102.4 6.3 %collective-permute-done.28.rest_6_ = f32[4,8,8,384]{3,2,1,0:T(8,128)S(1)} collective-permute-done((f32[4,8,8,384]{3,2,1,0:T(8,128)S(1)}, f32[4,8,8,384]{3,2,1,0:T(8,128)S(1)}, u32[]{:S(2)}, u32[]{:S(2)}) %collective-permute-start.28) | collective-permute-done | bytes 393248 | tf_op jit(solution)/shard_map/ppermute | solution.py:372
  109.7 1.9 %shard_map.65.left = f32[64,192]{1,0:T(8,128)S(1)} custom-call(f32[64,128]{1,0:T(8,128)S(1)} %shard_map.64.own, f32[64,128]{1,0:T(8,128)S(1)} %collective-permute-done.22.other), custom_call_target="tpu_custom_call" | custom-call | bytes 131072 | tf_op jit(solution)/shard_map/pallas_call | solution.py:439
  111.6 1.0 collective-permute-done.29.rest_7_
  112.6 0.7 shard_map.67
  113.4 3.4 %collective-permute-start.42 = (f32[2,32,8,384]{3,2,1,0:T(8,128)S(1)}, f32[2,32,8,384]{3,2,1,0:T(8,128)S(1)}, u32[]{:S(2)}, u32[]{:S(2)}) collective-permute-start(f32[2,32,8,384]{3,2,1,0:T(8,128)S(1)} %collective-permute-done.41.rest_4_), channel_id=1, source_target_pairs={{0,1},{1,0},{2,3},{3,2},{4,5},{5,4},{6,7},{7,6},{8,9},{9,8},{10,11... | collective-permute-start | bytes 2359304 | tf_op jit(solution)/shard_map/ppermute | solution.py:372
  116.8 2.1 %collective-permute-start.32 = (f32[2,4,4,8,384]{4,3,2,1,0:T(8,128)S(1)}, f32[2,4,4,8,384]{4,3,2,1,0:T(8,128)S(1)}, u32[]{:S(2)}, u32[]{:S(2)}) collective-permute-start(f32[2,4,4,8,384]{4,3,2,1,0:T(8,128)S(1)} %get-tuple-element.66), channel_id=1, source_target_pairs={{0,6},{1,7},{2,4},{3,5},{4,2},{5,3},{6,0},{7,1},{8,14},{9,15},{10,... | collective-permute-start | bytes 1179656 | tf_op jit(solution)/shard_map/ppermute | solution.py:372
  119.3 4.7 %collective-permute-done.30.refs_0_ = f32[2,4,4,8,384]{4,3,2,1,0:T(8,128)S(1)} collective-permute-done((f32[2,4,4,8,384]{4,3,2,1,0:T(8,128)S(1)}, f32[2,4,4,8,384]{4,3,2,1,0:T(8,128)S(1)}, u32[]{:S(2)}, u32[]{:S(2)}) %collective-permute-start.30) | collective-permute-done | bytes 393248 | tf_op jit(solution)/shard_map/ppermute | solution.py:372
  124.0 1.6 %collective-permute-start.31 = (f32[2,4,4,8,384]{4,3,2,1,0:T(8,128)S(1)}, f32[2,4,4,8,384]{4,3,2,1,0:T(8,128)S(1)}, u32[]{:S(2)}, u32[]{:S(2)}) collective-permute-start(f32[2,4,4,8,384]{4,3,2,1,0:T(8,128)S(1)} %collective-permute-done.30.refs_0_), channel_id=1, source_target_pairs={{0,1},{1,0},{2,3},{3,2},{4,5},{5,4},{6,7},{7,6},{8,9},{9,8},{10,11... | collective-permute-start | bytes 1179656 | tf_op jit(solution)/shard_map/ppermute | solution.py:372
  125.5 11.6 %collective-permute-done.32.refs_2_ = f32[2,4,4,8,384]{4,3,2,1,0:T(8,128)S(1)} collective-permute-done((f32[2,4,4,8,384]{4,3,2,1,0:T(8,128)S(1)}, f32[2,4,4,8,384]{4,3,2,1,0:T(8,128)S(1)}, u32[]{:S(2)}, u32[]{:S(2)}) %collective-permute-start.32) | collective-permute-done | bytes 393248 | tf_op jit(solution)/shard_map/ppermute | solution.py:372
  137.1 0.9 collective-permute-start.33
  138.0 3.5 %inner.1.refs_2_ = f32[8,6,32,384]{3,2,1,0:T(8,128)} custom-call(f32[64,192]{1,0:T(8,128)S(1)} %shard_map.65.left, f32[2,32,8,384]{3,2,1,0:T(8,128)S(1)} %get-tuple-element.56.refs_11_.rest_0_, f32[2,32,8,384]{3,2,1,0:T(8,128)S(1)} %collective-permute-done.37.rest_1_, f32[2,32,8,384]{3,2,1,0:T(8,128)S(1)} %collective-permute-done.38.one.rest_2_, ...), custom_call_target="tpu_custom_call" | custom-call | tf_op jit(solution)/shard_map/inner/pallas_call | solution.py:445
  141.6 0.9 shard_map.69.refs_6_
  142.5 1.2 shard_map.70
  (67 shorter events, 5.6 us)
Async XLA Ops:
  2.4 13.2 %collective-permute-start.5 = (f32[38,8,384]{2,1,0:T(8,128)S(1)}, f32[38,8,384]{2,1,0:T(8,128)S(1)}, u32[]{:S(2)}, u32[]{:S(2)}) collective-permute-start(f32[38,8,384]{2,1,0:T(8,128)S(1)} %get-tuple-element.39.e1), channel_id=1, source_target_pairs={{8,0},{16,8},{24,16},{32,24},{40,32},{48,40},{56,48},{64,56},{72,6... | collective-permute-start | bytes 1400840 | tf_op jit(solution)/shard_map/ppermute | solution.py:369
  5.0 17.6 %collective-permute-start = (f32[32,8,384]{2,1,0:T(8,128)S(1)}, f32[32,8,384]{2,1,0:T(8,128)S(1)}, u32[]{:S(2)}, u32[]{:S(2)}) collective-permute-start(f32[32,8,384]{2,1,0:T(8,128)S(1)} %get-tuple-element.37.e5), channel_id=1, source_target_pairs={{0,8},{8,16},{16,24},{24,32},{32,40},{40,48},{48,56},{56,64},{64,7... | collective-permute-start | bytes 1179656 | tf_op jit(solution)/shard_map/ppermute | solution.py:369
  10.0 13.8 %collective-permute-start.1 = (f32[32,8,384]{2,1,0:T(8,128)S(1)}, f32[32,8,384]{2,1,0:T(8,128)S(1)}, u32[]{:S(2)}, u32[]{:S(2)}) collective-permute-start(f32[32,8,384]{2,1,0:T(8,128)S(1)} %get-tuple-element.38.e0), channel_id=1, source_target_pairs={{8,0},{16,8},{24,16},{32,24},{40,32},{48,40},{56,48},{64,56},{72,6... | collective-permute-start | bytes 1179656 | tf_op jit(solution)/shard_map/ppermute | solution.py:369
  11.3 11.0 %copy-start.1 = (f32[3,32,6,384]{3,1,2,0:T(8,128)S(1)}, f32[3,32,6,384]{3,1,2,0:T(8,128)}, u32[]{:S(2)}) copy-start(f32[3,32,6,384]{3,1,2,0:T(8,128)} %param.6) | copy-start | bytes 2654212
  11.3 19.6 %collective-permute-start.3 = (f32[38,8,384]{2,1,0:T(8,128)S(1)}, f32[38,8,384]{2,1,0:T(8,128)S(1)}, u32[]{:S(2)}, u32[]{:S(2)}) collective-permute-start(f32[38,8,384]{2,1,0:T(8,128)S(1)} %get-tuple-element.42.e4), channel_id=1, source_target_pairs={{0,8},{8,16},{16,24},{24,32},{32,40},{40,48},{48,56},{56,64},{64,7... | collective-permute-start | bytes 1400840 | tf_op jit(solution)/shard_map/ppermute | solution.py:369
  15.7 21.7 %collective-permute-start.6 = (f32[38,8,384]{2,1,0:T(8,128)S(1)}, f32[38,8,384]{2,1,0:T(8,128)S(1)}, u32[]{:S(2)}, u32[]{:S(2)}) collective-permute-start(f32[38,8,384]{2,1,0:T(8,128)S(1)} %collective-permute-done.5.hi2), channel_id=1, source_target_pairs={{0,1},{1,0},{2,3},{3,2},{4,5},{5,4},{6,7},{7,6},{8,9},{9,8},{10,11... | collective-permute-start | bytes 1400840 | tf_op jit(solution)/shard_map/ppermute | solution.py:372
  26.6 63.9 %collective-permute-start.40 = (f32[2,32,8,384]{3,2,1,0:T(8,128)S(1)}, f32[2,32,8,384]{3,2,1,0:T(8,128)S(1)}, u32[]{:S(2)}, u32[]{:S(2)}) collective-permute-start(f32[2,32,8,384]{3,2,1,0:T(8,128)S(1)} %get-tuple-element.56.refs_11_.rest_0_), channel_id=1, source_target_pairs={{0,6},{1,7},{2,4},{3,5},{4,2},{5,3},{6,0},{7,1},{8,14},{9,15},{10,... | collective-permute-start | bytes 2359304 | tf_op jit(solution)/shard_map/ppermute | solution.py:372
  30.9 6.6 %collective-permute-start.4 = (f32[38,8,384]{2,1,0:T(8,128)S(1)}, f32[38,8,384]{2,1,0:T(8,128)S(1)}, u32[]{:S(2)}, u32[]{:S(2)}) collective-permute-start(f32[38,8,384]{2,1,0:T(8,128)S(1)} %collective-permute-done.3.lo2), channel_id=1, source_target_pairs={{0,1},{1,0},{2,3},{3,2},{4,5},{5,4},{6,7},{7,6},{8,9},{9,8},{10,11... | collective-permute-start | bytes 1400840 | tf_op jit(solution)/shard_map/ppermute | solution.py:372
  32.5 12.0 %collective-permute-start.2 = (f32[32,8,384]{2,1,0:T(8,128)S(1)}, f32[32,8,384]{2,1,0:T(8,128)S(1)}, u32[]{:S(2)}, u32[]{:S(2)}) collective-permute-start(f32[32,8,384]{2,1,0:T(8,128)S(1)} %get-tuple-element.43.f4), channel_id=1, source_target_pairs={{0,8},{8,16},{16,24},{24,32},{32,40},{40,48},{48,56},{56,64},{64,7... | collective-permute-start | bytes 1179656 | tf_op jit(solution)/shard_map/ppermute | solution.py:369
  36.1 12.6 %collective-permute-start.7 = (f32[32,8,384]{2,1,0:T(8,128)S(1)}, f32[32,8,384]{2,1,0:T(8,128)S(1)}, u32[]{:S(2)}, u32[]{:S(2)}) collective-permute-start(f32[32,8,384]{2,1,0:T(8,128)S(1)} %get-tuple-element.45.f1), channel_id=1, source_target_pairs={{8,0},{16,8},{24,16},{32,24},{40,32},{48,40},{56,48},{64,56},{72,6... | collective-permute-start | bytes 1179656 | tf_op jit(solution)/shard_map/ppermute | solution.py:369
  37.4 53.1 %collective-permute-start.38 = (f32[2,32,8,384]{3,2,1,0:T(8,128)S(1)}, f32[2,32,8,384]{3,2,1,0:T(8,128)S(1)}, u32[]{:S(2)}, u32[]{:S(2)}) collective-permute-start(f32[2,32,8,384]{3,2,1,0:T(8,128)S(1)} %get-tuple-element.56.refs_11_.rest_0_), channel_id=1, source_target_pairs={{0,2},{1,3},{2,0},{3,1},{4,6},{5,7},{6,4},{7,5},{8,10},{9,11},{10,... | collective-permute-start | bytes 2359304 | tf_op jit(solution)/shard_map/ppermute | solution.py:372
  37.5 11.2 %copy-start.4 = (s32[16]{0:T(128)S(1)}, s32[16]{0:T(128)}, u32[]{:S(2)}) copy-start(s32[16]{0:T(128)} %obs_column.1) | copy-start | bytes 196
  48.7 11.2 %copy-start.2 = (f32[32,16]{0,1:T(8,128)S(1)}, f32[32,16]{0,1:T(8,128)}, u32[]{:S(2)}) copy-start(f32[32,16]{0,1:T(8,128)} %param.8) | copy-start | bytes 6148
  48.7 11.2 %copy-start.3 = (f32[32,16]{0,1:T(8,128)S(1)}, f32[32,16]{0,1:T(8,128)}, u32[]{:S(2)}) copy-start(f32[32,16]{0,1:T(8,128)} %param.9) | copy-start | bytes 6148
  51.6 3.9 %collective-permute-start.13 = (f32[8,512]{1,0:T(8,128)S(1)}, f32[8,512]{1,0:T(8,128)S(1)}, u32[]{:S(2)}, u32[]{:S(2)}) collective-permute-start(f32[8,512]{1,0:T(8,128)S(1)} %get-tuple-element.59.refs_0_), channel_id=1, source_target_pairs={{0,6},{1,7},{2,4},{3,5},{4,2},{5,3},{6,0},{7,1},{8,14},{9,15},{10,... | collective-permute-start | bytes 49160 | tf_op jit(solution)/shard_map/ppermute | solution.py:372
  51.9 5.7 %collective-permute-start.11 = (f32[8,512]{1,0:T(8,128)S(1)}, f32[8,512]{1,0:T(8,128)S(1)}, u32[]{:S(2)}, u32[]{:S(2)}) collective-permute-start(f32[8,512]{1,0:T(8,128)S(1)} %get-tuple-element.59.refs_0_), channel_id=1, source_target_pairs={{0,4},{1,5},{2,6},{3,7},{4,0},{5,1},{6,2},{7,3},{8,12},{9,13},{10,... | collective-permute-start | bytes 49160 | tf_op jit(solution)/shard_map/ppermute | solution.py:372
  53.4 5.0 %collective-permute-start.9 = (f32[8,512]{1,0:T(8,128)S(1)}, f32[8,512]{1,0:T(8,128)S(1)}, u32[]{:S(2)}, u32[]{:S(2)}) collective-permute-start(f32[8,512]{1,0:T(8,128)S(1)} %get-tuple-element.59.refs_0_), channel_id=1, source_target_pairs={{0,2},{1,3},{2,0},{3,1},{4,6},{5,7},{6,4},{7,5},{8,10},{9,11},{10,... | collective-permute-start | bytes 49160 | tf_op jit(solution)/shard_map/ppermute | solution.py:372
  55.5 3.2 %collective-permute-start.8 = (f32[8,512]{1,0:T(8,128)S(1)}, f32[8,512]{1,0:T(8,128)S(1)}, u32[]{:S(2)}, u32[]{:S(2)}) collective-permute-start(f32[8,512]{1,0:T(8,128)S(1)} %get-tuple-element.59.refs_0_), channel_id=1, source_target_pairs={{0,1},{1,0},{2,3},{3,2},{4,5},{5,4},{6,7},{7,6},{8,9},{9,8},{10,11... | collective-permute-start | bytes 49160 | tf_op jit(solution)/shard_map/ppermute | solution.py:372
  57.6 1.6 %collective-permute-start.14 = (f32[8,512]{1,0:T(8,128)S(1)}, f32[8,512]{1,0:T(8,128)S(1)}, u32[]{:S(2)}, u32[]{:S(2)}) collective-permute-start(f32[8,512]{1,0:T(8,128)S(1)} %collective-permute-done.13.refs_6_), channel_id=1, source_target_pairs={{0,1},{1,0},{2,3},{3,2},{4,5},{5,4},{6,7},{7,6},{8,9},{9,8},{10,11... | collective-permute-start | bytes 49160 | tf_op jit(solution)/shard_map/ppermute | solution.py:372
  58.4 1.2 collective-permute-start.12
  58.7 1.2 collective-permute-start.10
  60.3 18.4 %collective-permute-start.18 = (f32[64,128]{1,0:T(8,128)S(1)}, f32[64,128]{1,0:T(8,128)S(1)}, u32[]{:S(2)}, u32[]{:S(2)}) collective-permute-start(f32[64,128]{1,0:T(8,128)S(1)} %shard_map.62), channel_id=1, source_target_pairs={{0,0},{1,33},{2,2},{3,35},{4,4},{5,37},{6,6},{7,39},{8,8},{9,41},{... | collective-permute-start | bytes 98312 | tf_op jit(solution)/shard_map/ppermute | solution.py:431
  70.9 9.0 %collective-permute-start.17 = (f32[64,128]{1,0:T(8,128)S(1)}, f32[64,128]{1,0:T(8,128)S(1)}, u32[]{:S(2)}, u32[]{:S(2)}) collective-permute-start(f32[64,128]{1,0:T(8,128)S(1)} %shard_map.62), channel_id=1, source_target_pairs={{0,24},{1,41},{2,26},{3,43},{4,28},{5,45},{6,30},{7,47},{8,32},{9,... | collective-permute-start | bytes 98312 | tf_op jit(solution)/shard_map/ppermute | solution.py:431
  71.0 8.9 %collective-permute-start.16 = (f32[64,128]{1,0:T(8,128)S(1)}, f32[64,128]{1,0:T(8,128)S(1)}, u32[]{:S(2)}, u32[]{:S(2)}) collective-permute-start(f32[64,128]{1,0:T(8,128)S(1)} %shard_map.62), channel_id=1, source_target_pairs={{0,16},{1,49},{2,18},{3,51},{4,20},{5,53},{6,22},{7,55},{8,24},{9,... | collective-permute-start | bytes 98312 | tf_op jit(solution)/shard_map/ppermute | solution.py:431
  78.7 2.8 %collective-permute-start.15 = (f32[64,128]{1,0:T(8,128)S(1)}, f32[64,128]{1,0:T(8,128)S(1)}, u32[]{:S(2)}, u32[]{:S(2)}) collective-permute-start(f32[64,128]{1,0:T(8,128)S(1)} %shard_map.62), channel_id=1, source_target_pairs={{0,8},{1,57},{2,10},{3,59},{4,12},{5,61},{6,14},{7,63},{8,16},{9,1... | collective-permute-start | bytes 98312 | tf_op jit(solution)/shard_map/ppermute | solution.py:431
  81.4 4.0 %collective-permute-start.21 = (f32[64,128]{1,0:T(8,128)S(1)}, f32[64,128]{1,0:T(8,128)S(1)}, u32[]{:S(2)}, u32[]{:S(2)}) collective-permute-start(f32[64,128]{1,0:T(8,128)S(1)} %shard_map.63.a), channel_id=1, source_target_pairs={{0,192},{1,193},{2,194},{3,195},{4,196},{5,197},{6,198},{7,199},{8... | collective-permute-start | bytes 98312 | tf_op jit(solution)/shard_map/ppermute | solution.py:431
  83.9 4.3 %collective-permute-start.20 = (f32[64,128]{1,0:T(8,128)S(1)}, f32[64,128]{1,0:T(8,128)S(1)}, u32[]{:S(2)}, u32[]{:S(2)}) collective-permute-start(f32[64,128]{1,0:T(8,128)S(1)} %shard_map.63.a), channel_id=1, source_target_pairs={{0,128},{1,129},{2,130},{3,131},{4,132},{5,133},{6,134},{7,135},{8... | collective-permute-start | bytes 98312 | tf_op jit(solution)/shard_map/ppermute | solution.py:431
  84.6 4.2 %collective-permute-start.19 = (f32[64,128]{1,0:T(8,128)S(1)}, f32[64,128]{1,0:T(8,128)S(1)}, u32[]{:S(2)}, u32[]{:S(2)}) collective-permute-start(f32[64,128]{1,0:T(8,128)S(1)} %shard_map.63.a), channel_id=1, source_target_pairs={{0,64},{1,65},{2,66},{3,67},{4,68},{5,69},{6,70},{7,71},{8,72},{9,... | collective-permute-start | bytes 98312 | tf_op jit(solution)/shard_map/ppermute | solution.py:431
  85.4 11.2 %collective-permute-start.24 = (f32[4,8,8,384]{3,2,1,0:T(8,128)S(1)}, f32[4,8,8,384]{3,2,1,0:T(8,128)S(1)}, u32[]{:S(2)}, u32[]{:S(2)}) collective-permute-start(f32[4,8,8,384]{3,2,1,0:T(8,128)S(1)} %get-tuple-element.62), channel_id=1, source_target_pairs={{0,2},{1,3},{2,0},{3,1},{4,6},{5,7},{6,4},{7,5},{8,10},{9,11},{10,... | collective-permute-start | bytes 1179656 | tf_op jit(solution)/shard_map/ppermute | solution.py:372
  88.2 14.1 %collective-permute-start.26 = (f32[4,8,8,384]{3,2,1,0:T(8,128)S(1)}, f32[4,8,8,384]{3,2,1,0:T(8,128)S(1)}, u32[]{:S(2)}, u32[]{:S(2)}) collective-permute-start(f32[4,8,8,384]{3,2,1,0:T(8,128)S(1)} %get-tuple-element.63), channel_id=1, source_target_pairs={{0,4},{1,5},{2,6},{3,7},{4,0},{5,1},{6,2},{7,3},{8,12},{9,13},{10,... | collective-permute-start | bytes 1179656 | tf_op jit(solution)/shard_map/ppermute | solution.py:372
  88.8 19.9 %collective-permute-start.28 = (f32[4,8,8,384]{3,2,1,0:T(8,128)S(1)}, f32[4,8,8,384]{3,2,1,0:T(8,128)S(1)}, u32[]{:S(2)}, u32[]{:S(2)}) collective-permute-start(f32[4,8,8,384]{3,2,1,0:T(8,128)S(1)} %get-tuple-element.64), channel_id=1, source_target_pairs={{0,6},{1,7},{2,4},{3,5},{4,2},{5,3},{6,0},{7,1},{8,14},{9,15},{10,... | collective-permute-start | bytes 1179656 | tf_op jit(solution)/shard_map/ppermute | solution.py:372
  90.5 18.1 %collective-permute-start.23 = (f32[4,8,8,384]{3,2,1,0:T(8,128)S(1)}, f32[4,8,8,384]{3,2,1,0:T(8,128)S(1)}, u32[]{:S(2)}, u32[]{:S(2)}) collective-permute-start(f32[4,8,8,384]{3,2,1,0:T(8,128)S(1)} %get-tuple-element.61.rest_0_), channel_id=1, source_target_pairs={{0,1},{1,0},{2,3},{3,2},{4,5},{5,4},{6,7},{7,6},{8,9},{9,8},{10,11... | collective-permute-start | bytes 1179656 | tf_op jit(solution)/shard_map/ppermute | solution.py:372
  90.5 11.7 %collective-permute-start.22 = (f32[64,128]{1,0:T(8,128)S(1)}, f32[64,128]{1,0:T(8,128)S(1)}, u32[]{:S(2)}, u32[]{:S(2)}) collective-permute-start(f32[64,128]{1,0:T(8,128)S(1)} %shard_map.64.own), channel_id=1, source_target_pairs={{0,1},{1,0},{2,3},{3,2},{4,5},{5,4},{6,7},{7,6},{8,9},{9,8},{10,11... | collective-permute-start | bytes 98312 | tf_op jit(solution)/shard_map/ppermute | solution.py:372
  96.6 12.5 %collective-permute-start.25 = (f32[4,8,8,384]{3,2,1,0:T(8,128)S(1)}, f32[4,8,8,384]{3,2,1,0:T(8,128)S(1)}, u32[]{:S(2)}, u32[]{:S(2)}) collective-permute-start(f32[4,8,8,384]{3,2,1,0:T(8,128)S(1)} %collective-permute-done.24.rest_2_), channel_id=1, source_target_pairs={{0,1},{1,0},{2,3},{3,2},{4,5},{5,4},{6,7},{7,6},{8,9},{9,8},{10,11... | collective-permute-start | bytes 1179656 | tf_op jit(solution)/shard_map/ppermute | solution.py:372
  102.3 7.0 %collective-permute-start.27 = (f32[4,8,8,384]{3,2,1,0:T(8,128)S(1)}, f32[4,8,8,384]{3,2,1,0:T(8,128)S(1)}, u32[]{:S(2)}, u32[]{:S(2)}) collective-permute-start(f32[4,8,8,384]{3,2,1,0:T(8,128)S(1)} %collective-permute-done.26.rest_4_), channel_id=1, source_target_pairs={{0,1},{1,0},{2,3},{3,2},{4,5},{5,4},{6,7},{7,6},{8,9},{9,8},{10,11... | collective-permute-start | bytes 1179656 | tf_op jit(solution)/shard_map/ppermute | solution.py:372
  102.3 11.1 %collective-permute-start.41 = (f32[2,32,8,384]{3,2,1,0:T(8,128)S(1)}, f32[2,32,8,384]{3,2,1,0:T(8,128)S(1)}, u32[]{:S(2)}, u32[]{:S(2)}) collective-permute-start(f32[2,32,8,384]{3,2,1,0:T(8,128)S(1)} %shard_map.68), channel_id=1, source_target_pairs={{0,6},{1,3},{2,4},{3,1},{4,2},{5,7},{6,0},{7,5},{8,14},{9,11},{10,... | collective-permute-start | bytes 2359304 | tf_op jit(solution)/shard_map/ppermute | solution.py:416
  108.6 8.2 %collective-permute-start.37 = (f32[2,32,8,384]{3,2,1,0:T(8,128)S(1)}, f32[2,32,8,384]{3,2,1,0:T(8,128)S(1)}, u32[]{:S(2)}, u32[]{:S(2)}) collective-permute-start(f32[2,32,8,384]{3,2,1,0:T(8,128)S(1)} %get-tuple-element.56.refs_11_.rest_0_), channel_id=1, source_target_pairs={{0,1},{1,0},{2,3},{3,2},{4,5},{5,4},{6,7},{7,6},{8,9},{9,8},{10,11... | collective-permute-start | bytes 2359304 | tf_op jit(solution)/shard_map/ppermute | solution.py:372
  108.6 10.3 %collective-permute-start.43 = (f32[2,32,8,384]{3,2,1,0:T(8,128)S(1)}, f32[2,32,8,384]{3,2,1,0:T(8,128)S(1)}, u32[]{:S(2)}, u32[]{:S(2)}) collective-permute-start(f32[2,32,8,384]{3,2,1,0:T(8,128)S(1)} %collective-permute-done.40.three.rest_6_), channel_id=1, source_target_pairs={{0,1},{1,0},{2,3},{3,2},{4,5},{5,4},{6,7},{7,6},{8,9},{9,8},{10,11... | collective-permute-start | bytes 2359304 | tf_op jit(solution)/shard_map/ppermute | solution.py:372
  109.2 3.5 %collective-permute-start.29 = (f32[4,8,8,384]{3,2,1,0:T(8,128)S(1)}, f32[4,8,8,384]{3,2,1,0:T(8,128)S(1)}, u32[]{:S(2)}, u32[]{:S(2)}) collective-permute-start(f32[4,8,8,384]{3,2,1,0:T(8,128)S(1)} %collective-permute-done.28.rest_6_), channel_id=1, source_target_pairs={{0,1},{1,0},{2,3},{3,2},{4,5},{5,4},{6,7},{7,6},{8,9},{9,8},{10,11... | collective-permute-start | bytes 1179656 | tf_op jit(solution)/shard_map/ppermute | solution.py:372
  109.3 9.7 %collective-permute-start.39 = (f32[2,32,8,384]{3,2,1,0:T(8,128)S(1)}, f32[2,32,8,384]{3,2,1,0:T(8,128)S(1)}, u32[]{:S(2)}, u32[]{:S(2)}) collective-permute-start(f32[2,32,8,384]{3,2,1,0:T(8,128)S(1)} %collective-permute-done.38.one.rest_2_), channel_id=1, source_target_pairs={{0,1},{1,0},{2,3},{3,2},{4,5},{5,4},{6,7},{7,6},{8,9},{9,8},{10,11... | collective-permute-start | bytes 2359304 | tf_op jit(solution)/shard_map/ppermute | solution.py:372
  113.3 10.6 %collective-permute-start.30 = (f32[2,4,4,8,384]{4,3,2,1,0:T(8,128)S(1)}, f32[2,4,4,8,384]{4,3,2,1,0:T(8,128)S(1)}, u32[]{:S(2)}, u32[]{:S(2)}) collective-permute-start(f32[2,4,4,8,384]{4,3,2,1,0:T(8,128)S(1)} %get-tuple-element.65), channel_id=1, source_target_pairs={{0,2},{1,3},{2,0},{3,1},{4,6},{5,7},{6,4},{7,5},{8,10},{9,11},{10,... | collective-permute-start | bytes 1179656 | tf_op jit(solution)/shard_map/ppermute | solution.py:372
  113.4 24.5 %collective-permute-start.42 = (f32[2,32,8,384]{3,2,1,0:T(8,128)S(1)}, f32[2,32,8,384]{3,2,1,0:T(8,128)S(1)}, u32[]{:S(2)}, u32[]{:S(2)}) collective-permute-start(f32[2,32,8,384]{3,2,1,0:T(8,128)S(1)} %collective-permute-done.41.rest_4_), channel_id=1, source_target_pairs={{0,1},{1,0},{2,3},{3,2},{4,5},{5,4},{6,7},{7,6},{8,9},{9,8},{10,11... | collective-permute-start | bytes 2359304 | tf_op jit(solution)/shard_map/ppermute | solution.py:372
  116.8 20.3 %collective-permute-start.32 = (f32[2,4,4,8,384]{4,3,2,1,0:T(8,128)S(1)}, f32[2,4,4,8,384]{4,3,2,1,0:T(8,128)S(1)}, u32[]{:S(2)}, u32[]{:S(2)}) collective-permute-start(f32[2,4,4,8,384]{4,3,2,1,0:T(8,128)S(1)} %get-tuple-element.66), channel_id=1, source_target_pairs={{0,6},{1,7},{2,4},{3,5},{4,2},{5,3},{6,0},{7,1},{8,14},{9,15},{10,... | collective-permute-start | bytes 1179656 | tf_op jit(solution)/shard_map/ppermute | solution.py:372
  118.9 19.1 %collective-permute-start.34 = (f32[2,4,4,8,384]{4,3,2,1,0:T(8,128)S(1)}, f32[2,4,4,8,384]{4,3,2,1,0:T(8,128)S(1)}, u32[]{:S(2)}, u32[]{:S(2)}) collective-permute-start(f32[2,4,4,8,384]{4,3,2,1,0:T(8,128)S(1)} %get-tuple-element.67), channel_id=1, source_target_pairs={{0,4},{1,5},{2,6},{3,7},{4,0},{5,1},{6,2},{7,3},{8,12},{9,13},{10,... | collective-permute-start | bytes 1179656 | tf_op jit(solution)/shard_map/ppermute | solution.py:372
  118.9 22.6 %collective-permute-start.36 = (f32[2,4,4,8,384]{4,3,2,1,0:T(8,128)S(1)}, f32[2,4,4,8,384]{4,3,2,1,0:T(8,128)S(1)}, u32[]{:S(2)}, u32[]{:S(2)}) collective-permute-start(f32[2,4,4,8,384]{4,3,2,1,0:T(8,128)S(1)} %get-tuple-element.68.refs_0_), channel_id=1, source_target_pairs={{0,1},{1,0},{2,3},{3,2},{4,5},{5,4},{6,7},{7,6},{8,9},{9,8},{10,11... | collective-permute-start | bytes 1179656 | tf_op jit(solution)/shard_map/ppermute | solution.py:372
  124.0 18.5 %collective-permute-start.31 = (f32[2,4,4,8,384]{4,3,2,1,0:T(8,128)S(1)}, f32[2,4,4,8,384]{4,3,2,1,0:T(8,128)S(1)}, u32[]{:S(2)}, u32[]{:S(2)}) collective-permute-start(f32[2,4,4,8,384]{4,3,2,1,0:T(8,128)S(1)} %collective-permute-done.30.refs_0_), channel_id=1, source_target_pairs={{0,1},{1,0},{2,3},{3,2},{4,5},{5,4},{6,7},{7,6},{8,9},{9,8},{10,11... | collective-permute-start | bytes 1179656 | tf_op jit(solution)/shard_map/ppermute | solution.py:372
  137.1 5.3 %collective-permute-start.33 = (f32[2,4,4,8,384]{4,3,2,1,0:T(8,128)S(1)}, f32[2,4,4,8,384]{4,3,2,1,0:T(8,128)S(1)}, u32[]{:S(2)}, u32[]{:S(2)}) collective-permute-start(f32[2,4,4,8,384]{4,3,2,1,0:T(8,128)S(1)} %collective-permute-done.32.refs_2_), channel_id=1, source_target_pairs={{0,1},{1,0},{2,3},{3,2},{4,5},{5,4},{6,7},{7,6},{8,9},{9,8},{10,11... | collective-permute-start | bytes 1179656 | tf_op jit(solution)/shard_map/ppermute | solution.py:372
  138.0 4.5 %collective-permute-start.35 = (f32[2,4,4,8,384]{4,3,2,1,0:T(8,128)S(1)}, f32[2,4,4,8,384]{4,3,2,1,0:T(8,128)S(1)}, u32[]{:S(2)}, u32[]{:S(2)}) collective-permute-start(f32[2,4,4,8,384]{4,3,2,1,0:T(8,128)S(1)} %collective-permute-done.34.refs_4_), channel_id=1, source_target_pairs={{0,1},{1,0},{2,3},{3,2},{4,5},{5,4},{6,7},{7,6},{8,9},{9,8},{10,11... | collective-permute-start | bytes 1179656 | tf_op jit(solution)/shard_map/ppermute | solution.py:372
  (1 other events, 1.2 us)
